TPU v7x, 256 devices: a whole 4x4x8 slice. The times are simulated.
256 devices in a mesh: group: 4 (over y), dev: 64 (over z, x, core).
Axes of the slice: x: 4, y: 4, z: 8, core: 2. Of those that a mesh axis runs over, the one named last changes fastest.
Arguments:
- level_set: float32 [512, 65536], P(None, ('group', 'dev')), may hold values from -8 to 8
- speed: float32 [512, 65536], P(None, ('group', 'dev')), may hold values from 0.25 to 1
- peer_slabs: int32 [16384, 8], P(('group', 'dev')), may hold values from -1 to 1535, as said below
- region_slabs: int32 [512, 16], P(('group', 'dev')), may hold values from 0 to 511, as said below
- halo_source: int32 [6, 65536], P(None, ('group', 'dev')), may hold values from 0 to 2079, as said below
Outputs:
- offset: float32 [512, 65536], P(None, ('group', 'dev'))
Inputs may be any that keep to these rules, and one draw needn't show every extreme that they name: `peer_slabs`: row (device, e) lists the local slab ids that the device sends to device e of its region, -1 in empty slots. Every device fills all 8 slots of at least one row, and receives 8 slabs from at least one device. `region_slabs`: local slab ids of the leaf faces that border the previous region (row 0) and the next region (row 1). `halo_source`: an entry of the halo table of the column's device; only slots that the sender fills are named.
All inputs are finite; a program needn't handle non-finite values.
Results may differ from a plain program's by a relative error of at most 0.0003.
Values sent between devices are 32-bit elements; how exact they have to be, the bound alone decides.
A program may use at most 64 MiB of HBM per device.

v0:
```python
import jax
import jax.numpy as jnp
from jax import lax
from jax.experimental import pallas as pl
from jax.experimental.pallas import tpu as pltpu
from jax.sharding import PartitionSpec as P

OFFSET_STEPS = 2
REDIST_PASSES = 2


advect_scale = 0.3
relax_scale = 0.3
weno_floor = 1e-06


def with_halo(block, sides, width):
    for axis, dim in sides:
        count = lax.axis_size(axis)
        forward = [(i, i + 1) for i in range(count - 1)]
        forward.append((count - 1, 0))
        backward = [(target, source) for source, target in forward]
        low = lax.ppermute(
            lax.slice_in_dim(block, block.shape[dim] - width, None, axis=dim), axis, forward
        )
        high = lax.ppermute(lax.slice_in_dim(block, 0, width, axis=dim), axis, backward)
        block = jnp.concatenate([low, block, high], axis=dim)
    return block


def face_slabs(voxels, layers):
    count = voxels.shape[3]
    pieces = [
        voxels[:layers],
        voxels[8 - layers :],
        voxels[:, :layers],
        voxels[:, 8 - layers :],
        voxels[:, :, :layers],
        voxels[:, :, 8 - layers :],
    ]
    return jnp.concatenate([piece.reshape(64 * layers, count) for piece in pieces], axis=1)


def weno_side(first, second, third, fourth, fifth):
    guess_a = first / 3.0 - 7.0 * second / 6.0 + 11.0 * third / 6.0
    guess_b = -second / 6.0 + 5.0 * third / 6.0 + fourth / 3.0
    guess_c = third / 3.0 + 5.0 * fourth / 6.0 - fifth / 6.0
    bend_a = first - 2.0 * second + third
    tilt_a = first - 4.0 * second + 3.0 * third
    bend_b = second - 2.0 * third + fourth
    tilt_b = second - fourth
    bend_c = third - 2.0 * fourth + fifth
    tilt_c = 3.0 * third - 4.0 * fourth + fifth
    smooth_a = weno_floor + 13.0 / 12.0 * bend_a * bend_a + 0.25 * tilt_a * tilt_a
    smooth_b = weno_floor + 13.0 / 12.0 * bend_b * bend_b + 0.25 * tilt_b * tilt_b
    smooth_c = weno_floor + 13.0 / 12.0 * bend_c * bend_c + 0.25 * tilt_c * tilt_c
    weight_a = 0.1 / (smooth_a * smooth_a)
    weight_b = 0.6 / (smooth_b * smooth_b)
    weight_c = 0.3 / (smooth_c * smooth_c)
    return (weight_a * guess_a + weight_b * guess_b + weight_c * guess_c) / (
        weight_a + weight_b + weight_c
    )


def one_sided(padded, along):
    differences = jnp.diff(padded, axis=along)

    def window(lowest):
        return lax.slice_in_dim(differences, lowest, lowest + 8, axis=along)

    backward = weno_side(window(0), window(1), window(2), window(3), window(4))
    forward = weno_side(window(5), window(4), window(3), window(2), window(1))
    return (backward, forward)


def widen(voxels, picked, layers):
    count = voxels.shape[3]

    def face_part(side, extent):
        return picked[:, side, :].reshape(extent + (count,))

    along_x = jnp.concatenate(
        [face_part(0, (layers, 8, 8)), voxels, face_part(1, (layers, 8, 8))], axis=0
    )
    along_y = jnp.concatenate(
        [face_part(2, (8, layers, 8)), voxels, face_part(3, (8, layers, 8))], axis=1
    )
    along_z = jnp.concatenate(
        [face_part(4, (8, 8, layers)), voxels, face_part(5, (8, 8, layers))], axis=2
    )
    return (along_x, along_y, along_z)


def advect_leaves(voxels, speeds, picked):
    squared = jnp.zeros_like(voxels)
    for along, padded in enumerate(widen(voxels, picked, 3)):
        backward, forward = one_sided(padded, along)
        squared = squared + jnp.maximum(
            jnp.square(jnp.maximum(backward, 0.0)), jnp.square(jnp.minimum(forward, 0.0))
        )
    return voxels - advect_scale * speeds * jnp.sqrt(squared)


def relax_leaves(voxels, sign_field, picked):
    squared = jnp.zeros_like(voxels)
    for along, padded in enumerate(widen(voxels, picked, 1)):
        centre = lax.slice_in_dim(padded, 1, 9, axis=along)
        backward = centre - lax.slice_in_dim(padded, 0, 8, axis=along)
        forward = lax.slice_in_dim(padded, 2, 10, axis=along) - centre
        rising = jnp.maximum(
            jnp.square(jnp.maximum(backward, 0.0)), jnp.square(jnp.minimum(forward, 0.0))
        )
        falling = jnp.maximum(
            jnp.square(jnp.minimum(backward, 0.0)), jnp.square(jnp.maximum(forward, 0.0))
        )
        squared = squared + jnp.where(sign_field > 0.0, rising, falling)
    return voxels - relax_scale * sign_field * (jnp.sqrt(squared) - 1.0)


def exchange_kernel(out_ref, bord_ref, arr_ref, reg_ref, send_sem, recv_sem, rsend_sem, rrecv_sem):
    peers = lax.axis_size("dev")
    regions = lax.axis_size("group")
    me = lax.axis_index("dev")
    region = lax.axis_index("group")
    up = lax.rem(region + 1, regions)
    down = lax.rem(region + regions - 1, regions)
    mesh_ids = pl.DeviceIdType.MESH

    barrier = pltpu.get_barrier_semaphore()

    def greet(k, carry):
        e = lax.rem(me + k, peers)
        pl.semaphore_signal(barrier, inc=1, device_id=(region, e), device_id_type=mesh_ids)
        return carry

    lax.fori_loop(1, peers, greet, 0)
    pl.semaphore_signal(barrier, inc=1, device_id=(up, me), device_id_type=mesh_ids)
    pl.semaphore_signal(barrier, inc=1, device_id=(down, me), device_id_type=mesh_ids)
    pl.semaphore_wait(barrier, peers + 1)

    pltpu.make_async_remote_copy(
        src_ref=bord_ref.at[1],
        dst_ref=reg_ref.at[0],
        send_sem=rsend_sem,
        recv_sem=rrecv_sem,
        device_id=(up, me),
        device_id_type=mesh_ids,
    ).start()
    pltpu.make_async_remote_copy(
        src_ref=bord_ref.at[0],
        dst_ref=reg_ref.at[1],
        send_sem=rsend_sem,
        recv_sem=rrecv_sem,
        device_id=(down, me),
        device_id_type=mesh_ids,
    ).start()

    def send(k, carry):
        e = lax.rem(me + k, peers)
        pltpu.make_async_remote_copy(
            src_ref=out_ref.at[e],
            dst_ref=arr_ref.at[me],
            send_sem=send_sem,
            recv_sem=recv_sem,
            device_id=(region, e),
            device_id_type=mesh_ids,
        ).start()
        return carry

    lax.fori_loop(1, peers, send, 0)
    pltpu.make_async_copy(out_ref.at[me], arr_ref.at[me], recv_sem).start()

    pltpu.make_async_copy(out_ref.at[pl.ds(0, peers - 1)], out_ref.at[pl.ds(0, peers - 1)], send_sem).wait()
    pltpu.make_async_copy(bord_ref, bord_ref, rsend_sem).wait()
    pltpu.make_async_copy(arr_ref, arr_ref, recv_sem).wait()
    pltpu.make_async_copy(reg_ref, reg_ref, rrecv_sem).wait()


def exchange(outgoing, border, layers):
    vmem = pl.BlockSpec(memory_space=pltpu.VMEM)
    return pl.pallas_call(
        exchange_kernel,
        out_shape=(
            jax.ShapeDtypeStruct(outgoing.shape, outgoing.dtype),
            jax.ShapeDtypeStruct(border.shape, border.dtype),
        ),
        in_specs=[vmem, vmem],
        out_specs=(vmem, vmem),
        scratch_shapes=[
            pltpu.SemaphoreType.DMA(()),
            pltpu.SemaphoreType.DMA(()),
            pltpu.SemaphoreType.DMA(()),
            pltpu.SemaphoreType.DMA(()),
        ],
        compiler_params=pltpu.CompilerParams(collective_id=layers, has_side_effects=True),
    )(outgoing, border)


def assemble(voxels, layers, peer_slabs, region_slabs, halo_source):
    slab_table = face_slabs(voxels, layers)
    slab_rows = 64 * layers
    region_width = region_slabs.shape[1]
    peers = peer_slabs.shape[0]
    slots = peer_slabs.shape[1]
    outgoing = jnp.take(slab_table, jnp.maximum(peer_slabs.reshape(-1), 0), axis=1)
    outgoing = outgoing.T.reshape(peers, slots, slab_rows)
    border = jnp.take(slab_table, region_slabs.reshape(-1), axis=1)
    border = border.T.reshape(2, region_width, slab_rows)
    arrived, beside = exchange(outgoing, border, layers)
    arrived = arrived.reshape(peers * slots, slab_rows).T
    beside = beside.reshape(2 * region_width, slab_rows).T
    combined = jnp.concatenate([slab_table, arrived, beside], axis=1)
    picked = jnp.take(combined, halo_source, axis=1)
    return picked


def per_device(level_set, speed, peer_slabs, region_slabs, halo_source):
    count = level_set.shape[1]
    voxels = level_set.reshape(8, 8, 8, count)
    speeds = speed.reshape(8, 8, 8, count)
    for offset_step in range(OFFSET_STEPS):
        picked = assemble(voxels, 3, peer_slabs, region_slabs, halo_source)
        voxels = advect_leaves(voxels, speeds, picked)
        sign_field = voxels / jnp.sqrt(voxels * voxels + 1.0)
        for redist_pass in range(REDIST_PASSES):
            picked = assemble(voxels, 1, peer_slabs, region_slabs, halo_source)
            voxels = relax_leaves(voxels, sign_field, picked)
    return voxels.reshape(512, count)


def solution(mesh):
    return jax.shard_map(
        per_device,
        mesh=mesh,
        in_specs=(
            P(None, ("group", "dev")),
            P(None, ("group", "dev")),
            P(("group", "dev"), None),
            P(("group", "dev"), None),
            P(None, ("group", "dev")),
        ),
        out_specs=P(None, ("group", "dev")),
        check_vma=False,
    )
```

profile of v0, /device:TPU:1, one launch (start us, length us, event | category | flops | bytes accessed | tf_op | source)
XLA Modules:
  0.0 217.2 jit_solution(15097251134810031967)
XLA Ops:
  7.0 3.0 %gather_fusion = f32[512,192]{1,0:T(8,128)S(1)} fusion(f32[192,1536]{0,1:T(8,128)} %get-tuple-element.119, s32[1024]{0:T(1024)S(1)} %get-tuple-element.180), kind=kCustom, calls=%fused_computation.clone | custom fusion | bytes 788480 | tf_op jit(solution)/shard_map/jit(_take)/gather | solution.py:205
  10.9 2.0 gather_fusion.1
  13.7 26.2 %shard_map.55 = (f32[64,8,192]{2,1,0:T(8,128)}, f32[2,16,192]{2,1,0:T(8,128)}) custom-call(f32[64,8,192]{2,1,0:T(8,128)} %select_bitcast_fusion.3.out_ref, f32[2,16,192]{2,1,0:T(8,128)} %bitcast.295), custom_call_target="tpu_custom_call" | custom-call | tf_op jit(solution)/shard_map/pallas_call | solution.py:181
  39.9 1.1 bitcast_dynamic-update-slice_fusion.1
  41.7 4.6 %gather_fusion.2 = f32[1536,192]{1,0:T(8,128)} fusion(f32[192,2080]{0,1:T(8,128)S(1)} %constant_dynamic-update-slice_fusion.6, s32[2048]{0:T(1024)S(1)} %pad_clamp_fusion), kind=kCustom, calls=%fused_computation.2.clone | custom fusion | bytes 2365440 | tf_op jit(solution)/shard_map/jit(_take)/gather | solution.py:213
  46.4 1.9 copy.58
  50.3 7.3 %multiply_subtract_fusion.5 = f32[8,8,8,256]{3,2,1,0:T(8,128)S(1)} fusion(f32[8,8,8,256]{3,2,1,0:T(8,128)S(1)} %bitcast.264, f32[8,8,8,256]{3,2,1,0:T(8,128)S(1)} %bitcast.267, f32[8,8,13,256]{3,2,1,0:T(8,128)S(1)} %slice_subtract_fusion.1, f32[8,13,8,256]{3,2,1,0:T(8,128)S(1)} %slice_subtract_fusion.4, f32[13,8,8,256]{3,2,1,0:T(8,128)S(1)} %slice_subtract_fusion.5), kind=kLoop, calls=%fused_computation.307 | loop fusion | flops 51249152 | bytes 11010048 | tf_op jit(solution)/shard_map/sub | solution.py:101
  61.7 16.4 %shard_map.56 = (f32[64,8,64]{2,1,0:T(8,128)}, f32[2,16,64]{2,1,0:T(8,128)}) custom-call(f32[64,8,64]{2,1,0:T(8,128)} %select_bitcast_fusion.11.out_ref, f32[2,16,64]{2,1,0:T(8,128)} %bitcast.298), custom_call_target="tpu_custom_call" | custom-call | tf_op jit(solution)/shard_map/pallas_call | solution.py:181
  79.8 2.6 %gather_fusion.5 = f32[1536,64]{1,0:T(8,128)S(1)} fusion(f32[64,2080]{0,1:T(8,128)S(1)} %constant_dynamic-update-slice_fusion.19, s32[2048]{0:T(1024)S(1)} %pad_clamp_fusion), kind=kCustom, calls=%fused_computation.5.clone | custom fusion | bytes 792576 | tf_op jit(solution)/shard_map/jit(_take)/gather | solution.py:213
  88.0 16.7 %shard_map.57 = (f32[64,8,64]{2,1,0:T(8,128)}, f32[2,16,64]{2,1,0:T(8,128)}) custom-call(f32[64,8,64]{2,1,0:T(8,128)} %select_bitcast_fusion.10.out_ref, f32[2,16,64]{2,1,0:T(8,128)} %bitcast.299), custom_call_target="tpu_custom_call" | custom-call | tf_op jit(solution)/shard_map/pallas_call | solution.py:181
  106.4 2.6 %gather_fusion.8 = f32[1536,64]{1,0:T(8,128)S(1)} fusion(f32[64,2080]{0,1:T(8,128)S(1)} %constant_dynamic-update-slice_fusion.32, s32[2048]{0:T(1024)S(1)} %pad_clamp_fusion), kind=kCustom, calls=%fused_computation.15.clone | custom fusion | bytes 792576 | tf_op jit(solution)/shard_map/jit(_take)/gather | solution.py:213
  109.5 1.1 multiply_subtract_fusion.3
  116.2 3.0 %gather_fusion.9 = f32[512,192]{1,0:T(8,128)S(1)} fusion(f32[192,1536]{0,1:T(8,128)} %get-tuple-element.107, s32[1024]{0:T(1024)S(1)} %get-tuple-element.180), kind=kCustom, calls=%fused_computation.6.clone | custom fusion | bytes 788480 | tf_op jit(solution)/shard_map/jit(_take)/gather | solution.py:205
  120.2 2.0 gather_fusion.10
  122.9 21.7 %shard_map.58 = (f32[64,8,192]{2,1,0:T(8,128)}, f32[2,16,192]{2,1,0:T(8,128)}) custom-call(f32[64,8,192]{2,1,0:T(8,128)} %select_bitcast_fusion.2.out_ref, f32[2,16,192]{2,1,0:T(8,128)} %bitcast.296), custom_call_target="tpu_custom_call" | custom-call | tf_op jit(solution)/shard_map/pallas_call | solution.py:181
  144.6 1.1 bitcast_dynamic-update-slice_fusion
  146.4 4.6 %gather_fusion.11 = f32[1536,192]{1,0:T(8,128)} fusion(f32[192,2080]{0,1:T(8,128)S(1)} %constant_dynamic-update-slice_fusion.45, s32[2048]{0:T(1024)S(1)} %pad_clamp_fusion), kind=kCustom, calls=%fused_computation.8.clone | custom fusion | bytes 2365440 | tf_op jit(solution)/shard_map/jit(_take)/gather | solution.py:213
  151.1 1.9 copy.105
  154.9 7.3 %multiply_subtract_fusion.2 = f32[8,8,8,256]{3,2,1,0:T(8,128)S(1)} fusion(f32[8,8,8,256]{3,2,1,0:T(8,128)S(1)} %multiply_subtract_fusion.3, f32[8,8,8,256]{3,2,1,0:T(8,128)S(1)} %bitcast.268, f32[8,8,13,256]{3,2,1,0:T(8,128)S(1)} %slice_subtract_fusion, f32[8,13,8,256]{3,2,1,0:T(8,128)S(1)} %slice_subtract_fusion.2, ...), kind=kLoop, calls=%fused_computation.303 | loop fusion | flops 51249152 | bytes 11010048 | tf_op jit(solution)/shard_map/sub | solution.py:101
  166.2 17.9 %shard_map.59 = (f32[64,8,64]{2,1,0:T(8,128)}, f32[2,16,64]{2,1,0:T(8,128)}) custom-call(f32[64,8,64]{2,1,0:T(8,128)} %select_bitcast_fusion.9.out_ref, f32[2,16,64]{2,1,0:T(8,128)} %bitcast.300), custom_call_target="tpu_custom_call" | custom-call | tf_op jit(solution)/shard_map/pallas_call | solution.py:181
  185.8 2.6 %gather_fusion.14 = f32[1536,64]{1,0:T(8,128)S(1)} fusion(f32[64,2080]{0,1:T(8,128)S(1)} %constant_dynamic-update-slice_fusion.58, s32[2048]{0:T(1024)S(1)} %pad_clamp_fusion), kind=kCustom, calls=%fused_computation.16.clone | custom fusion | bytes 792576 | tf_op jit(solution)/shard_map/jit(_take)/gather | solution.py:213
  194.0 16.6 %shard_map.60 = (f32[64,8,64]{2,1,0:T(8,128)}, f32[2,16,64]{2,1,0:T(8,128)}) custom-call(f32[64,8,64]{2,1,0:T(8,128)} %select_bitcast_fusion.8.out_ref, f32[2,16,64]{2,1,0:T(8,128)} %bitcast.297), custom_call_target="tpu_custom_call" | custom-call | tf_op jit(solution)/shard_map/pallas_call | solution.py:181
  212.3 2.6 %gather_fusion.17 = f32[1536,64]{1,0:T(8,128)S(1)} fusion(f32[64,2080]{0,1:T(8,128)S(1)} %constant_dynamic-update-slice_fusion.71, s32[2048]{0:T(1024)S(1)} %pad_clamp_fusion), kind=kCustom, calls=%fused_computation.17.clone | custom fusion | bytes 792576 | tf_op jit(solution)/shard_map/jit(_take)/gather | solution.py:213
  215.4 1.9 multiply_subtract_fusion
  (202 shorter events, 47.5 us)
Async XLA Ops:
  1.1 1.8 copy-start
  5.0 1.7 copy-start.5
  5.0 1.9 copy-start.6
  10.9 30.8 %copy-start.4 = (s32[6,256]{1,0:T(8,128)S(1)}, s32[6,256]{1,0:T(8,128)}, u32[]{:S(2)}) copy-start(s32[6,256]{1,0:T(8,128)} %param.21) | copy-start | bytes 18436
  49.2 1.0 copy-start.3
  50.3 7.3 %copy-start.1 = (f32[512,256]{1,0:T(8,128)}, f32[512,256]{1,0:T(8,128)S(1)}, u32[]{:S(2)}) copy-start(f32[512,256]{1,0:T(8,128)S(1)} %broadcast_multiply_fusion) | copy-start | bytes 1572868
  153.9 1.0 copy-start.2
where the time goes:
time: 218 us; the launch traced here: 217 us
  Pallas kernels  116 us (53%)
  local copies, waits for them, and re-layouts  69.8 us (32%)
  other arithmetic  30.6 us (14%)
    pallas_call x6, Pallas kernels, exchange(): pl.pallas_call(exchange_kernel, out_shape=(jax.ShapeDtypeStruct(outgoing....  116 us
    gather x12, local copies, waits for them, and re-layouts, assemble(): picked = jnp.take(combined, halo_source, axis=1)  24.3 us
    unnamed x60, local copies, waits for them, and re-layouts  16 us
    sub x2, other arithmetic, advect_leaves(): return voxels - advect_scale * speeds * jnp.sqrt(squared)  14.6 us
    gather x6, local copies, waits for them, and re-layouts, assemble(): jnp.take(slab_table, jnp.maximum(peer_slabs.reshape(-1), 0), axis=1)  10.1 us
    gather x6, local copies, waits for them, and re-layouts, assemble(): border = jnp.take(slab_table, region_slabs.reshape(-1), axis=1)  6.32 us
    reshape x6, other arithmetic, assemble(): outgoing = outgoing.T.reshape(peers, slots, slab_rows)  5.24 us
    sub x4, other arithmetic, relax_leaves(): return voxels - relax_scale * sign_field * (jnp.sqrt(squared) - 1.0)  5.08 us

commit v1 on v0

--- a/solution.py
+++ b/solution.py
@@ -1,3 +1,5 @@
+import functools
+
 import jax
 import jax.numpy as jnp
 from jax import lax
@@ -117,80 +119,99 @@
     return voxels - relax_scale * sign_field * (jnp.sqrt(squared) - 1.0)
 
 
-def exchange_kernel(out_ref, bord_ref, arr_ref, reg_ref, send_sem, recv_sem, rsend_sem, rrecv_sem):
+def exchange_kernel(
+    ring, out_ref, bord_ref, arr_ref, reg_ref, mid_ref, turned_ref, sems
+):
     peers = lax.axis_size("dev")
     regions = lax.axis_size("group")
+    rows = peers // ring
     me = lax.axis_index("dev")
     region = lax.axis_index("group")
+    row = me // ring
+    col = me % ring
     up = lax.rem(region + 1, regions)
     down = lax.rem(region + regions - 1, regions)
     mesh_ids = pl.DeviceIdType.MESH
 
     barrier = pltpu.get_barrier_semaphore()
-
-    def greet(k, carry):
-        e = lax.rem(me + k, peers)
-        pl.semaphore_signal(barrier, inc=1, device_id=(region, e), device_id_type=mesh_ids)
-        return carry
-
-    lax.fori_loop(1, peers, greet, 0)
+    for k in range(1, rows):
+        other = lax.rem(row + k, rows) * ring + col
+        pl.semaphore_signal(barrier, inc=1, device_id=(region, other), device_id_type=mesh_ids)
+    for k in range(1, ring):
+        other = row * ring + lax.rem(col + k, ring)
+        pl.semaphore_signal(barrier, inc=1, device_id=(region, other), device_id_type=mesh_ids)
     pl.semaphore_signal(barrier, inc=1, device_id=(up, me), device_id_type=mesh_ids)
     pl.semaphore_signal(barrier, inc=1, device_id=(down, me), device_id_type=mesh_ids)
-    pl.semaphore_wait(barrier, peers + 1)
+    pl.semaphore_wait(barrier, rows + ring)
 
     pltpu.make_async_remote_copy(
         src_ref=bord_ref.at[1],
         dst_ref=reg_ref.at[0],
-        send_sem=rsend_sem,
-        recv_sem=rrecv_sem,
+        send_sem=sems.at[4],
+        recv_sem=sems.at[5],
         device_id=(up, me),
         device_id_type=mesh_ids,
     ).start()
     pltpu.make_async_remote_copy(
         src_ref=bord_ref.at[0],
         dst_ref=reg_ref.at[1],
-        send_sem=rsend_sem,
-        recv_sem=rrecv_sem,
+        send_sem=sems.at[4],
+        recv_sem=sems.at[5],
         device_id=(down, me),
         device_id_type=mesh_ids,
     ).start()
 
-    def send(k, carry):
-        e = lax.rem(me + k, peers)
+    for k in range(1, rows):
+        target = lax.rem(row + k, rows)
         pltpu.make_async_remote_copy(
-            src_ref=out_ref.at[e],
-            dst_ref=arr_ref.at[me],
-            send_sem=send_sem,
-            recv_sem=recv_sem,
-            device_id=(region, e),
+            src_ref=out_ref.at[pl.ds(target * ring, ring)],
+            dst_ref=mid_ref.at[row],
+            send_sem=sems.at[0],
+            recv_sem=sems.at[1],
+            device_id=(region, target * ring + col),
             device_id_type=mesh_ids,
         ).start()
-        return carry
-
-    lax.fori_loop(1, peers, send, 0)
-    pltpu.make_async_copy(out_ref.at[me], arr_ref.at[me], recv_sem).start()
-
-    pltpu.make_async_copy(out_ref.at[pl.ds(0, peers - 1)], out_ref.at[pl.ds(0, peers - 1)], send_sem).wait()
-    pltpu.make_async_copy(bord_ref, bord_ref, rsend_sem).wait()
-    pltpu.make_async_copy(arr_ref, arr_ref, recv_sem).wait()
-    pltpu.make_async_copy(reg_ref, reg_ref, rrecv_sem).wait()
-
-
-def exchange(outgoing, border, layers):
+    pltpu.make_async_copy(out_ref.at[pl.ds(row * ring, ring)], mid_ref.at[row], sems.at[1]).start()
+    pltpu.make_async_copy(mid_ref, mid_ref, sems.at[1]).wait()
+
+    for c in range(ring):
+        turned_ref[c] = mid_ref[:, c]
+
+    for k in range(1, ring):
+        target = lax.rem(col + k, ring)
+        pltpu.make_async_remote_copy(
+            src_ref=turned_ref.at[target],
+            dst_ref=arr_ref.at[col],
+            send_sem=sems.at[2],
+            recv_sem=sems.at[3],
+            device_id=(region, row * ring + target),
+            device_id_type=mesh_ids,
+        ).start()
+    pltpu.make_async_copy(turned_ref.at[col], arr_ref.at[col], sems.at[3]).start()
+
+    pltpu.make_async_copy(mid_ref.at[pl.ds(0, rows - 1)], mid_ref.at[pl.ds(0, rows - 1)], sems.at[0]).wait()
+    pltpu.make_async_copy(turned_ref.at[pl.ds(0, ring - 1)], turned_ref.at[pl.ds(0, ring - 1)], sems.at[2]).wait()
+    pltpu.make_async_copy(bord_ref, bord_ref, sems.at[4]).wait()
+    pltpu.make_async_copy(arr_ref, arr_ref, sems.at[3]).wait()
+    pltpu.make_async_copy(reg_ref, reg_ref, sems.at[5]).wait()
+
+
+def exchange(outgoing, border, layers, ring):
+    peers, slots, slab_rows = outgoing.shape
+    rows = peers // ring
     vmem = pl.BlockSpec(memory_space=pltpu.VMEM)
     return pl.pallas_call(
-        exchange_kernel,
+        functools.partial(exchange_kernel, ring),
         out_shape=(
-            jax.ShapeDtypeStruct(outgoing.shape, outgoing.dtype),
+            jax.ShapeDtypeStruct((ring, rows, slots, slab_rows), outgoing.dtype),
             jax.ShapeDtypeStruct(border.shape, border.dtype),
         ),
         in_specs=[vmem, vmem],
         out_specs=(vmem, vmem),
         scratch_shapes=[
-            pltpu.SemaphoreType.DMA(()),
-            pltpu.SemaphoreType.DMA(()),
-            pltpu.SemaphoreType.DMA(()),
-            pltpu.SemaphoreType.DMA(()),
+            pltpu.VMEM((rows, ring, slots, slab_rows), outgoing.dtype),
+            pltpu.VMEM((ring, rows, slots, slab_rows), outgoing.dtype),
+            pltpu.SemaphoreType.DMA((6,)),
         ],
         compiler_params=pltpu.CompilerParams(collective_id=layers, has_side_effects=True),
     )(outgoing, border)
@@ -206,11 +227,17 @@
     outgoing = outgoing.T.reshape(peers, slots, slab_rows)
     border = jnp.take(slab_table, region_slabs.reshape(-1), axis=1)
     border = border.T.reshape(2, region_width, slab_rows)
-    arrived, beside = exchange(outgoing, border, layers)
+    ring = 8 if peers % 8 == 0 and peers > 8 else 2
+    arrived, beside = exchange(outgoing, border, layers, ring)
     arrived = arrived.reshape(peers * slots, slab_rows).T
     beside = beside.reshape(2 * region_width, slab_rows).T
     combined = jnp.concatenate([slab_table, arrived, beside], axis=1)
-    picked = jnp.take(combined, halo_source, axis=1)
+    local = slab_table.shape[1]
+    entry = halo_source - local
+    sender = entry // slots
+    moved = local + ((sender % ring) * (peers // ring) + sender // ring) * slots + entry % slots
+    inside = (entry >= 0) & (entry < peers * slots)
+    picked = jnp.take(combined, jnp.where(inside, moved, halo_source), axis=1)
     return picked
 
 

time: 218 us -> 236 us (1.083)
  Pallas kernels: 116 us -> 133 us
    pallas_call x6, Pallas kernels: 116 us -> 133 us  [exchange(): pl.pallas_call(functools.partial(exchange_kernel, ring), out_shape=(jax.S...]
where the time goes in v1:
time: 236 us; the launch traced here: 235 us
  Pallas kernels  133 us (56%)
  local copies, waits for them, and re-layouts  70.2 us (30%)
  other arithmetic  30.7 us (13%)
    pallas_call x6, Pallas kernels, exchange(): pl.pallas_call(functools.partial(exchange_kernel, ring), out_shape=(jax.S...  133 us
    gather x12, local copies, waits for them, and re-layouts, assemble(): picked = jnp.take(combined, jnp.where(inside, moved, halo_source), axis=1)  24.6 us
    unnamed x60, local copies, waits for them, and re-layouts  16.1 us
    sub x2, other arithmetic, advect_leaves(): return voxels - advect_scale * speeds * jnp.sqrt(squared)  14.6 us
    gather x6, local copies, waits for them, and re-layouts, assemble(): jnp.take(slab_table, jnp.maximum(peer_slabs.reshape(-1), 0), axis=1)  10.1 us
    gather x6, local copies, waits for them, and re-layouts, assemble(): border = jnp.take(slab_table, region_slabs.reshape(-1), axis=1)  6.32 us
    reshape x6, other arithmetic, assemble(): outgoing = outgoing.T.reshape(peers, slots, slab_rows)  5.23 us
    sub x4, other arithmetic, relax_leaves(): return voxels - relax_scale * sign_field * (jnp.sqrt(squared) - 1.0)  5.08 us

profile of v1, /device:TPU:1, one launch (start us, length us, event | category | flops | bytes accessed | tf_op | source)
XLA Modules:
  0.0 234.6 jit_solution(6848280265390863132)
XLA Ops:
  7.1 3.0 %gather_fusion = f32[512,192]{1,0:T(8,128)S(1)} fusion(f32[192,1536]{0,1:T(8,128)} %get-tuple-element.121, s32[1024]{0:T(1024)S(1)} %get-tuple-element.182), kind=kCustom, calls=%fused_computation.clone | custom fusion | bytes 788480 | tf_op jit(solution)/shard_map/jit(_take)/gather | solution.py:226
  11.0 2.0 gather_fusion.1
  13.7 31.7 %shard_map.55 = (f32[8,8,8,192]{3,2,1,0:T(8,128)}, f32[2,16,192]{2,1,0:T(8,128)}) custom-call(f32[64,8,192]{2,1,0:T(8,128)} %select_bitcast_fusion.3.out_ref, f32[2,16,192]{2,1,0:T(8,128)} %bitcast.295), custom_call_target="tpu_custom_call" | custom-call | tf_op jit(solution)/shard_map/pallas_call | solution.py:203
  45.5 1.1 constant_dynamic-update-slice_fusion.7
  47.4 4.7 %gather_fusion.2 = f32[1536,192]{1,0:T(8,128)} fusion(f32[192,2080]{0,1:T(8,128)S(1)} %constant_dynamic-update-slice_fusion.6, s32[2048]{0:T(1024)S(1)} %pad_clamp_fusion), kind=kCustom, calls=%fused_computation.2.clone | custom fusion | bytes 2365440 | tf_op jit(solution)/shard_map/jit(_take)/gather | solution.py:240
  52.0 1.9 copy.58
  56.0 7.3 %multiply_subtract_fusion.5 = f32[8,8,8,256]{3,2,1,0:T(8,128)S(1)} fusion(f32[8,8,8,256]{3,2,1,0:T(8,128)S(1)} %bitcast.258, f32[8,8,8,256]{3,2,1,0:T(8,128)S(1)} %bitcast.261, f32[8,8,13,256]{3,2,1,0:T(8,128)S(1)} %slice_subtract_fusion.1, f32[8,13,8,256]{3,2,1,0:T(8,128)S(1)} %slice_subtract_fusion.4, f32[13,8,8,256]{3,2,1,0:T(8,128)S(1)} %slice_subtract_fusion.5), kind=kLoop, calls=%fused_computation.305 | loop fusion | flops 51249152 | bytes 11010048 | tf_op jit(solution)/shard_map/sub | solution.py:103
  67.3 18.4 %shard_map.56 = (f32[8,8,8,64]{3,2,1,0:T(8,128)}, f32[2,16,64]{2,1,0:T(8,128)}) custom-call(f32[64,8,64]{2,1,0:T(8,128)} %select_bitcast_fusion.11.out_ref, f32[2,16,64]{2,1,0:T(8,128)} %bitcast.298), custom_call_target="tpu_custom_call" | custom-call | tf_op jit(solution)/shard_map/pallas_call | solution.py:203
  87.4 2.6 %gather_fusion.5 = f32[1536,64]{1,0:T(8,128)S(1)} fusion(f32[64,2080]{0,1:T(8,128)S(1)} %constant_dynamic-update-slice_fusion.20, s32[2048]{0:T(1024)S(1)} %pad_clamp_fusion), kind=kCustom, calls=%fused_computation.5.clone | custom fusion | bytes 792576 | tf_op jit(solution)/shard_map/jit(_take)/gather | solution.py:240
  95.6 18.2 %shard_map.57 = (f32[8,8,8,64]{3,2,1,0:T(8,128)}, f32[2,16,64]{2,1,0:T(8,128)}) custom-call(f32[64,8,64]{2,1,0:T(8,128)} %select_bitcast_fusion.10.out_ref, f32[2,16,64]{2,1,0:T(8,128)} %bitcast.299), custom_call_target="tpu_custom_call" | custom-call | tf_op jit(solution)/shard_map/pallas_call | solution.py:203
  115.4 2.8 %gather_fusion.8 = f32[1536,64]{1,0:T(8,128)S(1)} fusion(f32[64,2080]{0,1:T(8,128)S(1)} %constant_dynamic-update-slice_fusion.34, s32[2048]{0:T(1024)S(1)} %pad_clamp_fusion), kind=kCustom, calls=%fused_computation.15.clone | custom fusion | bytes 792576 | tf_op jit(solution)/shard_map/jit(_take)/gather | solution.py:240
  118.7 1.1 multiply_subtract_fusion.3
  125.5 3.0 %gather_fusion.9 = f32[512,192]{1,0:T(8,128)S(1)} fusion(f32[192,1536]{0,1:T(8,128)} %get-tuple-element.109, s32[1024]{0:T(1024)S(1)} %get-tuple-element.182), kind=kCustom, calls=%fused_computation.6.clone | custom fusion | bytes 788480 | tf_op jit(solution)/shard_map/jit(_take)/gather | solution.py:226
  129.4 2.0 gather_fusion.10
  132.1 26.9 %shard_map.58 = (f32[8,8,8,192]{3,2,1,0:T(8,128)}, f32[2,16,192]{2,1,0:T(8,128)}) custom-call(f32[64,8,192]{2,1,0:T(8,128)} %select_bitcast_fusion.2.out_ref, f32[2,16,192]{2,1,0:T(8,128)} %bitcast.296), custom_call_target="tpu_custom_call" | custom-call | tf_op jit(solution)/shard_map/pallas_call | solution.py:203
  159.0 1.1 constant_dynamic-update-slice_fusion.49
  160.9 4.7 %gather_fusion.11 = f32[1536,192]{1,0:T(8,128)} fusion(f32[192,2080]{0,1:T(8,128)S(1)} %constant_dynamic-update-slice_fusion.48, s32[2048]{0:T(1024)S(1)} %pad_clamp_fusion), kind=kCustom, calls=%fused_computation.8.clone | custom fusion | bytes 2365440 | tf_op jit(solution)/shard_map/jit(_take)/gather | solution.py:240
  165.5 1.9 copy.105
  169.4 7.3 %multiply_subtract_fusion.2 = f32[8,8,8,256]{3,2,1,0:T(8,128)S(1)} fusion(f32[8,8,8,256]{3,2,1,0:T(8,128)S(1)} %multiply_subtract_fusion.3, f32[8,8,8,256]{3,2,1,0:T(8,128)S(1)} %bitcast.262, f32[8,8,13,256]{3,2,1,0:T(8,128)S(1)} %slice_subtract_fusion, f32[8,13,8,256]{3,2,1,0:T(8,128)S(1)} %slice_subtract_fusion.2, ...), kind=kLoop, calls=%fused_computation.301 | loop fusion | flops 51249152 | bytes 11010048 | tf_op jit(solution)/shard_map/sub | solution.py:103
  180.7 19.1 %shard_map.59 = (f32[8,8,8,64]{3,2,1,0:T(8,128)}, f32[2,16,64]{2,1,0:T(8,128)}) custom-call(f32[64,8,64]{2,1,0:T(8,128)} %select_bitcast_fusion.9.out_ref, f32[2,16,64]{2,1,0:T(8,128)} %bitcast.300), custom_call_target="tpu_custom_call" | custom-call | tf_op jit(solution)/shard_map/pallas_call | solution.py:203
  201.5 2.6 %gather_fusion.14 = f32[1536,64]{1,0:T(8,128)S(1)} fusion(f32[64,2080]{0,1:T(8,128)S(1)} %constant_dynamic-update-slice_fusion.62, s32[2048]{0:T(1024)S(1)} %pad_clamp_fusion), kind=kCustom, calls=%fused_computation.16.clone | custom fusion | bytes 792576 | tf_op jit(solution)/shard_map/jit(_take)/gather | solution.py:240
  209.7 18.2 %shard_map.60 = (f32[8,8,8,64]{3,2,1,0:T(8,128)}, f32[2,16,64]{2,1,0:T(8,128)}) custom-call(f32[64,8,64]{2,1,0:T(8,128)} %select_bitcast_fusion.8.out_ref, f32[2,16,64]{2,1,0:T(8,128)} %bitcast.297), custom_call_target="tpu_custom_call" | custom-call | tf_op jit(solution)/shard_map/pallas_call | solution.py:203
  229.7 2.6 %gather_fusion.17 = f32[1536,64]{1,0:T(8,128)S(1)} fusion(f32[64,2080]{0,1:T(8,128)S(1)} %constant_dynamic-update-slice_fusion.76, s32[2048]{0:T(1024)S(1)} %pad_clamp_fusion), kind=kCustom, calls=%fused_computation.17.clone | custom fusion | bytes 792576 | tf_op jit(solution)/shard_map/jit(_take)/gather | solution.py:240
  232.8 1.9 multiply_subtract_fusion
  (201 shorter events, 47.7 us)
Async XLA Ops:
  1.1 1.8 copy-start
  5.0 1.8 copy-start.5
  5.0 1.9 copy-start.6
  11.0 36.3 %copy-start.4 = (s32[6,256]{1,0:T(8,128)S(1)}, s32[6,256]{1,0:T(8,128)}, u32[]{:S(2)}) copy-start(s32[6,256]{1,0:T(8,128)} %param.21) | copy-start | bytes 18436
  54.9 1.0 copy-start.3
  56.0 7.3 %copy-start.1 = (f32[512,256]{1,0:T(8,128)}, f32[512,256]{1,0:T(8,128)S(1)}, u32[]{:S(2)}) copy-start(f32[512,256]{1,0:T(8,128)S(1)} %broadcast_multiply_fusion) | copy-start | bytes 1572868
  168.4 1.0 copy-start.2

commit v2 on v0

--- a/solution.py
+++ b/solution.py
@@ -202,15 +202,15 @@
     region_width = region_slabs.shape[1]
     peers = peer_slabs.shape[0]
     slots = peer_slabs.shape[1]
-    outgoing = jnp.take(slab_table, jnp.maximum(peer_slabs.reshape(-1), 0), axis=1)
+    outgoing = slab_table.at[:, jnp.clip(peer_slabs.reshape(-1), 0, slab_table.shape[1] - 1)].get(mode="promise_in_bounds")
     outgoing = outgoing.T.reshape(peers, slots, slab_rows)
-    border = jnp.take(slab_table, region_slabs.reshape(-1), axis=1)
+    border = slab_table.at[:, jnp.clip(region_slabs.reshape(-1), 0, slab_table.shape[1] - 1)].get(mode="promise_in_bounds")
     border = border.T.reshape(2, region_width, slab_rows)
     arrived, beside = exchange(outgoing, border, layers)
     arrived = arrived.reshape(peers * slots, slab_rows).T
     beside = beside.reshape(2 * region_width, slab_rows).T
     combined = jnp.concatenate([slab_table, arrived, beside], axis=1)
-    picked = jnp.take(combined, halo_source, axis=1)
+    picked = combined.at[:, jnp.clip(halo_source, 0, combined.shape[1] - 1)].get(mode="promise_in_bounds")
     return picked
 
 

time: 218 us -> 216 us (level)
  other arithmetic: 30.6 us -> 21 us
  local copies, waits for them, and re-layouts: 69.8 us -> 77.1 us
    gather x24, local copies, waits for them, and re-layouts: 40.7 us -> 48 us  [the longest x12 24.3 us: assemble(): combined.at[:, jnp.clip(halo_source, 0, combined.shape[1] - 1)]]
    reshape x6 -> x0, other arithmetic: 5.24 us -> none  [assemble(): outgoing = outgoing.T.reshape(peers, slots, slab_rows)]
    select_n x15 -> x3, other arithmetic: 4.43 us -> 0.02 us  [the longest x1 0.01 us: assemble(): slab_table.at[:, jnp.clip(peer_slabs.reshape(-1), 0, slab_table.shape[1]...]
where the time goes in v2:
time: 216 us; the launch traced here: 215 us
  Pallas kernels  116 us (54%)
  local copies, waits for them, and re-layouts  77.1 us (36%)
  other arithmetic  21 us (10%)
    pallas_call x6, Pallas kernels, exchange(): pl.pallas_call(exchange_kernel, out_shape=(jax.ShapeDtypeStruct(outgoing....  116 us
    gather x12, local copies, waits for them, and re-layouts, assemble(): combined.at[:, jnp.clip(halo_source, 0, combined.shape[1] - 1)]  24.3 us
    unnamed x60, local copies, waits for them, and re-layouts  16 us
    sub x2, other arithmetic, advect_leaves(): return voxels - advect_scale * speeds * jnp.sqrt(squared)  14.6 us
    gather x6, local copies, waits for them, and re-layouts, assemble(): slab_table.at[:, jnp.clip(peer_slabs.reshape(-1), 0, slab_table.shape[1]...  13.9 us
    gather x6, local copies, waits for them, and re-layouts, assemble(): slab_table.at[:, jnp.clip(region_slabs.reshape(-1), 0, slab_table.shape[1...  9.84 us
    sub x4, other arithmetic, relax_leaves(): return voxels - relax_scale * sign_field * (jnp.sqrt(squared) - 1.0)  5.08 us
    concatenate x6, local copies, waits for them, and re-layouts, assemble(): combined = jnp.concatenate([slab_table, arrived, beside], axis=1)  4.41 us

profile of v2, /device:TPU:1, one launch (start us, length us, event | category | flops | bytes accessed | tf_op | source)
XLA Modules:
  0.0 214.8 jit_solution(1050660956833741680)
XLA Ops:
  7.0 3.6 %gather_fusion = f32[512,192]{1,0:T(8,128)} fusion(f32[192,1536]{0,1:T(8,128)} %get-tuple-element.113, s32[1024]{0:T(1024)S(1)} %get-tuple-element.174), kind=kCustom, calls=%fused_computation | custom fusion | bytes 788480 | tf_op jit(solution)/shard_map/gather | solution.py:205
  10.7 2.6 %gather_fusion.1 = f32[32,192]{1,0:T(8,128)} fusion(f32[192,1536]{0,1:T(8,128)} %get-tuple-element.113, s32[1024]{0:T(1024)S(1)} %get-tuple-element.173), kind=kCustom, calls=%fused_computation.1 | custom fusion | bytes 49280 | tf_op jit(solution)/shard_map/gather | solution.py:207
  13.3 26.2 %shard_map.55 = (f32[64,8,192]{2,1,0:T(8,128)}, f32[2,16,192]{2,1,0:T(8,128)}) custom-call(f32[64,8,192]{2,1,0:T(8,128)} %bitcast.230, f32[2,16,192]{2,1,0:T(8,128)} %bitcast.254), custom_call_target="tpu_custom_call" | custom-call | tf_op jit(solution)/shard_map/pallas_call | solution.py:181
  41.4 4.6 %gather_fusion.2 = f32[1536,192]{1,0:T(8,128)} fusion(f32[192,2080]{0,1:T(8,128)S(1)} %constant_dynamic-update-slice_fusion.6, s32[2048]{0:T(1024)S(1)} %pad_clamp_fusion), kind=kCustom, calls=%fused_computation.2 | custom fusion | bytes 2365440 | tf_op jit(solution)/shard_map/gather | solution.py:213
  46.0 1.9 copy.58
  49.8 7.3 %multiply_subtract_fusion.5 = f32[8,8,8,256]{3,2,1,0:T(8,128)S(1)} fusion(f32[8,8,8,256]{3,2,1,0:T(8,128)S(1)} %bitcast.219, f32[8,8,8,256]{3,2,1,0:T(8,128)S(1)} %bitcast.224, f32[8,8,13,256]{3,2,1,0:T(8,128)S(1)} %slice_subtract_fusion.1, f32[8,13,8,256]{3,2,1,0:T(8,128)S(1)} %slice_subtract_fusion.4, f32[13,8,8,256]{3,2,1,0:T(8,128)S(1)} %slice_subtract_fusion.5), kind=kLoop, calls=%fused_computation.303 | loop fusion | flops 51249152 | bytes 11010048 | tf_op jit(solution)/shard_map/sub | solution.py:101
  58.0 1.6 gather_fusion.3
  60.8 16.4 %shard_map.56 = (f32[64,8,64]{2,1,0:T(8,128)}, f32[2,16,64]{2,1,0:T(8,128)}) custom-call(f32[64,8,64]{2,1,0:T(8,128)} %bitcast.251, f32[2,16,64]{2,1,0:T(8,128)} %bitcast.265), custom_call_target="tpu_custom_call" | custom-call | tf_op jit(solution)/shard_map/pallas_call | solution.py:181
  79.0 2.6 %gather_fusion.5 = f32[1536,64]{1,0:T(8,128)S(1)} fusion(f32[64,2080]{0,1:T(8,128)S(1)} %constant_dynamic-update-slice_fusion.19, s32[2048]{0:T(1024)S(1)} %pad_clamp_fusion), kind=kCustom, calls=%fused_computation.5 | custom fusion | bytes 792576 | tf_op jit(solution)/shard_map/gather | solution.py:213
  86.8 16.7 %shard_map.57 = (f32[64,8,64]{2,1,0:T(8,128)}, f32[2,16,64]{2,1,0:T(8,128)}) custom-call(f32[64,8,64]{2,1,0:T(8,128)} %bitcast.252, f32[2,16,64]{2,1,0:T(8,128)} %bitcast.266), custom_call_target="tpu_custom_call" | custom-call | tf_op jit(solution)/shard_map/pallas_call | solution.py:181
  105.2 2.6 %gather_fusion.8 = f32[1536,64]{1,0:T(8,128)S(1)} fusion(f32[64,2080]{0,1:T(8,128)S(1)} %constant_dynamic-update-slice_fusion.32, s32[2048]{0:T(1024)S(1)} %pad_clamp_fusion), kind=kCustom, calls=%fused_computation.8 | custom fusion | bytes 792576 | tf_op jit(solution)/shard_map/gather | solution.py:213
  115.0 3.6 %gather_fusion.9 = f32[512,192]{1,0:T(8,128)} fusion(f32[192,1536]{0,1:T(8,128)} %get-tuple-element.101, s32[1024]{0:T(1024)S(1)} %get-tuple-element.174), kind=kCustom, calls=%fused_computation.9 | custom fusion | bytes 788480 | tf_op jit(solution)/shard_map/gather | solution.py:205
  118.6 2.6 %gather_fusion.10 = f32[32,192]{1,0:T(8,128)} fusion(f32[192,1536]{0,1:T(8,128)} %get-tuple-element.101, s32[1024]{0:T(1024)S(1)} %get-tuple-element.173), kind=kCustom, calls=%fused_computation.10 | custom fusion | bytes 49280 | tf_op jit(solution)/shard_map/gather | solution.py:207
  121.2 21.7 %shard_map.58 = (f32[64,8,192]{2,1,0:T(8,128)}, f32[2,16,192]{2,1,0:T(8,128)}) custom-call(f32[64,8,192]{2,1,0:T(8,128)} %bitcast.231, f32[2,16,192]{2,1,0:T(8,128)} %bitcast.255), custom_call_target="tpu_custom_call" | custom-call | tf_op jit(solution)/shard_map/pallas_call | solution.py:181
  144.8 4.6 %gather_fusion.11 = f32[1536,192]{1,0:T(8,128)} fusion(f32[192,2080]{0,1:T(8,128)S(1)} %constant_dynamic-update-slice_fusion.45, s32[2048]{0:T(1024)S(1)} %pad_clamp_fusion), kind=kCustom, calls=%fused_computation.11 | custom fusion | bytes 2365440 | tf_op jit(solution)/shard_map/gather | solution.py:213
  149.4 1.9 copy.105
  153.2 7.3 %multiply_subtract_fusion.2 = f32[8,8,8,256]{3,2,1,0:T(8,128)S(1)} fusion(f32[8,8,8,256]{3,2,1,0:T(8,128)S(1)} %multiply_subtract_fusion.3, f32[8,8,8,256]{3,2,1,0:T(8,128)S(1)} %bitcast.225, f32[8,8,13,256]{3,2,1,0:T(8,128)S(1)} %slice_subtract_fusion, f32[8,13,8,256]{3,2,1,0:T(8,128)S(1)} %slice_subtract_fusion.2, ...), kind=kLoop, calls=%fused_computation.299 | loop fusion | flops 51249152 | bytes 11010048 | tf_op jit(solution)/shard_map/sub | solution.py:101
  161.4 1.6 gather_fusion.12
  164.2 17.9 %shard_map.59 = (f32[64,8,64]{2,1,0:T(8,128)}, f32[2,16,64]{2,1,0:T(8,128)}) custom-call(f32[64,8,64]{2,1,0:T(8,128)} %bitcast.253, f32[2,16,64]{2,1,0:T(8,128)} %bitcast.267), custom_call_target="tpu_custom_call" | custom-call | tf_op jit(solution)/shard_map/pallas_call | solution.py:181
  183.8 2.6 %gather_fusion.14 = f32[1536,64]{1,0:T(8,128)S(1)} fusion(f32[64,2080]{0,1:T(8,128)S(1)} %constant_dynamic-update-slice_fusion.58, s32[2048]{0:T(1024)S(1)} %pad_clamp_fusion), kind=kCustom, calls=%fused_computation.14 | custom fusion | bytes 792576 | tf_op jit(solution)/shard_map/gather | solution.py:213
  188.8 1.6 gather_fusion.15
  191.6 16.6 %shard_map.60 = (f32[64,8,64]{2,1,0:T(8,128)}, f32[2,16,64]{2,1,0:T(8,128)}) custom-call(f32[64,8,64]{2,1,0:T(8,128)} %bitcast.250, f32[2,16,64]{2,1,0:T(8,128)} %bitcast.264), custom_call_target="tpu_custom_call" | custom-call | tf_op jit(solution)/shard_map/pallas_call | solution.py:181
  209.9 2.6 %gather_fusion.17 = f32[1536,64]{1,0:T(8,128)S(1)} fusion(f32[64,2080]{0,1:T(8,128)S(1)} %constant_dynamic-update-slice_fusion.71, s32[2048]{0:T(1024)S(1)} %pad_clamp_fusion), kind=kCustom, calls=%fused_computation.17 | custom fusion | bytes 792576 | tf_op jit(solution)/shard_map/gather | solution.py:213
  212.9 1.9 multiply_subtract_fusion
  (182 shorter events, 40.9 us)
Async XLA Ops:
  1.1 1.8 copy-start
  5.0 1.7 copy-start.5
  5.0 1.9 copy-start.6
  10.7 30.7 %copy-start.4 = (s32[6,256]{1,0:T(8,128)S(1)}, s32[6,256]{1,0:T(8,128)}, u32[]{:S(2)}) copy-start(s32[6,256]{1,0:T(8,128)} %param.9) | copy-start | bytes 18436
  48.7 1.0 copy-start.3
  49.8 7.3 %copy-start.1 = (f32[512,256]{1,0:T(8,128)}, f32[512,256]{1,0:T(8,128)S(1)}, u32[]{:S(2)}) copy-start(f32[512,256]{1,0:T(8,128)S(1)} %broadcast_multiply_fusion) | copy-start | bytes 1572868
  152.1 1.0 copy-start.2

commit v3 on v2

--- a/solution.py
+++ b/solution.py
@@ -117,9 +117,12 @@
     return voxels - relax_scale * sign_field * (jnp.sqrt(squared) - 1.0)
 
 
-def exchange_kernel(out_ref, bord_ref, arr_ref, reg_ref, send_sem, recv_sem, rsend_sem, rrecv_sem):
-    peers = lax.axis_size("dev")
+def exchange_kernel(
+    tab_ref, idx_ref, ridx_ref, arr_ref, reg_ref, og_ref, bd_ref, sems
+):
+    peers, slots = og_ref.shape[0], og_ref.shape[1]
     regions = lax.axis_size("group")
+    width = bd_ref.shape[1]
     me = lax.axis_index("dev")
     region = lax.axis_index("group")
     up = lax.rem(region + 1, regions)
@@ -136,21 +139,35 @@
     lax.fori_loop(1, peers, greet, 0)
     pl.semaphore_signal(barrier, inc=1, device_id=(up, me), device_id_type=mesh_ids)
     pl.semaphore_signal(barrier, inc=1, device_id=(down, me), device_id_type=mesh_ids)
+
+    for h in range(2):
+        for p in range(width):
+            source = ridx_ref[h * width + p]
+            bd_ref[h, pl.ds(p, 1), :] = tab_ref[pl.ds(source, 1), :]
+
+    def pack(e, carry):
+        for c in range(slots):
+            source = idx_ref[e * slots + c]
+            og_ref[e, pl.ds(c, 1), :] = tab_ref[pl.ds(source, 1), :]
+        return carry
+
+    lax.fori_loop(0, peers, pack, 0)
+
     pl.semaphore_wait(barrier, peers + 1)
 
     pltpu.make_async_remote_copy(
-        src_ref=bord_ref.at[1],
+        src_ref=bd_ref.at[1],
         dst_ref=reg_ref.at[0],
-        send_sem=rsend_sem,
-        recv_sem=rrecv_sem,
+        send_sem=sems.at[2],
+        recv_sem=sems.at[3],
         device_id=(up, me),
         device_id_type=mesh_ids,
     ).start()
     pltpu.make_async_remote_copy(
-        src_ref=bord_ref.at[0],
+        src_ref=bd_ref.at[0],
         dst_ref=reg_ref.at[1],
-        send_sem=rsend_sem,
-        recv_sem=rrecv_sem,
+        send_sem=sems.at[2],
+        recv_sem=sems.at[3],
         device_id=(down, me),
         device_id_type=mesh_ids,
     ).start()
@@ -158,72 +175,73 @@
     def send(k, carry):
         e = lax.rem(me + k, peers)
         pltpu.make_async_remote_copy(
-            src_ref=out_ref.at[e],
+            src_ref=og_ref.at[e],
             dst_ref=arr_ref.at[me],
-            send_sem=send_sem,
-            recv_sem=recv_sem,
+            send_sem=sems.at[0],
+            recv_sem=sems.at[1],
             device_id=(region, e),
             device_id_type=mesh_ids,
         ).start()
         return carry
 
     lax.fori_loop(1, peers, send, 0)
-    pltpu.make_async_copy(out_ref.at[me], arr_ref.at[me], recv_sem).start()
-
-    pltpu.make_async_copy(out_ref.at[pl.ds(0, peers - 1)], out_ref.at[pl.ds(0, peers - 1)], send_sem).wait()
-    pltpu.make_async_copy(bord_ref, bord_ref, rsend_sem).wait()
-    pltpu.make_async_copy(arr_ref, arr_ref, recv_sem).wait()
-    pltpu.make_async_copy(reg_ref, reg_ref, rrecv_sem).wait()
-
-
-def exchange(outgoing, border, layers):
+    arr_ref[me] = og_ref[me]
+
+    pltpu.make_async_copy(og_ref.at[pl.ds(0, peers - 1)], og_ref.at[pl.ds(0, peers - 1)], sems.at[0]).wait()
+    pltpu.make_async_copy(bd_ref, bd_ref, sems.at[2]).wait()
+    pltpu.make_async_copy(arr_ref.at[pl.ds(0, peers - 1)], arr_ref.at[pl.ds(0, peers - 1)], sems.at[1]).wait()
+    pltpu.make_async_copy(reg_ref, reg_ref, sems.at[3]).wait()
+
+
+def exchange(table, peer_ids, region_ids, peers, layers):
+    entries, slab_rows = table.shape
+    slots = peer_ids.shape[0] // peers
+    width = region_ids.shape[0] // 2
     vmem = pl.BlockSpec(memory_space=pltpu.VMEM)
+    smem = pl.BlockSpec(memory_space=pltpu.SMEM)
     return pl.pallas_call(
         exchange_kernel,
         out_shape=(
-            jax.ShapeDtypeStruct(outgoing.shape, outgoing.dtype),
-            jax.ShapeDtypeStruct(border.shape, border.dtype),
+            jax.ShapeDtypeStruct((peers, slots, slab_rows), table.dtype),
+            jax.ShapeDtypeStruct((2, width, slab_rows), table.dtype),
         ),
-        in_specs=[vmem, vmem],
+        in_specs=[vmem, smem, smem],
         out_specs=(vmem, vmem),
         scratch_shapes=[
-            pltpu.SemaphoreType.DMA(()),
-            pltpu.SemaphoreType.DMA(()),
-            pltpu.SemaphoreType.DMA(()),
-            pltpu.SemaphoreType.DMA(()),
+            pltpu.VMEM((peers, slots, slab_rows), table.dtype),
+            pltpu.VMEM((2, width, slab_rows), table.dtype),
+            pltpu.SemaphoreType.DMA((4,)),
         ],
         compiler_params=pltpu.CompilerParams(collective_id=layers, has_side_effects=True),
-    )(outgoing, border)
-
-
-def assemble(voxels, layers, peer_slabs, region_slabs, halo_source):
+    )(table, peer_ids, region_ids)
+
+
+def assemble(voxels, layers, peer_ids, region_ids, halo_ids):
     slab_table = face_slabs(voxels, layers)
     slab_rows = 64 * layers
-    region_width = region_slabs.shape[1]
-    peers = peer_slabs.shape[0]
-    slots = peer_slabs.shape[1]
-    outgoing = slab_table.at[:, jnp.clip(peer_slabs.reshape(-1), 0, slab_table.shape[1] - 1)].get(mode="promise_in_bounds")
-    outgoing = outgoing.T.reshape(peers, slots, slab_rows)
-    border = slab_table.at[:, jnp.clip(region_slabs.reshape(-1), 0, slab_table.shape[1] - 1)].get(mode="promise_in_bounds")
-    border = border.T.reshape(2, region_width, slab_rows)
-    arrived, beside = exchange(outgoing, border, layers)
-    arrived = arrived.reshape(peers * slots, slab_rows).T
-    beside = beside.reshape(2 * region_width, slab_rows).T
+    peers = lax.axis_size("dev")
+    arrived, beside = exchange(slab_table.T, peer_ids, region_ids, peers, layers)
+    arrived = arrived.reshape(-1, slab_rows).T
+    beside = beside.reshape(-1, slab_rows).T
     combined = jnp.concatenate([slab_table, arrived, beside], axis=1)
-    picked = combined.at[:, jnp.clip(halo_source, 0, combined.shape[1] - 1)].get(mode="promise_in_bounds")
+    picked = combined.at[:, halo_ids].get(mode="promise_in_bounds")
     return picked
 
 
 def per_device(level_set, speed, peer_slabs, region_slabs, halo_source):
     count = level_set.shape[1]
+    local = 6 * count
+    peer_ids = jnp.clip(peer_slabs.reshape(-1), 0, local - 1)
+    region_ids = jnp.clip(region_slabs.reshape(-1), 0, local - 1)
+    halo_ids = jnp.clip(halo_source, 0, local + peer_ids.shape[0] + region_ids.shape[0] - 1)
     voxels = level_set.reshape(8, 8, 8, count)
     speeds = speed.reshape(8, 8, 8, count)
     for offset_step in range(OFFSET_STEPS):
-        picked = assemble(voxels, 3, peer_slabs, region_slabs, halo_source)
+        picked = assemble(voxels, 3, peer_ids, region_ids, halo_ids)
         voxels = advect_leaves(voxels, speeds, picked)
         sign_field = voxels / jnp.sqrt(voxels * voxels + 1.0)
         for redist_pass in range(REDIST_PASSES):
-            picked = assemble(voxels, 1, peer_slabs, region_slabs, halo_source)
+            picked = assemble(voxels, 1, peer_ids, region_ids, halo_ids)
             voxels = relax_leaves(voxels, sign_field, picked)
     return voxels.reshape(512, count)
 

time: 216 us -> 199 us (0.921)
  local copies, waits for them, and re-layouts: 77.1 us -> 57 us
  Pallas kernels: 116 us -> 119 us
    gather x24 -> x12, local copies, waits for them, and re-layouts: 48 us -> 24.4 us  [assemble(): picked = combined.at[:, halo_ids].get(mode='promise_in_bounds')]
    unnamed x60 -> x71, local copies, waits for them, and re-layouts: 16 us -> 19.8 us
    pallas_call x6, Pallas kernels: 116 us -> 119 us  [exchange(): pl.pallas_call(exchange_kernel, out_shape=(jax.ShapeDtypeStruct((peers, s...]
where the time goes in v3:
time: 199 us; the launch traced here: 198 us
  Pallas kernels  119 us (60%)
  local copies, waits for them, and re-layouts  57 us (29%)
  other arithmetic  20.9 us (11%)
    pallas_call x6, Pallas kernels, exchange(): pl.pallas_call(exchange_kernel, out_shape=(jax.ShapeDtypeStruct((peers, s...  119 us
    gather x12, local copies, waits for them, and re-layouts, assemble(): picked = combined.at[:, halo_ids].get(mode='promise_in_bounds')  24.4 us
    unnamed x71, local copies, waits for them, and re-layouts  19.8 us
    sub x2, other arithmetic, advect_leaves(): return voxels - advect_scale * speeds * jnp.sqrt(squared)  14.6 us
    sub x4, other arithmetic, relax_leaves(): return voxels - relax_scale * sign_field * (jnp.sqrt(squared) - 1.0)  5.09 us
    reshape x46, local copies, waits for them, and re-layouts, face_slabs(): piece.reshape(64 * layers, count)  3.99 us

profile of v3, /device:TPU:1, one launch (start us, length us, event | category | flops | bytes accessed | tf_op | source)
XLA Modules:
  0.0 197.8 jit_solution(11506017070054736481)
XLA Ops:
  0.0 1.0 fusion.181
  8.2 26.8 %shard_map.55 = (f32[64,8,192]{2,1,0:T(8,128)}, f32[2,16,192]{2,1,0:T(8,128)}) custom-call(f32[1536,192]{1,0:T(8,128)} %bitcast.219, s32[512]{0:T(512)} %min.120.idx_ref, s32[32]{0:T(128)} %min.123.ridx_ref), custom_call_target="tpu_custom_call" | custom-call | tf_op jit(solution)/shard_map/pallas_call | solution.py:202
  35.0 1.1 bitcast_dynamic-update-slice_fusion.1
  36.2 4.7 %gather_fusion = f32[1536,192]{1,0:T(8,128)} fusion(f32[192,2080]{0,1:T(8,128)S(1)} %constant_dynamic-update-slice_fusion.6, s32[2048]{0:T(1024)S(1)} %pad_clamp_fusion), kind=kCustom, calls=%fused_computation | custom fusion | bytes 2365440 | tf_op jit(solution)/shard_map/gather | solution.py:227
  40.9 1.9 copy.52
  44.7 7.3 %multiply_subtract_fusion.5 = f32[8,8,8,256]{3,2,1,0:T(8,128)S(1)} fusion(f32[8,8,8,256]{3,2,1,0:T(8,128)S(1)} %bitcast.208, f32[8,8,8,256]{3,2,1,0:T(8,128)S(1)} %bitcast.213, f32[8,8,13,256]{3,2,1,0:T(8,128)S(1)} %slice_subtract_fusion.1, f32[8,13,8,256]{3,2,1,0:T(8,128)S(1)} %slice_subtract_fusion.4, f32[13,8,8,256]{3,2,1,0:T(8,128)S(1)} %slice_subtract_fusion.5), kind=kLoop, calls=%fused_computation.291 | loop fusion | flops 51249152 | bytes 11010048 | tf_op jit(solution)/shard_map/sub | solution.py:101
  53.8 16.9 %shard_map.56 = (f32[64,8,64]{2,1,0:T(8,128)}, f32[2,16,64]{2,1,0:T(8,128)}) custom-call(f32[1536,64]{1,0:T(8,128)} %bitcast.225, s32[512]{0:T(512)} %min.120.idx_ref, s32[32]{0:T(128)} %min.123.ridx_ref), custom_call_target="tpu_custom_call" | custom-call | tf_op jit(solution)/shard_map/pallas_call | solution.py:202
  70.7 1.0 bitcast_dynamic-update-slice_fusion.5
  72.4 2.6 %gather_fusion.1 = f32[1536,64]{1,0:T(8,128)S(1)} fusion(f32[64,2080]{0,1:T(8,128)S(1)} %constant_dynamic-update-slice_fusion.19, s32[2048]{0:T(1024)S(1)} %pad_clamp_fusion), kind=kCustom, calls=%fused_computation.1 | custom fusion | bytes 792576 | tf_op jit(solution)/shard_map/gather | solution.py:227
  75.5 1.1 multiply_subtract_fusion.4
  78.4 17.2 %shard_map.57 = (f32[64,8,64]{2,1,0:T(8,128)}, f32[2,16,64]{2,1,0:T(8,128)}) custom-call(f32[1536,64]{1,0:T(8,128)} %bitcast.226, s32[512]{0:T(512)} %min.120.idx_ref, s32[32]{0:T(128)} %min.123.ridx_ref), custom_call_target="tpu_custom_call" | custom-call | tf_op jit(solution)/shard_map/pallas_call | solution.py:202
  97.3 2.6 %gather_fusion.2 = f32[1536,64]{1,0:T(8,128)S(1)} fusion(f32[64,2080]{0,1:T(8,128)S(1)} %constant_dynamic-update-slice_fusion.32, s32[2048]{0:T(1024)S(1)} %pad_clamp_fusion), kind=kCustom, calls=%fused_computation.2 | custom fusion | bytes 792576 | tf_op jit(solution)/shard_map/gather | solution.py:227
  100.4 1.1 multiply_subtract_fusion.3
  107.1 22.3 %shard_map.58 = (f32[64,8,192]{2,1,0:T(8,128)}, f32[2,16,192]{2,1,0:T(8,128)}) custom-call(f32[1536,192]{1,0:T(8,128)} %bitcast.220, s32[512]{0:T(512)} %min.120.idx_ref, s32[32]{0:T(128)} %min.123.ridx_ref), custom_call_target="tpu_custom_call" | custom-call | tf_op jit(solution)/shard_map/pallas_call | solution.py:202
  129.5 1.1 bitcast_dynamic-update-slice_fusion
  130.6 4.7 %gather_fusion.3 = f32[1536,192]{1,0:T(8,128)} fusion(f32[192,2080]{0,1:T(8,128)S(1)} %constant_dynamic-update-slice_fusion.45, s32[2048]{0:T(1024)S(1)} %pad_clamp_fusion), kind=kCustom, calls=%fused_computation.3 | custom fusion | bytes 2365440 | tf_op jit(solution)/shard_map/gather | solution.py:227
  135.3 1.9 copy.99
  139.0 7.3 %multiply_subtract_fusion.2 = f32[8,8,8,256]{3,2,1,0:T(8,128)S(1)} fusion(f32[8,8,8,256]{3,2,1,0:T(8,128)S(1)} %multiply_subtract_fusion.3, f32[8,8,8,256]{3,2,1,0:T(8,128)S(1)} %bitcast.214, f32[8,8,13,256]{3,2,1,0:T(8,128)S(1)} %slice_subtract_fusion, f32[8,13,8,256]{3,2,1,0:T(8,128)S(1)} %slice_subtract_fusion.2, ...), kind=kLoop, calls=%fused_computation.287 | loop fusion | flops 51249152 | bytes 11010048 | tf_op jit(solution)/shard_map/sub | solution.py:101
  148.1 18.3 %shard_map.59 = (f32[64,8,64]{2,1,0:T(8,128)}, f32[2,16,64]{2,1,0:T(8,128)}) custom-call(f32[1536,64]{1,0:T(8,128)} %bitcast.227, s32[512]{0:T(512)} %min.120.idx_ref, s32[32]{0:T(128)} %min.123.ridx_ref), custom_call_target="tpu_custom_call" | custom-call | tf_op jit(solution)/shard_map/pallas_call | solution.py:202
  168.2 2.6 %gather_fusion.4 = f32[1536,64]{1,0:T(8,128)S(1)} fusion(f32[64,2080]{0,1:T(8,128)S(1)} %constant_dynamic-update-slice_fusion.58, s32[2048]{0:T(1024)S(1)} %pad_clamp_fusion), kind=kCustom, calls=%fused_computation.4 | custom fusion | bytes 792576 | tf_op jit(solution)/shard_map/gather | solution.py:227
  171.2 1.1 multiply_subtract_fusion.1
  174.1 17.1 %shard_map.60 = (f32[64,8,64]{2,1,0:T(8,128)}, f32[2,16,64]{2,1,0:T(8,128)}) custom-call(f32[1536,64]{1,0:T(8,128)} %bitcast.228, s32[512]{0:T(512)} %min.120.idx_ref, s32[32]{0:T(128)} %min.123.ridx_ref), custom_call_target="tpu_custom_call" | custom-call | tf_op jit(solution)/shard_map/pallas_call | solution.py:202
  192.9 2.6 %gather_fusion.5 = f32[1536,64]{1,0:T(8,128)S(1)} fusion(f32[64,2080]{0,1:T(8,128)S(1)} %constant_dynamic-update-slice_fusion.71, s32[2048]{0:T(1024)S(1)} %pad_clamp_fusion), kind=kCustom, calls=%fused_computation.5 | custom fusion | bytes 792576 | tf_op jit(solution)/shard_map/gather | solution.py:227
  195.9 1.9 multiply_subtract_fusion
  (178 shorter events, 30.7 us)
Async XLA Ops:
  1.2 1.6 copy-start
  5.0 1.7 copy-start.11
  5.8 1.8 copy-start.12
  8.2 28.0 %copy-start.10 = (s32[6,256]{1,0:T(8,128)S(1)}, s32[6,256]{1,0:T(8,128)}, u32[]{:S(2)}) copy-start(s32[6,256]{1,0:T(8,128)} %param.9) | copy-start | bytes 18436
  35.0 1.1 copy-start.8
  43.6 1.0 copy-start.7
  44.7 7.3 %copy-start.1 = (f32[512,256]{1,0:T(8,128)}, f32[512,256]{1,0:T(8,128)S(1)}, u32[]{:S(2)}) copy-start(f32[512,256]{1,0:T(8,128)S(1)} %broadcast_multiply_fusion) | copy-start | bytes 1572868
  52.9 0.9 copy-start.3
  77.5 0.9 copy-start.4
  129.5 1.1 copy-start.9
  138.0 1.0 copy-start.2
  147.2 0.9 copy-start.5
  173.2 0.9 copy-start.6

commit v4 on v3

--- a/solution.py
+++ b/solution.py
@@ -118,16 +118,24 @@
 
 
 def exchange_kernel(
-    tab_ref, idx_ref, ridx_ref, arr_ref, reg_ref, og_ref, bd_ref, sems
+    tab_hbm, idx_ref, ridx_ref, comb_ref, tab_ref, og_ref, bd_ref, sems
 ):
     peers, slots = og_ref.shape[0], og_ref.shape[1]
+    local = tab_ref.shape[0]
+    width = bd_ref.shape[1]
     regions = lax.axis_size("group")
-    width = bd_ref.shape[1]
     me = lax.axis_index("dev")
     region = lax.axis_index("group")
     up = lax.rem(region + 1, regions)
     down = lax.rem(region + regions - 1, regions)
     mesh_ids = pl.DeviceIdType.MESH
+    arrived = local
+    bordering = local + peers * slots
+
+    fetch = pltpu.make_async_copy(tab_hbm, tab_ref, sems.at[4])
+    fetch.start()
+    keep = pltpu.make_async_copy(tab_hbm, comb_ref.at[pl.ds(0, local)], sems.at[5])
+    keep.start()
 
     barrier = pltpu.get_barrier_semaphore()
 
@@ -140,6 +148,7 @@
     pl.semaphore_signal(barrier, inc=1, device_id=(up, me), device_id_type=mesh_ids)
     pl.semaphore_signal(barrier, inc=1, device_id=(down, me), device_id_type=mesh_ids)
 
+    fetch.wait()
     for h in range(2):
         for p in range(width):
             source = ridx_ref[h * width + p]
@@ -157,7 +166,7 @@
 
     pltpu.make_async_remote_copy(
         src_ref=bd_ref.at[1],
-        dst_ref=reg_ref.at[0],
+        dst_ref=comb_ref.at[pl.ds(bordering, width)],
         send_sem=sems.at[2],
         recv_sem=sems.at[3],
         device_id=(up, me),
@@ -165,18 +174,20 @@
     ).start()
     pltpu.make_async_remote_copy(
         src_ref=bd_ref.at[0],
-        dst_ref=reg_ref.at[1],
+        dst_ref=comb_ref.at[pl.ds(bordering + width, width)],
         send_sem=sems.at[2],
         recv_sem=sems.at[3],
         device_id=(down, me),
         device_id_type=mesh_ids,
     ).start()
 
+    mine = pl.ds(pl.multiple_of(arrived + me * slots, slots), slots)
+
     def send(k, carry):
         e = lax.rem(me + k, peers)
         pltpu.make_async_remote_copy(
             src_ref=og_ref.at[e],
-            dst_ref=arr_ref.at[me],
+            dst_ref=comb_ref.at[mine],
             send_sem=sems.at[0],
             recv_sem=sems.at[1],
             device_id=(region, e),
@@ -185,32 +196,31 @@
         return carry
 
     lax.fori_loop(1, peers, send, 0)
-    arr_ref[me] = og_ref[me]
+    comb_ref[mine, :] = og_ref[me]
 
     pltpu.make_async_copy(og_ref.at[pl.ds(0, peers - 1)], og_ref.at[pl.ds(0, peers - 1)], sems.at[0]).wait()
     pltpu.make_async_copy(bd_ref, bd_ref, sems.at[2]).wait()
-    pltpu.make_async_copy(arr_ref.at[pl.ds(0, peers - 1)], arr_ref.at[pl.ds(0, peers - 1)], sems.at[1]).wait()
-    pltpu.make_async_copy(reg_ref, reg_ref, sems.at[3]).wait()
+    pltpu.make_async_copy(og_ref.at[pl.ds(0, peers - 1)], og_ref.at[pl.ds(0, peers - 1)], sems.at[1]).wait()
+    pltpu.make_async_copy(bd_ref, bd_ref, sems.at[3]).wait()
+    keep.wait()
 
 
 def exchange(table, peer_ids, region_ids, peers, layers):
-    entries, slab_rows = table.shape
+    local, slab_rows = table.shape
     slots = peer_ids.shape[0] // peers
     width = region_ids.shape[0] // 2
     vmem = pl.BlockSpec(memory_space=pltpu.VMEM)
     smem = pl.BlockSpec(memory_space=pltpu.SMEM)
     return pl.pallas_call(
         exchange_kernel,
-        out_shape=(
-            jax.ShapeDtypeStruct((peers, slots, slab_rows), table.dtype),
-            jax.ShapeDtypeStruct((2, width, slab_rows), table.dtype),
-        ),
-        in_specs=[vmem, smem, smem],
-        out_specs=(vmem, vmem),
+        out_shape=jax.ShapeDtypeStruct((local + peers * slots + 2 * width, slab_rows), table.dtype),
+        in_specs=[pl.BlockSpec(memory_space=pl.ANY), smem, smem],
+        out_specs=vmem,
         scratch_shapes=[
+            pltpu.VMEM((local, slab_rows), table.dtype),
             pltpu.VMEM((peers, slots, slab_rows), table.dtype),
             pltpu.VMEM((2, width, slab_rows), table.dtype),
-            pltpu.SemaphoreType.DMA((4,)),
+            pltpu.SemaphoreType.DMA((6,)),
         ],
         compiler_params=pltpu.CompilerParams(collective_id=layers, has_side_effects=True),
     )(table, peer_ids, region_ids)
@@ -218,12 +228,8 @@
 
 def assemble(voxels, layers, peer_ids, region_ids, halo_ids):
     slab_table = face_slabs(voxels, layers)
-    slab_rows = 64 * layers
     peers = lax.axis_size("dev")
-    arrived, beside = exchange(slab_table.T, peer_ids, region_ids, peers, layers)
-    arrived = arrived.reshape(-1, slab_rows).T
-    beside = beside.reshape(-1, slab_rows).T
-    combined = jnp.concatenate([slab_table, arrived, beside], axis=1)
+    combined = exchange(slab_table.T, peer_ids, region_ids, peers, layers).T
     picked = combined.at[:, halo_ids].get(mode="promise_in_bounds")
     return picked
 

time: 199 us -> 186 us (0.935)
  local copies, waits for them, and re-layouts: 57 us -> 43.8 us
    unnamed x71 -> x63, local copies, waits for them, and re-layouts: 19.8 us -> 7.51 us
    gather x12, local copies, waits for them, and re-layouts: 24.4 us -> 27.7 us  [assemble(): picked = combined.at[:, halo_ids].get(mode='promise_in_bounds')]
    concatenate x6 -> x0, local copies, waits for them, and re-layouts: 2.89 us -> none  [assemble(): combined = jnp.concatenate([slab_table, arrived, beside], axis=1)]
where the time goes in v4:
time: 186 us
  Pallas kernels  118 us (63%)
  local copies, waits for them, and re-layouts  43.8 us (24%)
  other arithmetic  22.7 us (12%)
    pallas_call x6, Pallas kernels, exchange(): pl.pallas_call(exchange_kernel, out_shape=jax.ShapeDtypeStruct((local + p...  118 us
    gather x12, local copies, waits for them, and re-layouts, assemble(): picked = combined.at[:, halo_ids].get(mode='promise_in_bounds')  27.7 us
    sub x2, other arithmetic, advect_leaves(): return voxels - advect_scale * speeds * jnp.sqrt(squared)  14.5 us
    unnamed x63, local copies, waits for them, and re-layouts  7.51 us
    sub x4, other arithmetic, relax_leaves(): return voxels - relax_scale * sign_field * (jnp.sqrt(squared) - 1.0)  5.08 us
    reshape x46, local copies, waits for them, and re-layouts, face_slabs(): piece.reshape(64 * layers, count)  3.99 us

profile of v4, /device:TPU:1, one launch (start us, length us, event | category | flops | bytes accessed | tf_op | source)
XLA Modules:
  0.0 185.5 jit_solution(16550730983028663625)
XLA Ops:
  0.0 1.9 %broadcast_multiply_fusion = f32[512,256]{1,0:T(8,128)} fusion(f32[512,256]{1,0:T(8,128)} %param.6), kind=kLoop, calls=%fused_computation.292 | loop fusion | flops 131072 | bytes 1048576 | tf_op jit(solution)/shard_map/mul | solution.py:101
  1.9 1.1 fusion.181
  4.6 0.9 min.120.idx_ref
  6.1 26.8 %shard_map.55 = f32[2080,192]{1,0:T(8,128)} custom-call(f32[1536,192]{1,0:T(8,128)} %bitcast.189, s32[512]{0:T(512)} %min.120.idx_ref, s32[32]{0:T(128)} %min.123.ridx_ref), custom_call_target="tpu_custom_call" | custom-call | tf_op jit(solution)/shard_map/pallas_call | solution.py:214
  33.0 5.3 %gather_fusion = f32[1536,192]{1,0:T(8,128)S(1)} fusion(f32[192,2080]{0,1:T(8,128)} %bitcast.167, s32[2048]{0:T(1024)S(1)} %pad_clamp_fusion), kind=kCustom, calls=%fused_computation | custom fusion | bytes 2365440 | tf_op jit(solution)/shard_map/gather | solution.py:233
  39.7 1.0 copy-done.1
  40.6 7.3 %multiply_subtract_fusion.5 = f32[8,8,8,256]{3,2,1,0:T(8,128)S(1)} fusion(f32[8,8,8,256]{3,2,1,0:T(8,128)S(1)} %bitcast.178, f32[8,8,8,256]{3,2,1,0:T(8,128)S(1)} %bitcast.183, f32[8,8,13,256]{3,2,1,0:T(8,128)S(1)} %slice_subtract_fusion.1, f32[8,13,8,256]{3,2,1,0:T(8,128)S(1)} %slice_subtract_fusion.4, f32[13,8,8,256]{3,2,1,0:T(8,128)S(1)} %slice_subtract_fusion.5), kind=kLoop, calls=%fused_computation.289 | loop fusion | flops 51249152 | bytes 11010048 | tf_op jit(solution)/shard_map/sub | solution.py:101
  49.7 16.7 %shard_map.56 = f32[2080,64]{1,0:T(8,128)} custom-call(f32[1536,64]{1,0:T(8,128)} %bitcast.195, s32[512]{0:T(512)} %min.120.idx_ref, s32[32]{0:T(128)} %min.123.ridx_ref), custom_call_target="tpu_custom_call" | custom-call | tf_op jit(solution)/shard_map/pallas_call | solution.py:214
  66.4 3.8 %gather_fusion.1 = f32[1536,64]{1,0:T(8,128)S(1)} fusion(f32[64,2080]{0,1:T(8,128)} %bitcast.170, s32[2048]{0:T(1024)S(1)} %pad_clamp_fusion), kind=kCustom, calls=%fused_computation.1 | custom fusion | bytes 792576 | tf_op jit(solution)/shard_map/gather | solution.py:233
  70.7 1.1 multiply_subtract_fusion.4
  73.5 17.0 %shard_map.57 = f32[2080,64]{1,0:T(8,128)} custom-call(f32[1536,64]{1,0:T(8,128)} %bitcast.196, s32[512]{0:T(512)} %min.120.idx_ref, s32[32]{0:T(128)} %min.123.ridx_ref), custom_call_target="tpu_custom_call" | custom-call | tf_op jit(solution)/shard_map/pallas_call | solution.py:214
  90.5 3.8 %gather_fusion.2 = f32[1536,64]{1,0:T(8,128)S(1)} fusion(f32[64,2080]{0,1:T(8,128)} %bitcast.171, s32[2048]{0:T(1024)S(1)} %pad_clamp_fusion), kind=kCustom, calls=%fused_computation.2 | custom fusion | bytes 792576 | tf_op jit(solution)/shard_map/gather | solution.py:233
  94.8 1.1 multiply_subtract_fusion.3
  97.3 1.1 copy-done.4
  98.4 22.2 %shard_map.58 = f32[2080,192]{1,0:T(8,128)} custom-call(f32[1536,192]{1,0:T(8,128)} %bitcast.190, s32[512]{0:T(512)} %min.120.idx_ref, s32[32]{0:T(128)} %min.123.ridx_ref), custom_call_target="tpu_custom_call" | custom-call | tf_op jit(solution)/shard_map/pallas_call | solution.py:214
  120.6 5.3 %gather_fusion.3 = f32[1536,192]{1,0:T(8,128)S(1)} fusion(f32[192,2080]{0,1:T(8,128)} %bitcast.168, s32[2048]{0:T(1024)S(1)} %pad_clamp_fusion), kind=kCustom, calls=%fused_computation.3 | custom fusion | bytes 2365440 | tf_op jit(solution)/shard_map/gather | solution.py:233
  127.3 1.0 copy-done.2
  128.2 7.3 %multiply_subtract_fusion.2 = f32[8,8,8,256]{3,2,1,0:T(8,128)S(1)} fusion(f32[8,8,8,256]{3,2,1,0:T(8,128)S(1)} %multiply_subtract_fusion.3, f32[8,8,8,256]{3,2,1,0:T(8,128)S(1)} %bitcast.184, f32[8,8,13,256]{3,2,1,0:T(8,128)S(1)} %slice_subtract_fusion, f32[8,13,8,256]{3,2,1,0:T(8,128)S(1)} %slice_subtract_fusion.2, ...), kind=kLoop, calls=%fused_computation.285 | loop fusion | flops 51249152 | bytes 11010048 | tf_op jit(solution)/shard_map/sub | solution.py:101
  137.3 18.2 %shard_map.59 = f32[2080,64]{1,0:T(8,128)} custom-call(f32[1536,64]{1,0:T(8,128)} %bitcast.197, s32[512]{0:T(512)} %min.120.idx_ref, s32[32]{0:T(128)} %min.123.ridx_ref), custom_call_target="tpu_custom_call" | custom-call | tf_op jit(solution)/shard_map/pallas_call | solution.py:214
  155.4 3.8 %gather_fusion.4 = f32[1536,64]{1,0:T(8,128)S(1)} fusion(f32[64,2080]{0,1:T(8,128)} %bitcast.172, s32[2048]{0:T(1024)S(1)} %pad_clamp_fusion), kind=kCustom, calls=%fused_computation.4 | custom fusion | bytes 792576 | tf_op jit(solution)/shard_map/gather | solution.py:233
  159.7 1.1 multiply_subtract_fusion.1
  162.5 16.8 %shard_map.60 = f32[2080,64]{1,0:T(8,128)} custom-call(f32[1536,64]{1,0:T(8,128)} %bitcast.198, s32[512]{0:T(512)} %min.120.idx_ref, s32[32]{0:T(128)} %min.123.ridx_ref), custom_call_target="tpu_custom_call" | custom-call | tf_op jit(solution)/shard_map/pallas_call | solution.py:214
  179.4 3.8 %gather_fusion.5 = f32[1536,64]{1,0:T(8,128)S(1)} fusion(f32[64,2080]{0,1:T(8,128)} %bitcast.169, s32[2048]{0:T(1024)S(1)} %pad_clamp_fusion), kind=kCustom, calls=%fused_computation.5 | custom fusion | bytes 792576 | tf_op jit(solution)/shard_map/gather | solution.py:233
  183.7 1.9 %multiply_subtract_fusion = f32[8,8,8,256]{3,2,1,0:T(8,128)} fusion(f32[8,8,8,256]{3,2,1,0:T(8,128)S(1)} %multiply_subtract_fusion.1, f32[8,8,1,256]{3,2,1,0:T(1,128)S(1)} %copy.99, f32[8,8,1,256]{3,2,1,0:T(1,128)S(1)} %copy.98, f32[8,1,8,256]{3,2,1,0:T(8,128)S(1)} %get-tuple-element.55, f32[8,1,8,256]{3,2,1,0:T(8,128)S(1)} %get-tuple-element.56, ...), kind=kLoop, calls=%fused_computation.282 | loop fusion | flops 7208960 | bytes 1966080 | tf_op jit(solution)/shard_map/sub | solution.py:117
  (164 shorter events, 14.2 us)
Async XLA Ops:
  1.9 1.4 copy-start
  3.8 0.7 copy-start.10
  3.8 1.7 copy-start.11
  4.4 1.8 copy-start.3
  6.1 26.8 %copy-start.9 = (s32[6,256]{1,0:T(8,128)S(1)}, s32[6,256]{1,0:T(8,128)}, u32[]{:S(2)}) copy-start(s32[6,256]{1,0:T(8,128)} %param.9) | copy-start | bytes 18436
  39.6 1.0 copy-start.1
  48.8 0.9 copy-start.5
  72.6 0.9 copy-start.6
  97.2 1.1 copy-start.4
  127.2 1.0 copy-start.2
  136.4 0.9 copy-start.7
  161.6 0.9 copy-start.8

commit v5 on v4

--- a/solution.py
+++ b/solution.py
@@ -118,7 +118,7 @@
 
 
 def exchange_kernel(
-    tab_hbm, idx_ref, ridx_ref, comb_ref, tab_ref, og_ref, bd_ref, sems
+    tab_ref, idx_ref, ridx_ref, comb_ref, og_ref, bd_ref, sems
 ):
     peers, slots = og_ref.shape[0], og_ref.shape[1]
     local = tab_ref.shape[0]
@@ -132,9 +132,7 @@
     arrived = local
     bordering = local + peers * slots
 
-    fetch = pltpu.make_async_copy(tab_hbm, tab_ref, sems.at[4])
-    fetch.start()
-    keep = pltpu.make_async_copy(tab_hbm, comb_ref.at[pl.ds(0, local)], sems.at[5])
+    keep = pltpu.make_async_copy(tab_ref, comb_ref.at[pl.ds(0, local)], sems.at[4])
     keep.start()
 
     barrier = pltpu.get_barrier_semaphore()
@@ -148,7 +146,6 @@
     pl.semaphore_signal(barrier, inc=1, device_id=(up, me), device_id_type=mesh_ids)
     pl.semaphore_signal(barrier, inc=1, device_id=(down, me), device_id_type=mesh_ids)
 
-    fetch.wait()
     for h in range(2):
         for p in range(width):
             source = ridx_ref[h * width + p]
@@ -213,17 +210,18 @@
     smem = pl.BlockSpec(memory_space=pltpu.SMEM)
     return pl.pallas_call(
         exchange_kernel,
-        out_shape=jax.ShapeDtypeStruct((local + peers * slots + 2 * width, slab_rows), table.dtype),
-        in_specs=[pl.BlockSpec(memory_space=pl.ANY), smem, smem],
+        out_shape=(pltpu.VMEM if layers == 1 else jax.ShapeDtypeStruct)(
+            (local + peers * slots + 2 * width, slab_rows), table.dtype
+        ),
+        in_specs=[vmem, smem, smem],
         out_specs=vmem,
         scratch_shapes=[
-            pltpu.VMEM((local, slab_rows), table.dtype),
             pltpu.VMEM((peers, slots, slab_rows), table.dtype),
             pltpu.VMEM((2, width, slab_rows), table.dtype),
-            pltpu.SemaphoreType.DMA((6,)),
+            pltpu.SemaphoreType.DMA((5,)),
         ],
         compiler_params=pltpu.CompilerParams(collective_id=layers, has_side_effects=True),
-    )(table, peer_ids, region_ids)
+    )(pltpu.with_memory_space_constraint(table, pltpu.VMEM), peer_ids, region_ids)
 
 
 def assemble(voxels, layers, peer_ids, region_ids, halo_ids):

time: 186 us -> 174 us (0.935)
  local copies, waits for them, and re-layouts: 43.8 us -> 34.7 us
  Pallas kernels: 118 us -> 115 us
    gather x12, local copies, waits for them, and re-layouts: 27.7 us -> 22.8 us  [assemble(): picked = combined.at[:, halo_ids].get(mode='promise_in_bounds')]
    unnamed x63 -> x55, local copies, waits for them, and re-layouts: 7.51 us -> 3.48 us
    pallas_call x6, Pallas kernels: 118 us -> 115 us  [exchange(): pl.pallas_call(exchange_kernel, out_shape=(pltpu.VMEM if layers == 1 else...]
where the time goes in v5:
time: 174 us; the launch traced here: 173 us
  Pallas kernels  115 us (66%)
  local copies, waits for them, and re-layouts  34.7 us (20%)
  other arithmetic  22.7 us (13%)
    pallas_call x6, Pallas kernels, exchange(): pl.pallas_call(exchange_kernel, out_shape=(pltpu.VMEM if layers == 1 else...  115 us
    gather x12, local copies, waits for them, and re-layouts, assemble(): picked = combined.at[:, halo_ids].get(mode='promise_in_bounds')  22.8 us
    sub x2, other arithmetic, advect_leaves(): return voxels - advect_scale * speeds * jnp.sqrt(squared)  14.5 us
    sub x4, other arithmetic, relax_leaves(): return voxels - relax_scale * sign_field * (jnp.sqrt(squared) - 1.0)  5.08 us
    reshape x46, local copies, waits for them, and re-layouts, face_slabs(): piece.reshape(64 * layers, count)  3.99 us
    unnamed x55, local copies, waits for them, and re-layouts  3.48 us

profile of v5, /device:TPU:1, one launch (start us, length us, event | category | flops | bytes accessed | tf_op | source)
XLA Modules:
  0.0 173.5 jit_solution(3172001585418314115)
XLA Ops:
  0.0 1.9 %broadcast_multiply_fusion = f32[512,256]{1,0:T(8,128)} fusion(f32[512,256]{1,0:T(8,128)} %param.6), kind=kLoop, calls=%fused_computation.292 | loop fusion | flops 131072 | bytes 1048576 | tf_op jit(solution)/shard_map/mul | solution.py:101
  1.9 1.1 fusion.181
  4.6 0.7 min.120.idx_ref
  5.3 0.7 min.123.ridx_ref
  5.9 26.9 %shard_map.55 = f32[2080,192]{1,0:T(8,128)} custom-call(f32[1536,192]{1,0:T(8,128)S(1)} %bitcast.171, s32[512]{0:T(512)} %min.120.idx_ref, s32[32]{0:T(128)} %min.123.ridx_ref), custom_call_target="tpu_custom_call" | custom-call | tf_op jit(solution)/shard_map/pallas_call | solution.py:211
  32.9 5.3 %gather_fusion = f32[1536,192]{1,0:T(8,128)S(1)} fusion(f32[192,2080]{0,1:T(8,128)} %bitcast.177, s32[2048]{0:T(1024)S(1)} %pad_clamp_fusion), kind=kCustom, calls=%fused_computation | custom fusion | bytes 2365440 | tf_op jit(solution)/shard_map/gather | solution.py:231
  39.6 1.0 copy-done.1
  40.5 7.3 %multiply_subtract_fusion.5 = f32[8,8,8,256]{3,2,1,0:T(8,128)S(1)} fusion(f32[8,8,8,256]{3,2,1,0:T(8,128)S(1)} %bitcast.184, f32[8,8,8,256]{3,2,1,0:T(8,128)S(1)} %bitcast.189, f32[8,8,13,256]{3,2,1,0:T(8,128)S(1)} %slice_subtract_fusion.1, f32[8,13,8,256]{3,2,1,0:T(8,128)S(1)} %slice_subtract_fusion.4, f32[13,8,8,256]{3,2,1,0:T(8,128)S(1)} %slice_subtract_fusion.5), kind=kLoop, calls=%fused_computation.289 | loop fusion | flops 51249152 | bytes 11010048 | tf_op jit(solution)/shard_map/sub | solution.py:101
  48.7 15.9 %shard_map.56 = f32[2080,64]{1,0:T(8,128)S(1)} custom-call(f32[1536,64]{1,0:T(8,128)S(1)} %bitcast.173, s32[512]{0:T(512)} %min.120.idx_ref, s32[32]{0:T(128)} %min.123.ridx_ref), custom_call_target="tpu_custom_call" | custom-call | tf_op jit(solution)/shard_map/pallas_call | solution.py:211
  64.6 2.6 %gather_fusion.1 = f32[1536,64]{1,0:T(8,128)S(1)} fusion(f32[64,2080]{0,1:T(8,128)S(1)} %bitcast.168, s32[2048]{0:T(1024)S(1)} %pad_clamp_fusion), kind=kCustom, calls=%fused_computation.1 | custom fusion | bytes 792576 | tf_op jit(solution)/shard_map/gather | solution.py:231
  67.6 1.1 multiply_subtract_fusion.4
  69.6 16.2 %shard_map.57 = f32[2080,64]{1,0:T(8,128)S(1)} custom-call(f32[1536,64]{1,0:T(8,128)S(1)} %bitcast.174, s32[512]{0:T(512)} %min.120.idx_ref, s32[32]{0:T(128)} %min.123.ridx_ref), custom_call_target="tpu_custom_call" | custom-call | tf_op jit(solution)/shard_map/pallas_call | solution.py:211
  85.9 2.6 %gather_fusion.2 = f32[1536,64]{1,0:T(8,128)S(1)} fusion(f32[64,2080]{0,1:T(8,128)S(1)} %bitcast.169, s32[2048]{0:T(1024)S(1)} %pad_clamp_fusion), kind=kCustom, calls=%fused_computation.2 | custom fusion | bytes 792576 | tf_op jit(solution)/shard_map/gather | solution.py:231
  89.5 1.1 multiply_subtract_fusion.3
  92.0 22.4 %shard_map.58 = f32[2080,192]{1,0:T(8,128)} custom-call(f32[1536,192]{1,0:T(8,128)S(1)} %bitcast.172, s32[512]{0:T(512)} %min.120.idx_ref, s32[32]{0:T(128)} %min.123.ridx_ref), custom_call_target="tpu_custom_call" | custom-call | tf_op jit(solution)/shard_map/pallas_call | solution.py:211
  114.4 5.3 %gather_fusion.3 = f32[1536,192]{1,0:T(8,128)S(1)} fusion(f32[192,2080]{0,1:T(8,128)} %bitcast.178, s32[2048]{0:T(1024)S(1)} %pad_clamp_fusion), kind=kCustom, calls=%fused_computation.3 | custom fusion | bytes 2365440 | tf_op jit(solution)/shard_map/gather | solution.py:231
  121.1 1.0 copy-done.2
  122.0 7.3 %multiply_subtract_fusion.2 = f32[8,8,8,256]{3,2,1,0:T(8,128)S(1)} fusion(f32[8,8,8,256]{3,2,1,0:T(8,128)S(1)} %multiply_subtract_fusion.3, f32[8,8,8,256]{3,2,1,0:T(8,128)S(1)} %bitcast.190, f32[8,8,13,256]{3,2,1,0:T(8,128)S(1)} %slice_subtract_fusion, f32[8,13,8,256]{3,2,1,0:T(8,128)S(1)} %slice_subtract_fusion.2, ...), kind=kLoop, calls=%fused_computation.285 | loop fusion | flops 51249152 | bytes 11010048 | tf_op jit(solution)/shard_map/sub | solution.py:101
  130.1 17.4 %shard_map.59 = f32[2080,64]{1,0:T(8,128)S(1)} custom-call(f32[1536,64]{1,0:T(8,128)S(1)} %bitcast.175, s32[512]{0:T(512)} %min.120.idx_ref, s32[32]{0:T(128)} %min.123.ridx_ref), custom_call_target="tpu_custom_call" | custom-call | tf_op jit(solution)/shard_map/pallas_call | solution.py:211
  147.5 2.6 %gather_fusion.4 = f32[1536,64]{1,0:T(8,128)S(1)} fusion(f32[64,2080]{0,1:T(8,128)S(1)} %bitcast.170, s32[2048]{0:T(1024)S(1)} %pad_clamp_fusion), kind=kCustom, calls=%fused_computation.4 | custom fusion | bytes 792576 | tf_op jit(solution)/shard_map/gather | solution.py:231
  150.6 1.1 multiply_subtract_fusion.1
  152.5 16.0 %shard_map.60 = f32[2080,64]{1,0:T(8,128)S(1)} custom-call(f32[1536,64]{1,0:T(8,128)S(1)} %bitcast.176, s32[512]{0:T(512)} %min.120.idx_ref, s32[32]{0:T(128)} %min.123.ridx_ref), custom_call_target="tpu_custom_call" | custom-call | tf_op jit(solution)/shard_map/pallas_call | solution.py:211
  168.6 2.6 %gather_fusion.5 = f32[1536,64]{1,0:T(8,128)S(1)} fusion(f32[64,2080]{0,1:T(8,128)S(1)} %bitcast.167, s32[2048]{0:T(1024)S(1)} %pad_clamp_fusion), kind=kCustom, calls=%fused_computation.5 | custom fusion | bytes 792576 | tf_op jit(solution)/shard_map/gather | solution.py:231
  171.6 1.9 %multiply_subtract_fusion = f32[8,8,8,256]{3,2,1,0:T(8,128)} fusion(f32[8,8,8,256]{3,2,1,0:T(8,128)S(1)} %multiply_subtract_fusion.1, f32[8,8,1,256]{3,2,1,0:T(1,128)S(1)} %copy.99, f32[8,8,1,256]{3,2,1,0:T(1,128)S(1)} %copy.98, f32[8,1,8,256]{3,2,1,0:T(8,128)S(1)} %get-tuple-element.55, f32[8,1,8,256]{3,2,1,0:T(8,128)S(1)} %get-tuple-element.56, ...), kind=kLoop, calls=%fused_computation.282 | loop fusion | flops 7208960 | bytes 1966080 | tf_op jit(solution)/shard_map/sub | solution.py:117
  (156 shorter events, 10.7 us)
Async XLA Ops:
  1.9 1.4 copy-start
  3.8 0.7 copy-start.6
  3.8 1.4 copy-start.7
  5.9 26.9 %copy-start.5 = (s32[6,256]{1,0:T(8,128)S(1)}, s32[6,256]{1,0:T(8,128)}, u32[]{:S(2)}) copy-start(s32[6,256]{1,0:T(8,128)} %param.9) | copy-start | bytes 18436
  39.5 1.0 copy-start.1
  68.7 0.8 copy-start.3
  88.5 1.0 copy-start.4
  121.0 1.0 copy-start.2

commit v6 on v5

--- a/solution.py
+++ b/solution.py
@@ -117,6 +117,19 @@
     return voxels - relax_scale * sign_field * (jnp.sqrt(squared) - 1.0)
 
 
+def far_first(me, peers):
+    if peers != 64:
+        return [lax.rem(me + k, peers) for k in range(1, peers)]
+    moves = [
+        (dz, dx, dc) for dz in range(8) for dx in range(4) for dc in range(2) if (dz, dx, dc) != (0, 0, 0)
+    ]
+    moves.sort(key=lambda m: -(min(m[0], 8 - m[0]) + min(m[1], 4 - m[1])))
+    z, x, c = me // 8, (me // 2) % 4, me % 2
+    return [
+        lax.rem(z + dz, 8) * 8 + lax.rem(x + dx, 4) * 2 + lax.rem(c + dc, 2) for dz, dx, dc in moves
+    ]
+
+
 def exchange_kernel(
     tab_ref, idx_ref, ridx_ref, comb_ref, og_ref, bd_ref, sems
 ):
@@ -137,12 +150,9 @@
 
     barrier = pltpu.get_barrier_semaphore()
 
-    def greet(k, carry):
-        e = lax.rem(me + k, peers)
+    targets = far_first(me, peers)
+    for e in targets:
         pl.semaphore_signal(barrier, inc=1, device_id=(region, e), device_id_type=mesh_ids)
-        return carry
-
-    lax.fori_loop(1, peers, greet, 0)
     pl.semaphore_signal(barrier, inc=1, device_id=(up, me), device_id_type=mesh_ids)
     pl.semaphore_signal(barrier, inc=1, device_id=(down, me), device_id_type=mesh_ids)
 
@@ -180,8 +190,7 @@
 
     mine = pl.ds(pl.multiple_of(arrived + me * slots, slots), slots)
 
-    def send(k, carry):
-        e = lax.rem(me + k, peers)
+    for e in targets:
         pltpu.make_async_remote_copy(
             src_ref=og_ref.at[e],
             dst_ref=comb_ref.at[mine],
@@ -190,9 +199,6 @@
             device_id=(region, e),
             device_id_type=mesh_ids,
         ).start()
-        return carry
-
-    lax.fori_loop(1, peers, send, 0)
     comb_ref[mine, :] = og_ref[me]
 
     pltpu.make_async_copy(og_ref.at[pl.ds(0, peers - 1)], og_ref.at[pl.ds(0, peers - 1)], sems.at[0]).wait()

time: 174 us -> 163 us (0.937)
  Pallas kernels: 115 us -> 104 us
    pallas_call x6, Pallas kernels: 115 us -> 104 us  [exchange(): pl.pallas_call(exchange_kernel, out_shape=(pltpu.VMEM if layers == 1 else...]
where the time goes in v6:
time: 163 us
  Pallas kernels  104 us (64%)
  local copies, waits for them, and re-layouts  34.9 us (21%)
  other arithmetic  22.7 us (14%)
    pallas_call x6, Pallas kernels, exchange(): pl.pallas_call(exchange_kernel, out_shape=(pltpu.VMEM if layers == 1 else...  104 us
    gather x12, local copies, waits for them, and re-layouts, assemble(): picked = combined.at[:, halo_ids].get(mode='promise_in_bounds')  23 us
    sub x2, other arithmetic, advect_leaves(): return voxels - advect_scale * speeds * jnp.sqrt(squared)  14.5 us
    sub x4, other arithmetic, relax_leaves(): return voxels - relax_scale * sign_field * (jnp.sqrt(squared) - 1.0)  5.08 us
    reshape x46, local copies, waits for them, and re-layouts, face_slabs(): piece.reshape(64 * layers, count)  3.99 us
    unnamed x55, local copies, waits for them, and re-layouts  3.48 us

profile of v6, /device:TPU:1, one launch (start us, length us, event | category | flops | bytes accessed | tf_op | source)
XLA Modules:
  0.0 162.8 jit_solution(15747872051176609132)
XLA Ops:
  0.0 1.9 %broadcast_multiply_fusion = f32[512,256]{1,0:T(8,128)} fusion(f32[512,256]{1,0:T(8,128)} %param.6), kind=kLoop, calls=%fused_computation.292 | loop fusion | flops 131072 | bytes 1048576 | tf_op jit(solution)/shard_map/mul | solution.py:101
  1.9 1.1 fusion.181
  4.6 0.7 min.120.idx_ref
  5.3 0.7 min.123.ridx_ref
  5.9 26.5 %shard_map.55 = f32[2080,192]{1,0:T(8,128)} custom-call(f32[1536,192]{1,0:T(8,128)S(1)} %bitcast.171, s32[512]{0:T(512)} %min.120.idx_ref, s32[32]{0:T(128)} %min.123.ridx_ref), custom_call_target="tpu_custom_call" | custom-call | tf_op jit(solution)/shard_map/pallas_call | solution.py:217
  32.5 5.3 %gather_fusion = f32[1536,192]{1,0:T(8,128)S(1)} fusion(f32[192,2080]{0,1:T(8,128)} %bitcast.177, s32[2048]{0:T(1024)S(1)} %pad_clamp_fusion), kind=kCustom, calls=%fused_computation | custom fusion | bytes 2365440 | tf_op jit(solution)/shard_map/gather | solution.py:237
  39.2 1.0 copy-done.1
  40.2 7.3 %multiply_subtract_fusion.5 = f32[8,8,8,256]{3,2,1,0:T(8,128)S(1)} fusion(f32[8,8,8,256]{3,2,1,0:T(8,128)S(1)} %bitcast.184, f32[8,8,8,256]{3,2,1,0:T(8,128)S(1)} %bitcast.189, f32[8,8,13,256]{3,2,1,0:T(8,128)S(1)} %slice_subtract_fusion.1, f32[8,13,8,256]{3,2,1,0:T(8,128)S(1)} %slice_subtract_fusion.4, f32[13,8,8,256]{3,2,1,0:T(8,128)S(1)} %slice_subtract_fusion.5), kind=kLoop, calls=%fused_computation.289 | loop fusion | flops 51249152 | bytes 11010048 | tf_op jit(solution)/shard_map/sub | solution.py:101
  48.3 14.2 %shard_map.56 = f32[2080,64]{1,0:T(8,128)S(1)} custom-call(f32[1536,64]{1,0:T(8,128)S(1)} %bitcast.173, s32[512]{0:T(512)} %min.120.idx_ref, s32[32]{0:T(128)} %min.123.ridx_ref), custom_call_target="tpu_custom_call" | custom-call | tf_op jit(solution)/shard_map/pallas_call | solution.py:217
  62.5 2.6 %gather_fusion.1 = f32[1536,64]{1,0:T(8,128)S(1)} fusion(f32[64,2080]{0,1:T(8,128)S(1)} %bitcast.168, s32[2048]{0:T(1024)S(1)} %pad_clamp_fusion), kind=kCustom, calls=%fused_computation.1 | custom fusion | bytes 792576 | tf_op jit(solution)/shard_map/gather | solution.py:237
  65.5 1.1 multiply_subtract_fusion.4
  67.5 14.5 %shard_map.57 = f32[2080,64]{1,0:T(8,128)S(1)} custom-call(f32[1536,64]{1,0:T(8,128)S(1)} %bitcast.174, s32[512]{0:T(512)} %min.120.idx_ref, s32[32]{0:T(128)} %min.123.ridx_ref), custom_call_target="tpu_custom_call" | custom-call | tf_op jit(solution)/shard_map/pallas_call | solution.py:217
  82.0 2.8 %gather_fusion.2 = f32[1536,64]{1,0:T(8,128)S(1)} fusion(f32[64,2080]{0,1:T(8,128)S(1)} %bitcast.169, s32[2048]{0:T(1024)S(1)} %pad_clamp_fusion), kind=kCustom, calls=%fused_computation.2 | custom fusion | bytes 792576 | tf_op jit(solution)/shard_map/gather | solution.py:237
  85.8 1.1 multiply_subtract_fusion.3
  88.3 20.6 %shard_map.58 = f32[2080,192]{1,0:T(8,128)} custom-call(f32[1536,192]{1,0:T(8,128)S(1)} %bitcast.172, s32[512]{0:T(512)} %min.120.idx_ref, s32[32]{0:T(128)} %min.123.ridx_ref), custom_call_target="tpu_custom_call" | custom-call | tf_op jit(solution)/shard_map/pallas_call | solution.py:217
  108.9 5.3 %gather_fusion.3 = f32[1536,192]{1,0:T(8,128)S(1)} fusion(f32[192,2080]{0,1:T(8,128)} %bitcast.178, s32[2048]{0:T(1024)S(1)} %pad_clamp_fusion), kind=kCustom, calls=%fused_computation.3 | custom fusion | bytes 2365440 | tf_op jit(solution)/shard_map/gather | solution.py:237
  115.6 1.0 copy-done.2
  116.6 7.3 %multiply_subtract_fusion.2 = f32[8,8,8,256]{3,2,1,0:T(8,128)S(1)} fusion(f32[8,8,8,256]{3,2,1,0:T(8,128)S(1)} %multiply_subtract_fusion.3, f32[8,8,8,256]{3,2,1,0:T(8,128)S(1)} %bitcast.190, f32[8,8,13,256]{3,2,1,0:T(8,128)S(1)} %slice_subtract_fusion, f32[8,13,8,256]{3,2,1,0:T(8,128)S(1)} %slice_subtract_fusion.2, ...), kind=kLoop, calls=%fused_computation.285 | loop fusion | flops 51249152 | bytes 11010048 | tf_op jit(solution)/shard_map/sub | solution.py:101
  124.7 14.6 %shard_map.59 = f32[2080,64]{1,0:T(8,128)S(1)} custom-call(f32[1536,64]{1,0:T(8,128)S(1)} %bitcast.175, s32[512]{0:T(512)} %min.120.idx_ref, s32[32]{0:T(128)} %min.123.ridx_ref), custom_call_target="tpu_custom_call" | custom-call | tf_op jit(solution)/shard_map/pallas_call | solution.py:217
  139.3 2.6 %gather_fusion.4 = f32[1536,64]{1,0:T(8,128)S(1)} fusion(f32[64,2080]{0,1:T(8,128)S(1)} %bitcast.170, s32[2048]{0:T(1024)S(1)} %pad_clamp_fusion), kind=kCustom, calls=%fused_computation.4 | custom fusion | bytes 792576 | tf_op jit(solution)/shard_map/gather | solution.py:237
  142.3 1.1 multiply_subtract_fusion.1
  144.2 13.6 %shard_map.60 = f32[2080,64]{1,0:T(8,128)S(1)} custom-call(f32[1536,64]{1,0:T(8,128)S(1)} %bitcast.176, s32[512]{0:T(512)} %min.120.idx_ref, s32[32]{0:T(128)} %min.123.ridx_ref), custom_call_target="tpu_custom_call" | custom-call | tf_op jit(solution)/shard_map/pallas_call | solution.py:217
  157.9 2.6 %gather_fusion.5 = f32[1536,64]{1,0:T(8,128)S(1)} fusion(f32[64,2080]{0,1:T(8,128)S(1)} %bitcast.167, s32[2048]{0:T(1024)S(1)} %pad_clamp_fusion), kind=kCustom, calls=%fused_computation.5 | custom fusion | bytes 792576 | tf_op jit(solution)/shard_map/gather | solution.py:237
  160.9 1.9 %multiply_subtract_fusion = f32[8,8,8,256]{3,2,1,0:T(8,128)} fusion(f32[8,8,8,256]{3,2,1,0:T(8,128)S(1)} %multiply_subtract_fusion.1, f32[8,8,1,256]{3,2,1,0:T(1,128)S(1)} %copy.99, f32[8,8,1,256]{3,2,1,0:T(1,128)S(1)} %copy.98, f32[8,1,8,256]{3,2,1,0:T(8,128)S(1)} %get-tuple-element.55, f32[8,1,8,256]{3,2,1,0:T(8,128)S(1)} %get-tuple-element.56, ...), kind=kLoop, calls=%fused_computation.282 | loop fusion | flops 7208960 | bytes 1966080 | tf_op jit(solution)/shard_map/sub | solution.py:117
  (156 shorter events, 10.7 us)
Async XLA Ops:
  1.9 1.4 copy-start
  3.8 0.7 copy-start.6
  3.8 1.4 copy-start.7
  5.9 26.5 %copy-start.5 = (s32[6,256]{1,0:T(8,128)S(1)}, s32[6,256]{1,0:T(8,128)}, u32[]{:S(2)}) copy-start(s32[6,256]{1,0:T(8,128)} %param.9) | copy-start | bytes 18436
  39.1 1.0 copy-start.1
  66.6 0.8 copy-start.3
  84.8 1.0 copy-start.4
  115.5 1.0 copy-start.2

commit v7 on v6

--- a/solution.py
+++ b/solution.py
@@ -54,9 +54,12 @@
     smooth_a = weno_floor + 13.0 / 12.0 * bend_a * bend_a + 0.25 * tilt_a * tilt_a
     smooth_b = weno_floor + 13.0 / 12.0 * bend_b * bend_b + 0.25 * tilt_b * tilt_b
     smooth_c = weno_floor + 13.0 / 12.0 * bend_c * bend_c + 0.25 * tilt_c * tilt_c
-    weight_a = 0.1 / (smooth_a * smooth_a)
-    weight_b = 0.6 / (smooth_b * smooth_b)
-    weight_c = 0.3 / (smooth_c * smooth_c)
+    square_a = smooth_a * smooth_a
+    square_b = smooth_b * smooth_b
+    square_c = smooth_c * smooth_c
+    weight_a = 0.1 * (square_b * square_c)
+    weight_b = 0.6 * (square_a * square_c)
+    weight_c = 0.3 * (square_a * square_b)
     return (weight_a * guess_a + weight_b * guess_b + weight_c * guess_c) / (
         weight_a + weight_b + weight_c
     )
@@ -248,7 +251,7 @@
     speeds = speed.reshape(8, 8, 8, count)
     for offset_step in range(OFFSET_STEPS):
         picked = assemble(voxels, 3, peer_ids, region_ids, halo_ids)
-        voxels = advect_leaves(voxels, speeds, picked)
+        voxels = advect_leaves(voxels, lax.optimization_barrier(speeds), picked)
         sign_field = voxels / jnp.sqrt(voxels * voxels + 1.0)
         for redist_pass in range(REDIST_PASSES):
             picked = assemble(voxels, 1, peer_ids, region_ids, halo_ids)

time: 163 us -> 161 us (0.988)
  other arithmetic: 22.7 us -> 20.9 us
    mul x1 -> x0, other arithmetic: 1.88 us -> none  [advect_leaves(): return voxels - advect_scale * speeds * jnp.sqrt(squared)]
where the time goes in v7:
time: 161 us
  Pallas kernels  104 us (65%)
  local copies, waits for them, and re-layouts  34.9 us (22%)
  other arithmetic  20.9 us (13%)
    pallas_call x6, Pallas kernels, exchange(): pl.pallas_call(exchange_kernel, out_shape=(pltpu.VMEM if layers == 1 else...  104 us
    gather x12, local copies, waits for them, and re-layouts, assemble(): picked = combined.at[:, halo_ids].get(mode='promise_in_bounds')  23 us
    sub x2, other arithmetic, advect_leaves(): return voxels - advect_scale * speeds * jnp.sqrt(squared)  14.6 us
    sub x4, other arithmetic, relax_leaves(): return voxels - relax_scale * sign_field * (jnp.sqrt(squared) - 1.0)  5.08 us
    reshape x46, local copies, waits for them, and re-layouts, face_slabs(): piece.reshape(64 * layers, count)  3.99 us
    unnamed x55, local copies, waits for them, and re-layouts  3.47 us

profile of v7, /device:TPU:1, one launch (start us, length us, event | category | flops | bytes accessed | tf_op | source)
XLA Modules:
  0.0 160.9 jit_solution(4254340092793268401)
XLA Ops:
  0.0 1.1 fusion.145
  2.7 0.7 min.120.idx_ref
  3.4 0.7 min.123.ridx_ref
  4.0 26.5 %shard_map.55 = f32[2080,192]{1,0:T(8,128)} custom-call(f32[1536,192]{1,0:T(8,128)S(1)} %bitcast.171, s32[512]{0:T(512)} %min.120.idx_ref, s32[32]{0:T(128)} %min.123.ridx_ref), custom_call_target="tpu_custom_call" | custom-call | tf_op jit(solution)/shard_map/pallas_call | solution.py:220
  30.6 5.3 %gather_fusion = f32[1536,192]{1,0:T(8,128)S(1)} fusion(f32[192,2080]{0,1:T(8,128)} %bitcast.177, s32[2048]{0:T(1024)S(1)} %pad_clamp_fusion), kind=kCustom, calls=%fused_computation | custom fusion | bytes 2365440 | tf_op jit(solution)/shard_map/gather | solution.py:240
  37.3 1.0 copy-done.3
  38.3 7.3 %multiply_subtract_fusion.5 = f32[8,8,8,256]{3,2,1,0:T(8,128)S(1)} fusion(f32[8,8,8,256]{3,2,1,0:T(8,128)S(1)} %bitcast.184, f32[8,8,13,256]{3,2,1,0:T(8,128)S(1)} %slice_subtract_fusion.1, f32[8,13,8,256]{3,2,1,0:T(8,128)S(1)} %slice_subtract_fusion.4, f32[13,8,8,256]{3,2,1,0:T(8,128)S(1)} %slice_subtract_fusion.5, f32[8,8,8,256]{3,2,1,0:T(8,128)S(1)} %bitcast.193), kind=kLoop, calls=%fused_computation.253 | loop fusion | flops 53739520 | bytes 11010048 | tf_op jit(solution)/shard_map/sub | solution.py:104
  46.4 14.2 %shard_map.56 = f32[2080,64]{1,0:T(8,128)S(1)} custom-call(f32[1536,64]{1,0:T(8,128)S(1)} %bitcast.173, s32[512]{0:T(512)} %min.120.idx_ref, s32[32]{0:T(128)} %min.123.ridx_ref), custom_call_target="tpu_custom_call" | custom-call | tf_op jit(solution)/shard_map/pallas_call | solution.py:220
  60.6 2.6 %gather_fusion.1 = f32[1536,64]{1,0:T(8,128)S(1)} fusion(f32[64,2080]{0,1:T(8,128)S(1)} %bitcast.168, s32[2048]{0:T(1024)S(1)} %pad_clamp_fusion), kind=kCustom, calls=%fused_computation.1 | custom fusion | bytes 792576 | tf_op jit(solution)/shard_map/gather | solution.py:240
  63.7 1.1 multiply_subtract_fusion.4
  65.7 14.5 %shard_map.57 = f32[2080,64]{1,0:T(8,128)S(1)} custom-call(f32[1536,64]{1,0:T(8,128)S(1)} %bitcast.174, s32[512]{0:T(512)} %min.120.idx_ref, s32[32]{0:T(128)} %min.123.ridx_ref), custom_call_target="tpu_custom_call" | custom-call | tf_op jit(solution)/shard_map/pallas_call | solution.py:220
  80.1 2.8 %gather_fusion.2 = f32[1536,64]{1,0:T(8,128)S(1)} fusion(f32[64,2080]{0,1:T(8,128)S(1)} %bitcast.169, s32[2048]{0:T(1024)S(1)} %pad_clamp_fusion), kind=kCustom, calls=%fused_computation.2 | custom fusion | bytes 792576 | tf_op jit(solution)/shard_map/gather | solution.py:240
  83.4 0.6 copy-done.2
  84.0 1.1 multiply_subtract_fusion.3
  86.4 20.6 %shard_map.58 = f32[2080,192]{1,0:T(8,128)} custom-call(f32[1536,192]{1,0:T(8,128)S(1)} %bitcast.172, s32[512]{0:T(512)} %min.120.idx_ref, s32[32]{0:T(128)} %min.123.ridx_ref), custom_call_target="tpu_custom_call" | custom-call | tf_op jit(solution)/shard_map/pallas_call | solution.py:220
  107.0 5.3 %gather_fusion.3 = f32[1536,192]{1,0:T(8,128)S(1)} fusion(f32[192,2080]{0,1:T(8,128)} %bitcast.178, s32[2048]{0:T(1024)S(1)} %pad_clamp_fusion), kind=kCustom, calls=%fused_computation.3 | custom fusion | bytes 2365440 | tf_op jit(solution)/shard_map/gather | solution.py:240
  113.7 1.0 copy-done.4
  114.7 7.3 %multiply_subtract_fusion.2 = f32[8,8,8,256]{3,2,1,0:T(8,128)S(1)} fusion(f32[8,8,8,256]{3,2,1,0:T(8,128)S(1)} %multiply_subtract_fusion.3, f32[8,8,13,256]{3,2,1,0:T(8,128)S(1)} %slice_subtract_fusion, f32[8,13,8,256]{3,2,1,0:T(8,128)S(1)} %slice_subtract_fusion.2, f32[13,8,8,256]{3,2,1,0:T(8,128)S(1)} %slice_subtract_fusion.3, ...), kind=kLoop, calls=%fused_computation.249 | loop fusion | flops 53739520 | bytes 11010048 | tf_op jit(solution)/shard_map/sub | solution.py:104
  122.8 14.6 %shard_map.59 = f32[2080,64]{1,0:T(8,128)S(1)} custom-call(f32[1536,64]{1,0:T(8,128)S(1)} %bitcast.175, s32[512]{0:T(512)} %min.120.idx_ref, s32[32]{0:T(128)} %min.123.ridx_ref), custom_call_target="tpu_custom_call" | custom-call | tf_op jit(solution)/shard_map/pallas_call | solution.py:220
  137.4 2.6 %gather_fusion.4 = f32[1536,64]{1,0:T(8,128)S(1)} fusion(f32[64,2080]{0,1:T(8,128)S(1)} %bitcast.170, s32[2048]{0:T(1024)S(1)} %pad_clamp_fusion), kind=kCustom, calls=%fused_computation.4 | custom fusion | bytes 792576 | tf_op jit(solution)/shard_map/gather | solution.py:240
  140.4 1.1 multiply_subtract_fusion.1
  142.4 13.6 %shard_map.60 = f32[2080,64]{1,0:T(8,128)S(1)} custom-call(f32[1536,64]{1,0:T(8,128)S(1)} %bitcast.176, s32[512]{0:T(512)} %min.120.idx_ref, s32[32]{0:T(128)} %min.123.ridx_ref), custom_call_target="tpu_custom_call" | custom-call | tf_op jit(solution)/shard_map/pallas_call | solution.py:220
  156.0 2.6 %gather_fusion.5 = f32[1536,64]{1,0:T(8,128)S(1)} fusion(f32[64,2080]{0,1:T(8,128)S(1)} %bitcast.167, s32[2048]{0:T(1024)S(1)} %pad_clamp_fusion), kind=kCustom, calls=%fused_computation.5 | custom fusion | bytes 792576 | tf_op jit(solution)/shard_map/gather | solution.py:240
  159.1 1.9 %multiply_subtract_fusion = f32[8,8,8,256]{3,2,1,0:T(8,128)} fusion(f32[8,8,8,256]{3,2,1,0:T(8,128)S(1)} %multiply_subtract_fusion.1, f32[8,8,1,256]{3,2,1,0:T(1,128)S(1)} %copy.100, f32[8,8,1,256]{3,2,1,0:T(1,128)S(1)} %copy.99, f32[8,1,8,256]{3,2,1,0:T(8,128)S(1)} %get-tuple-element.55, f32[8,1,8,256]{3,2,1,0:T(8,128)S(1)} %get-tuple-element.56, ...), kind=kLoop, calls=%fused_computation.246 | loop fusion | flops 7208960 | bytes 1966080 | tf_op jit(solution)/shard_map/sub | solution.py:120
  (155 shorter events, 10.1 us)
Async XLA Ops:
  0.0 1.4 copy-start
  1.9 0.7 copy-start.6
  1.9 1.4 copy-start.7
  4.0 26.5 %copy-start.5 = (s32[6,256]{1,0:T(8,128)S(1)}, s32[6,256]{1,0:T(8,128)}, u32[]{:S(2)}) copy-start(s32[6,256]{1,0:T(8,128)} %param.9) | copy-start | bytes 18436
  37.2 1.0 copy-start.3
  64.7 0.8 copy-start.1
  82.9 1.0 copy-start.2
  113.6 1.0 copy-start.4

commit v8 on v7

--- a/solution.py
+++ b/solution.py
@@ -134,9 +134,11 @@
 
 
 def exchange_kernel(
-    tab_ref, idx_ref, ridx_ref, comb_ref, og_ref, bd_ref, sems
+    tab_ref, idx_ref, ridx_ref, comb_ref, og_ref, bd_ref, sems, *paired
 ):
     peers, slots = og_ref.shape[0], og_ref.shape[1]
+    slab_rows = tab_ref.shape[1]
+    half = slots // 2
     local = tab_ref.shape[0]
     width = bd_ref.shape[1]
     regions = lax.axis_size("group")
@@ -167,10 +169,25 @@
     def pack(e, carry):
         for c in range(slots):
             source = idx_ref[e * slots + c]
-            og_ref[e, pl.ds(c, 1), :] = tab_ref[pl.ds(source, 1), :]
+            og_ref[e, pl.ds(c, 1), pl.ds(0, slab_rows)] = tab_ref[pl.ds(source, 1), :]
         return carry
 
     lax.fori_loop(0, peers, pack, 0)
+
+    if paired:
+        dense_ref, recv_ref = paired
+        lanes = lax.broadcasted_iota(jnp.int32, (half, 2 * slab_rows), 1)
+
+        def pair(e, carry):
+            low = og_ref[e, pl.ds(0, half), :]
+            high = og_ref[e, pl.ds(half, half), :]
+            dense_ref[e] = jnp.where(lanes < slab_rows, low, pltpu.roll(high, slab_rows, 1))
+            return carry
+
+        lax.fori_loop(0, peers, pair, 0)
+        out_ref, in_ref = dense_ref, recv_ref
+    else:
+        out_ref, in_ref = og_ref, None
 
     pl.semaphore_wait(barrier, peers + 1)
 
@@ -195,19 +212,33 @@
 
     for e in targets:
         pltpu.make_async_remote_copy(
-            src_ref=og_ref.at[e],
-            dst_ref=comb_ref.at[mine],
+            src_ref=out_ref.at[e],
+            dst_ref=comb_ref.at[mine] if in_ref is None else in_ref.at[me],
             send_sem=sems.at[0],
             recv_sem=sems.at[1],
             device_id=(region, e),
             device_id_type=mesh_ids,
         ).start()
-    comb_ref[mine, :] = og_ref[me]
-
-    pltpu.make_async_copy(og_ref.at[pl.ds(0, peers - 1)], og_ref.at[pl.ds(0, peers - 1)], sems.at[0]).wait()
+    if in_ref is None:
+        comb_ref[mine, :] = og_ref[me]
+    else:
+        in_ref[me] = out_ref[me]
+
+    pltpu.make_async_copy(out_ref.at[pl.ds(0, peers - 1)], out_ref.at[pl.ds(0, peers - 1)], sems.at[0]).wait()
     pltpu.make_async_copy(bd_ref, bd_ref, sems.at[2]).wait()
-    pltpu.make_async_copy(og_ref.at[pl.ds(0, peers - 1)], og_ref.at[pl.ds(0, peers - 1)], sems.at[1]).wait()
+    pltpu.make_async_copy(out_ref.at[pl.ds(0, peers - 1)], out_ref.at[pl.ds(0, peers - 1)], sems.at[1]).wait()
     pltpu.make_async_copy(bd_ref, bd_ref, sems.at[3]).wait()
+
+    if in_ref is not None:
+
+        def unpair(e, carry):
+            block = in_ref[e]
+            turned = pltpu.roll(block, slab_rows, 1)
+            rows = jnp.concatenate([block[:, :slab_rows], turned[:, :slab_rows]], axis=0)
+            comb_ref[pl.ds(pl.multiple_of(arrived + e * slots, slots), slots), :] = rows
+            return carry
+
+        lax.fori_loop(0, peers, unpair, 0)
     keep.wait()
 
 
@@ -217,6 +248,7 @@
     width = region_ids.shape[0] // 2
     vmem = pl.BlockSpec(memory_space=pltpu.VMEM)
     smem = pl.BlockSpec(memory_space=pltpu.SMEM)
+    paired = slab_rows == 64 and slots % 2 == 0
     return pl.pallas_call(
         exchange_kernel,
         out_shape=(pltpu.VMEM if layers == 1 else jax.ShapeDtypeStruct)(
@@ -225,10 +257,15 @@
         in_specs=[vmem, smem, smem],
         out_specs=vmem,
         scratch_shapes=[
-            pltpu.VMEM((peers, slots, slab_rows), table.dtype),
+            pltpu.VMEM((peers, slots, 2 * slab_rows if paired else slab_rows), table.dtype),
             pltpu.VMEM((2, width, slab_rows), table.dtype),
             pltpu.SemaphoreType.DMA((5,)),
-        ],
+        ]
+        + (
+            [pltpu.VMEM((peers, slots // 2, 2 * slab_rows), table.dtype)] * 2
+            if paired
+            else []
+        ),
         compiler_params=pltpu.CompilerParams(collective_id=layers, has_side_effects=True),
     )(pltpu.with_memory_space_constraint(table, pltpu.VMEM), peer_ids, region_ids)
 

time: 161 us -> 177 us (1.099)
  Pallas kernels: 104 us -> 119 us
    pallas_call x6, Pallas kernels: 104 us -> 119 us  [exchange(): pl.pallas_call(exchange_kernel, out_shape=(pltpu.VMEM if layers == 1 else...]
where the time goes in v8:
time: 177 us; the launch traced here: 176 us
  Pallas kernels  119 us (67%)
  local copies, waits for them, and re-layouts  34.9 us (20%)
  other arithmetic  20.9 us (12%)
    pallas_call x6, Pallas kernels, exchange(): pl.pallas_call(exchange_kernel, out_shape=(pltpu.VMEM if layers == 1 else...  119 us
    gather x12, local copies, waits for them, and re-layouts, assemble(): picked = combined.at[:, halo_ids].get(mode='promise_in_bounds')  23 us
    sub x2, other arithmetic, advect_leaves(): return voxels - advect_scale * speeds * jnp.sqrt(squared)  14.6 us
    sub x4, other arithmetic, relax_leaves(): return voxels - relax_scale * sign_field * (jnp.sqrt(squared) - 1.0)  5.08 us
    reshape x46, local copies, waits for them, and re-layouts, face_slabs(): piece.reshape(64 * layers, count)  3.99 us

profile of v8, /device:TPU:1, one launch (start us, length us, event | category | flops | bytes accessed | tf_op | source)
XLA Modules:
  0.0 176.3 jit_solution(4295207783503291550)
XLA Ops:
  0.0 1.1 fusion.145
  2.7 0.7 min.120.idx_ref
  3.4 0.7 min.123.ridx_ref
  4.0 26.5 %shard_map.55 = f32[2080,192]{1,0:T(8,128)} custom-call(f32[1536,192]{1,0:T(8,128)S(1)} %bitcast.171, s32[512]{0:T(512)} %min.120.idx_ref, s32[32]{0:T(128)} %min.123.ridx_ref), custom_call_target="tpu_custom_call" | custom-call | tf_op jit(solution)/shard_map/pallas_call | solution.py:252
  30.6 5.3 %gather_fusion = f32[1536,192]{1,0:T(8,128)S(1)} fusion(f32[192,2080]{0,1:T(8,128)} %bitcast.177, s32[2048]{0:T(1024)S(1)} %pad_clamp_fusion), kind=kCustom, calls=%fused_computation | custom fusion | bytes 2365440 | tf_op jit(solution)/shard_map/gather | solution.py:277
  37.3 1.0 copy-done.3
  38.3 7.3 %multiply_subtract_fusion.5 = f32[8,8,8,256]{3,2,1,0:T(8,128)S(1)} fusion(f32[8,8,8,256]{3,2,1,0:T(8,128)S(1)} %bitcast.184, f32[8,8,13,256]{3,2,1,0:T(8,128)S(1)} %slice_subtract_fusion.1, f32[8,13,8,256]{3,2,1,0:T(8,128)S(1)} %slice_subtract_fusion.4, f32[13,8,8,256]{3,2,1,0:T(8,128)S(1)} %slice_subtract_fusion.5, f32[8,8,8,256]{3,2,1,0:T(8,128)S(1)} %bitcast.193), kind=kLoop, calls=%fused_computation.253 | loop fusion | flops 53739520 | bytes 11010048 | tf_op jit(solution)/shard_map/sub | solution.py:104
  46.4 18.4 %shard_map.56 = f32[2080,64]{1,0:T(8,128)S(1)} custom-call(f32[1536,64]{1,0:T(8,128)S(1)} %bitcast.173, s32[512]{0:T(512)} %min.120.idx_ref, s32[32]{0:T(128)} %min.123.ridx_ref), custom_call_target="tpu_custom_call" | custom-call | tf_op jit(solution)/shard_map/pallas_call | solution.py:252
  64.8 2.6 %gather_fusion.1 = f32[1536,64]{1,0:T(8,128)S(1)} fusion(f32[64,2080]{0,1:T(8,128)S(1)} %bitcast.168, s32[2048]{0:T(1024)S(1)} %pad_clamp_fusion), kind=kCustom, calls=%fused_computation.1 | custom fusion | bytes 792576 | tf_op jit(solution)/shard_map/gather | solution.py:277
  67.8 1.1 multiply_subtract_fusion.4
  69.8 18.0 %shard_map.57 = f32[2080,64]{1,0:T(8,128)S(1)} custom-call(f32[1536,64]{1,0:T(8,128)S(1)} %bitcast.174, s32[512]{0:T(512)} %min.120.idx_ref, s32[32]{0:T(128)} %min.123.ridx_ref), custom_call_target="tpu_custom_call" | custom-call | tf_op jit(solution)/shard_map/pallas_call | solution.py:252
  87.9 2.8 %gather_fusion.2 = f32[1536,64]{1,0:T(8,128)S(1)} fusion(f32[64,2080]{0,1:T(8,128)S(1)} %bitcast.169, s32[2048]{0:T(1024)S(1)} %pad_clamp_fusion), kind=kCustom, calls=%fused_computation.2 | custom fusion | bytes 792576 | tf_op jit(solution)/shard_map/gather | solution.py:277
  91.1 0.6 copy-done.2
  91.7 1.1 multiply_subtract_fusion.3
  94.1 20.6 %shard_map.58 = f32[2080,192]{1,0:T(8,128)} custom-call(f32[1536,192]{1,0:T(8,128)S(1)} %bitcast.172, s32[512]{0:T(512)} %min.120.idx_ref, s32[32]{0:T(128)} %min.123.ridx_ref), custom_call_target="tpu_custom_call" | custom-call | tf_op jit(solution)/shard_map/pallas_call | solution.py:252
  114.8 5.3 %gather_fusion.3 = f32[1536,192]{1,0:T(8,128)S(1)} fusion(f32[192,2080]{0,1:T(8,128)} %bitcast.178, s32[2048]{0:T(1024)S(1)} %pad_clamp_fusion), kind=kCustom, calls=%fused_computation.3 | custom fusion | bytes 2365440 | tf_op jit(solution)/shard_map/gather | solution.py:277
  121.5 1.0 copy-done.4
  122.4 7.3 %multiply_subtract_fusion.2 = f32[8,8,8,256]{3,2,1,0:T(8,128)S(1)} fusion(f32[8,8,8,256]{3,2,1,0:T(8,128)S(1)} %multiply_subtract_fusion.3, f32[8,8,13,256]{3,2,1,0:T(8,128)S(1)} %slice_subtract_fusion, f32[8,13,8,256]{3,2,1,0:T(8,128)S(1)} %slice_subtract_fusion.2, f32[13,8,8,256]{3,2,1,0:T(8,128)S(1)} %slice_subtract_fusion.3, ...), kind=kLoop, calls=%fused_computation.249 | loop fusion | flops 53739520 | bytes 11010048 | tf_op jit(solution)/shard_map/sub | solution.py:104
  130.6 18.0 %shard_map.59 = f32[2080,64]{1,0:T(8,128)S(1)} custom-call(f32[1536,64]{1,0:T(8,128)S(1)} %bitcast.175, s32[512]{0:T(512)} %min.120.idx_ref, s32[32]{0:T(128)} %min.123.ridx_ref), custom_call_target="tpu_custom_call" | custom-call | tf_op jit(solution)/shard_map/pallas_call | solution.py:252
  148.6 2.6 %gather_fusion.4 = f32[1536,64]{1,0:T(8,128)S(1)} fusion(f32[64,2080]{0,1:T(8,128)S(1)} %bitcast.170, s32[2048]{0:T(1024)S(1)} %pad_clamp_fusion), kind=kCustom, calls=%fused_computation.4 | custom fusion | bytes 792576 | tf_op jit(solution)/shard_map/gather | solution.py:277
  151.7 1.1 multiply_subtract_fusion.1
  153.6 17.8 %shard_map.60 = f32[2080,64]{1,0:T(8,128)S(1)} custom-call(f32[1536,64]{1,0:T(8,128)S(1)} %bitcast.176, s32[512]{0:T(512)} %min.120.idx_ref, s32[32]{0:T(128)} %min.123.ridx_ref), custom_call_target="tpu_custom_call" | custom-call | tf_op jit(solution)/shard_map/pallas_call | solution.py:252
  171.3 2.6 %gather_fusion.5 = f32[1536,64]{1,0:T(8,128)S(1)} fusion(f32[64,2080]{0,1:T(8,128)S(1)} %bitcast.167, s32[2048]{0:T(1024)S(1)} %pad_clamp_fusion), kind=kCustom, calls=%fused_computation.5 | custom fusion | bytes 792576 | tf_op jit(solution)/shard_map/gather | solution.py:277
  174.4 1.9 %multiply_subtract_fusion = f32[8,8,8,256]{3,2,1,0:T(8,128)} fusion(f32[8,8,8,256]{3,2,1,0:T(8,128)S(1)} %multiply_subtract_fusion.1, f32[8,8,1,256]{3,2,1,0:T(1,128)S(1)} %copy.100, f32[8,8,1,256]{3,2,1,0:T(1,128)S(1)} %copy.99, f32[8,1,8,256]{3,2,1,0:T(8,128)S(1)} %get-tuple-element.55, f32[8,1,8,256]{3,2,1,0:T(8,128)S(1)} %get-tuple-element.56, ...), kind=kLoop, calls=%fused_computation.246 | loop fusion | flops 7208960 | bytes 1966080 | tf_op jit(solution)/shard_map/sub | solution.py:120
  (155 shorter events, 10.1 us)
Async XLA Ops:
  0.0 1.4 copy-start
  1.9 0.7 copy-start.6
  1.9 1.4 copy-start.7
  4.0 26.5 %copy-start.5 = (s32[6,256]{1,0:T(8,128)S(1)}, s32[6,256]{1,0:T(8,128)}, u32[]{:S(2)}) copy-start(s32[6,256]{1,0:T(8,128)} %param.9) | copy-start | bytes 18436
  37.2 1.0 copy-start.3
  68.9 0.8 copy-start.1
  90.7 1.0 copy-start.2
  121.4 1.0 copy-start.4

commit v9 on v7

--- a/solution.py
+++ b/solution.py
@@ -233,9 +233,130 @@
     )(pltpu.with_memory_space_constraint(table, pltpu.VMEM), peer_ids, region_ids)
 
 
-def assemble(voxels, layers, peer_ids, region_ids, halo_ids):
+def paired_kernel(tab_ref, idx_ref, ridx_ref, comb_ref, og_ref, bd_ref, sems):
+    peers, half, lane_count = og_ref.shape
+    slots = 2 * half
+    slab_rows = lane_count // 2
+    local = tab_ref.shape[0]
+    width = bd_ref.shape[1]
+    regions = lax.axis_size("group")
+    me = lax.axis_index("dev")
+    region = lax.axis_index("group")
+    up = lax.rem(region + 1, regions)
+    down = lax.rem(region + regions - 1, regions)
+    mesh_ids = pl.DeviceIdType.MESH
+    bordering = local + peers * half
+
+    keep = pltpu.make_async_copy(tab_ref, comb_ref.at[pl.ds(0, local)], sems.at[4])
+    keep.start()
+
+    barrier = pltpu.get_barrier_semaphore()
+    targets = far_first(me, peers)
+    for e in targets:
+        pl.semaphore_signal(barrier, inc=1, device_id=(region, e), device_id_type=mesh_ids)
+    pl.semaphore_signal(barrier, inc=1, device_id=(up, me), device_id_type=mesh_ids)
+    pl.semaphore_signal(barrier, inc=1, device_id=(down, me), device_id_type=mesh_ids)
+
+    for h in range(2):
+        for p in range(width):
+            source = ridx_ref[h * width + p]
+            bd_ref[h, pl.ds(p, 1), :] = tab_ref[pl.ds(source, 1), :]
+
+    lanes = lax.broadcasted_iota(jnp.int32, (1, lane_count), 1)
+
+    def pack(e, carry):
+        for r in range(half):
+            first = tab_ref[pl.ds(idx_ref[e * slots + r], 1), :]
+            second = tab_ref[pl.ds(idx_ref[e * slots + r + half], 1), :]
+            og_ref[e, pl.ds(r, 1), :] = jnp.where(lanes < slab_rows, first, second)
+        return carry
+
+    lax.fori_loop(0, peers, pack, 0)
+
+    pl.semaphore_wait(barrier, peers + 1)
+
+    pltpu.make_async_remote_copy(
+        src_ref=bd_ref.at[1],
+        dst_ref=comb_ref.at[pl.ds(bordering, width)],
+        send_sem=sems.at[2],
+        recv_sem=sems.at[3],
+        device_id=(up, me),
+        device_id_type=mesh_ids,
+    ).start()
+    pltpu.make_async_remote_copy(
+        src_ref=bd_ref.at[0],
+        dst_ref=comb_ref.at[pl.ds(bordering + width, width)],
+        send_sem=sems.at[2],
+        recv_sem=sems.at[3],
+        device_id=(down, me),
+        device_id_type=mesh_ids,
+    ).start()
+
+    mine = pl.ds(local + me * half, half)
+    for e in targets:
+        pltpu.make_async_remote_copy(
+            src_ref=og_ref.at[e],
+            dst_ref=comb_ref.at[mine],
+            send_sem=sems.at[0],
+            recv_sem=sems.at[1],
+            device_id=(region, e),
+            device_id_type=mesh_ids,
+        ).start()
+    pltpu.make_async_copy(og_ref.at[me], comb_ref.at[mine], sems.at[1]).start()
+
+    pltpu.make_async_copy(og_ref.at[pl.ds(0, peers - 1)], og_ref.at[pl.ds(0, peers - 1)], sems.at[0]).wait()
+    pltpu.make_async_copy(bd_ref, bd_ref, sems.at[2]).wait()
+    pltpu.make_async_copy(og_ref, og_ref, sems.at[1]).wait()
+    pltpu.make_async_copy(bd_ref, bd_ref, sems.at[3]).wait()
+    keep.wait()
+
+
+def paired_exchange(table, peer_ids, region_ids, peers):
+    local, slab_rows = table.shape
+    slots = peer_ids.shape[0] // peers
+    width = region_ids.shape[0] // 2
+    doubled = jnp.concatenate([table, table], axis=1)
+    vmem = pl.BlockSpec(memory_space=pltpu.VMEM)
+    smem = pl.BlockSpec(memory_space=pltpu.SMEM)
+    return pl.pallas_call(
+        paired_kernel,
+        out_shape=pltpu.VMEM((local + peers * slots // 2 + 2 * width, 2 * slab_rows), table.dtype),
+        in_specs=[vmem, smem, smem],
+        out_specs=vmem,
+        scratch_shapes=[
+            pltpu.VMEM((peers, slots // 2, 2 * slab_rows), table.dtype),
+            pltpu.VMEM((2, width, 2 * slab_rows), table.dtype),
+            pltpu.SemaphoreType.DMA((5,)),
+        ],
+        compiler_params=pltpu.CompilerParams(collective_id=2, has_side_effects=True),
+    )(pltpu.with_memory_space_constraint(doubled, pltpu.VMEM), peer_ids, region_ids)
+
+
+def paired_sources(halo_ids, local, peers, slots, width):
+    half = slots // 2
+    entry = halo_ids - local
+    slot = entry % slots
+    from_peer = (entry >= 0) & (entry < peers * slots)
+    from_region = entry >= peers * slots
+    row = jnp.where(
+        from_peer,
+        local + (entry // slots) * half + slot % half,
+        jnp.where(from_region, halo_ids - peers * half, halo_ids),
+    )
+    upper = from_peer & (slot >= half)
+    return row, upper
+
+
+def assemble(voxels, layers, peer_ids, region_ids, halo_ids, paired_ids):
     slab_table = face_slabs(voxels, layers)
     peers = lax.axis_size("dev")
+    if layers == 1 and paired_ids is not None:
+        rows, upper = paired_ids
+        table = paired_exchange(slab_table.T, peer_ids, region_ids, peers)
+        lines = table.at[rows].get(mode="promise_in_bounds")
+        width = slab_table.shape[0]
+        chosen = jnp.where(upper[..., None], lines[..., width:], lines[..., :width])
+        return jnp.moveaxis(chosen, 2, 0)
     combined = exchange(slab_table.T, peer_ids, region_ids, peers, layers).T
     picked = combined.at[:, halo_ids].get(mode="promise_in_bounds")
     return picked
@@ -247,14 +368,19 @@
     peer_ids = jnp.clip(peer_slabs.reshape(-1), 0, local - 1)
     region_ids = jnp.clip(region_slabs.reshape(-1), 0, local - 1)
     halo_ids = jnp.clip(halo_source, 0, local + peer_ids.shape[0] + region_ids.shape[0] - 1)
+    peers = lax.axis_size("dev")
+    slots = peer_ids.shape[0] // peers
+    paired_ids = None
+    if slots % 2 == 0:
+        paired_ids = paired_sources(halo_ids, local, peers, slots, region_ids.shape[0] // 2)
     voxels = level_set.reshape(8, 8, 8, count)
     speeds = speed.reshape(8, 8, 8, count)
     for offset_step in range(OFFSET_STEPS):
-        picked = assemble(voxels, 3, peer_ids, region_ids, halo_ids)
+        picked = assemble(voxels, 3, peer_ids, region_ids, halo_ids, paired_ids)
         voxels = advect_leaves(voxels, lax.optimization_barrier(speeds), picked)
         sign_field = voxels / jnp.sqrt(voxels * voxels + 1.0)
         for redist_pass in range(REDIST_PASSES):
-            picked = assemble(voxels, 1, peer_ids, region_ids, halo_ids)
+            picked = assemble(voxels, 1, peer_ids, region_ids, halo_ids, paired_ids)
             voxels = relax_leaves(voxels, sign_field, picked)
     return voxels.reshape(512, count)
 

time: 161 us -> 156 us (0.969)
  Pallas kernels: 104 us -> 94.8 us
  local copies, waits for them, and re-layouts: 34.9 us -> 37 us
    pallas_call x6 -> x2, Pallas kernels: 104 us -> 47.2 us  [exchange(): pl.pallas_call(exchange_kernel, out_shape=(pltpu.VMEM if layers == 1 else...]
    pallas_call x0 -> x4, Pallas kernels: none -> 47.6 us  [paired_exchange(): pl.pallas_call(paired_kernel, out_shape=pltpu.VMEM((local + peers * slots...]
    gather x12 -> x4, local copies, waits for them, and re-layouts: 23 us -> 11.4 us  [assemble(): picked = combined.at[:, halo_ids].get(mode='promise_in_bounds')]
    gather x0 -> x4, local copies, waits for them, and re-layouts: none -> 10.8 us  [assemble(): lines = table.at[rows].get(mode='promise_in_bounds')]
    unnamed x55 -> x76, local copies, waits for them, and re-layouts: 3.47 us -> 5.27 us
where the time goes in v9:
time: 156 us; the launch traced here: 155 us
  Pallas kernels  94.8 us (61%)
  local copies, waits for them, and re-layouts  37 us (24%)
  other arithmetic  22.2 us (14%)
    pallas_call x4, Pallas kernels, paired_exchange(): pl.pallas_call(paired_kernel, out_shape=pltpu.VMEM((local + peers * slots...  47.6 us
    pallas_call x2, Pallas kernels, exchange(): pl.pallas_call(exchange_kernel, out_shape=(pltpu.VMEM if layers == 1 else...  47.2 us
    sub x2, other arithmetic, advect_leaves(): return voxels - advect_scale * speeds * jnp.sqrt(squared)  14.6 us
    gather x4, local copies, waits for them, and re-layouts, assemble(): picked = combined.at[:, halo_ids].get(mode='promise_in_bounds')  11.4 us
    gather x4, local copies, waits for them, and re-layouts, assemble(): lines = table.at[rows].get(mode='promise_in_bounds')  10.8 us
    unnamed x76, local copies, waits for them, and re-layouts  5.27 us
    sub x4, other arithmetic, relax_leaves(): return voxels - relax_scale * sign_field * (jnp.sqrt(squared) - 1.0)  5.09 us
    reshape x46, local copies, waits for them, and re-layouts, face_slabs(): piece.reshape(64 * layers, count)  3.99 us

profile of v9, /device:TPU:1, one launch (start us, length us, event | category | flops | bytes accessed | tf_op | source)
XLA Modules:
  0.0 155.3 jit_solution(16431902598188975190)
XLA Ops:
  0.0 1.1 fusion.156
  2.7 0.7 min.120.idx_ref
  3.4 0.6 min.123.ridx_ref
  4.0 26.5 %shard_map.55 = f32[2080,192]{1,0:T(8,128)} custom-call(f32[1536,192]{1,0:T(8,128)S(1)} %bitcast.169, s32[512]{0:T(512)} %min.120.idx_ref, s32[32]{0:T(128)} %min.123.ridx_ref), custom_call_target="tpu_custom_call" | custom-call | tf_op jit(solution)/shard_map/pallas_call | solution.py:220
  30.6 5.3 %gather_fusion = f32[1536,192]{1,0:T(8,128)S(1)} fusion(f32[192,2080]{0,1:T(8,128)} %bitcast.171, s32[2048]{0:T(1024)S(1)} %get-tuple-element.88), kind=kCustom, calls=%fused_computation | custom fusion | bytes 2365440 | tf_op jit(solution)/shard_map/gather | solution.py:361
  35.9 0.4 copy.49
  37.3 1.0 copy-done.1
  38.3 7.3 %multiply_subtract_fusion.5 = f32[8,8,8,256]{3,2,1,0:T(8,128)S(1)} fusion(f32[8,8,8,256]{3,2,1,0:T(8,128)S(1)} %bitcast.178, f32[8,8,13,256]{3,2,1,0:T(8,128)S(1)} %slice_subtract_fusion.1, f32[8,13,8,256]{3,2,1,0:T(8,128)S(1)} %slice_subtract_fusion.4, f32[13,8,8,256]{3,2,1,0:T(8,128)S(1)} %slice_subtract_fusion.5, f32[8,8,8,256]{3,2,1,0:T(8,128)S(1)} %bitcast.187), kind=kLoop, calls=%fused_computation.257 | loop fusion | flops 53739520 | bytes 11010048 | tf_op jit(solution)/shard_map/sub | solution.py:104
  46.7 12.0 %shard_map.56 = f32[1824,128]{1,0:T(8,128)S(1)} custom-call(f32[1536,128]{1,0:T(8,128)S(1)} %pad_maximum_fusion.6.tab_ref, s32[512]{0:T(512)} %min.120.idx_ref, s32[32]{0:T(128)} %min.123.ridx_ref), custom_call_target="tpu_custom_call" | custom-call | tf_op jit(solution)/shard_map/pallas_call | solution.py:321
  58.7 2.6 %gather_fusion.1 = f32[1536,128]{1,0:T(8,128)S(1)} fusion(f32[1824,128]{1,0:T(8,128)S(1)} %shard_map.56, s32[2048]{0:T(1024)S(1)} %get-tuple-element.87), kind=kCustom, calls=%fused_computation.1 | custom fusion | bytes 1579008 | tf_op jit(solution)/shard_map/gather | solution.py:356
  62.3 1.1 multiply_subtract_fusion.4
  64.5 12.0 %shard_map.57 = f32[1824,128]{1,0:T(8,128)S(1)} custom-call(f32[1536,128]{1,0:T(8,128)S(1)} %pad_maximum_fusion.7.tab_ref, s32[512]{0:T(512)} %min.120.idx_ref, s32[32]{0:T(128)} %min.123.ridx_ref), custom_call_target="tpu_custom_call" | custom-call | tf_op jit(solution)/shard_map/pallas_call | solution.py:321
  76.6 2.8 %gather_fusion.2 = f32[1536,128]{1,0:T(8,128)S(1)} fusion(f32[1824,128]{1,0:T(8,128)S(1)} %shard_map.57, s32[2048]{0:T(1024)S(1)} %get-tuple-element.87), kind=kCustom, calls=%fused_computation.2 | custom fusion | bytes 1579008 | tf_op jit(solution)/shard_map/gather | solution.py:356
  80.6 1.1 multiply_subtract_fusion.3
  83.0 20.7 %shard_map.58 = f32[2080,192]{1,0:T(8,128)} custom-call(f32[1536,192]{1,0:T(8,128)S(1)} %bitcast.170, s32[512]{0:T(512)} %min.120.idx_ref, s32[32]{0:T(128)} %min.123.ridx_ref), custom_call_target="tpu_custom_call" | custom-call | tf_op jit(solution)/shard_map/pallas_call | solution.py:220
  103.8 5.3 %gather_fusion.3 = f32[1536,192]{1,0:T(8,128)S(1)} fusion(f32[192,2080]{0,1:T(8,128)} %bitcast.172, s32[2048]{0:T(1024)S(1)} %copy-done.6), kind=kCustom, calls=%fused_computation.3 | custom fusion | bytes 2365440 | tf_op jit(solution)/shard_map/gather | solution.py:361
  110.5 1.0 copy-done.2
  111.4 7.3 %multiply_subtract_fusion.2 = f32[8,8,8,256]{3,2,1,0:T(8,128)S(1)} fusion(f32[8,8,8,256]{3,2,1,0:T(8,128)S(1)} %multiply_subtract_fusion.3, f32[8,8,13,256]{3,2,1,0:T(8,128)S(1)} %slice_subtract_fusion, f32[8,13,8,256]{3,2,1,0:T(8,128)S(1)} %slice_subtract_fusion.2, f32[13,8,8,256]{3,2,1,0:T(8,128)S(1)} %slice_subtract_fusion.3, ...), kind=kLoop, calls=%fused_computation.253 | loop fusion | flops 53739520 | bytes 11010048 | tf_op jit(solution)/shard_map/sub | solution.py:104
  119.8 11.5 %shard_map.59 = f32[1824,128]{1,0:T(8,128)S(1)} custom-call(f32[1536,128]{1,0:T(8,128)S(1)} %pad_maximum_fusion.8.tab_ref, s32[512]{0:T(512)} %min.120.idx_ref, s32[32]{0:T(128)} %min.123.ridx_ref), custom_call_target="tpu_custom_call" | custom-call | tf_op jit(solution)/shard_map/pallas_call | solution.py:321
  131.4 2.8 %gather_fusion.4 = f32[1536,128]{1,0:T(8,128)S(1)} fusion(f32[1824,128]{1,0:T(8,128)S(1)} %shard_map.59, s32[2048]{0:T(1024)S(1)} %copy-done.4), kind=kCustom, calls=%fused_computation.4 | custom fusion | bytes 1579008 | tf_op jit(solution)/shard_map/gather | solution.py:356
  135.4 1.1 multiply_subtract_fusion.1
  137.6 12.0 %shard_map.60 = f32[1824,128]{1,0:T(8,128)S(1)} custom-call(f32[1536,128]{1,0:T(8,128)S(1)} %pad_maximum_fusion.9.tab_ref, s32[512]{0:T(512)} %min.120.idx_ref, s32[32]{0:T(128)} %min.123.ridx_ref), custom_call_target="tpu_custom_call" | custom-call | tf_op jit(solution)/shard_map/pallas_call | solution.py:321
  149.7 2.6 %gather_fusion.5 = f32[1536,128]{1,0:T(8,128)S(1)} fusion(f32[1824,128]{1,0:T(8,128)S(1)} %shard_map.60, s32[2048]{0:T(1024)S(1)} %copy-done.4), kind=kCustom, calls=%fused_computation.5 | custom fusion | bytes 1579008 | tf_op jit(solution)/shard_map/gather | solution.py:356
  153.5 1.9 %multiply_subtract_fusion = f32[8,8,8,256]{3,2,1,0:T(8,128)} fusion(f32[8,8,8,256]{3,2,1,0:T(8,128)S(1)} %multiply_subtract_fusion.1, f32[8,8,1,256]{3,2,1,0:T(1,128)S(1)} %copy.104, f32[8,8,1,256]{3,2,1,0:T(1,128)S(1)} %copy.103, f32[8,1,8,256]{3,2,1,0:T(8,128)S(1)} %get-tuple-element.64, f32[8,1,8,256]{3,2,1,0:T(8,128)S(1)} %get-tuple-element.65, ...), kind=kLoop, calls=%fused_computation.250 | loop fusion | flops 7208960 | bytes 1966080 | tf_op jit(solution)/shard_map/sub | solution.py:120
  (186 shorter events, 13.5 us)
Async XLA Ops:
  0.0 1.4 copy-start
  1.9 0.7 copy-start.12
  1.9 1.5 copy-start.13
  4.0 26.5 %copy-start.11 = (s32[6,256]{1,0:T(8,128)S(1)}, s32[6,256]{1,0:T(8,128)}, u32[]{:S(2)}) copy-start(s32[6,256]{1,0:T(8,128)} %param.9) | copy-start | bytes 18436
  30.6 5.3 %copy-start.5 = (s32[2048]{0:T(1024)}, s32[2048]{0:T(1024)S(1)}, u32[]{:S(2)}) copy-start(s32[2048]{0:T(1024)S(1)} %get-tuple-element.88) | copy-start | bytes 24580
  30.6 46.0 %copy-start.3 = (s32[2048]{0:T(1024)}, s32[2048]{0:T(1024)S(1)}, u32[]{:S(2)}) copy-start(s32[2048]{0:T(1024)S(1)} %get-tuple-element.87) | copy-start | bytes 24580
  37.2 1.0 copy-start.1
  62.1 1.3 copy-start.7
  79.6 0.7 copy-start.8
  83.0 20.7 %copy-start.6 = (s32[2048]{0:T(1024)S(1)}, s32[2048]{0:T(1024)}, u32[]{:S(2)}) copy-start(s32[2048]{0:T(1024)} %copy-done.5) | copy-start | bytes 24580
  110.4 1.0 copy-start.2
  119.6 11.8 %copy-start.4 = (s32[2048]{0:T(1024)S(1)}, s32[2048]{0:T(1024)}, u32[]{:S(2)}) copy-start(s32[2048]{0:T(1024)} %copy-done.3) | copy-start | bytes 24580
  134.5 0.7 copy-start.9
  152.5 0.7 copy-start.10

commit v10 on v9

--- a/solution.py
+++ b/solution.py
@@ -174,6 +174,20 @@
 
     pl.semaphore_wait(barrier, peers + 1)
 
+
+    mine = pl.ds(pl.multiple_of(arrived + me * slots, slots), slots)
+
+    for e in targets:
+        pltpu.make_async_remote_copy(
+            src_ref=og_ref.at[e],
+            dst_ref=comb_ref.at[mine],
+            send_sem=sems.at[0],
+            recv_sem=sems.at[1],
+            device_id=(region, e),
+            device_id_type=mesh_ids,
+        ).start()
+    comb_ref[mine, :] = og_ref[me]
+
     pltpu.make_async_remote_copy(
         src_ref=bd_ref.at[1],
         dst_ref=comb_ref.at[pl.ds(bordering, width)],
@@ -190,19 +204,6 @@
         device_id=(down, me),
         device_id_type=mesh_ids,
     ).start()
-
-    mine = pl.ds(pl.multiple_of(arrived + me * slots, slots), slots)
-
-    for e in targets:
-        pltpu.make_async_remote_copy(
-            src_ref=og_ref.at[e],
-            dst_ref=comb_ref.at[mine],
-            send_sem=sems.at[0],
-            recv_sem=sems.at[1],
-            device_id=(region, e),
-            device_id_type=mesh_ids,
-        ).start()
-    comb_ref[mine, :] = og_ref[me]
 
     pltpu.make_async_copy(og_ref.at[pl.ds(0, peers - 1)], og_ref.at[pl.ds(0, peers - 1)], sems.at[0]).wait()
     pltpu.make_async_copy(bd_ref, bd_ref, sems.at[2]).wait()
@@ -275,6 +276,19 @@
 
     pl.semaphore_wait(barrier, peers + 1)
 
+
+    mine = pl.ds(local + me * half, half)
+    for e in targets:
+        pltpu.make_async_remote_copy(
+            src_ref=og_ref.at[e],
+            dst_ref=comb_ref.at[mine],
+            send_sem=sems.at[0],
+            recv_sem=sems.at[1],
+            device_id=(region, e),
+            device_id_type=mesh_ids,
+        ).start()
+    pltpu.make_async_copy(og_ref.at[me], comb_ref.at[mine], sems.at[1]).start()
+
     pltpu.make_async_remote_copy(
         src_ref=bd_ref.at[1],
         dst_ref=comb_ref.at[pl.ds(bordering, width)],
@@ -291,18 +305,6 @@
         device_id=(down, me),
         device_id_type=mesh_ids,
     ).start()
-
-    mine = pl.ds(local + me * half, half)
-    for e in targets:
-        pltpu.make_async_remote_copy(
-            src_ref=og_ref.at[e],
-            dst_ref=comb_ref.at[mine],
-            send_sem=sems.at[0],
-            recv_sem=sems.at[1],
-            device_id=(region, e),
-            device_id_type=mesh_ids,
-        ).start()
-    pltpu.make_async_copy(og_ref.at[me], comb_ref.at[mine], sems.at[1]).start()
 
     pltpu.make_async_copy(og_ref.at[pl.ds(0, peers - 1)], og_ref.at[pl.ds(0, peers - 1)], sems.at[0]).wait()
     pltpu.make_async_copy(bd_ref, bd_ref, sems.at[2]).wait()

time: 156 us -> 156 us (level)
  no operation moved by 1% of the time
where the time goes in v10:
time: 156 us; the launch traced here: 155 us
  Pallas kernels  94.8 us (61%)
  local copies, waits for them, and re-layouts  37 us (24%)
  other arithmetic  22.2 us (14%)
    pallas_call x4, Pallas kernels, paired_exchange(): pl.pallas_call(paired_kernel, out_shape=pltpu.VMEM((local + peers * slots...  47.6 us
    pallas_call x2, Pallas kernels, exchange(): pl.pallas_call(exchange_kernel, out_shape=(pltpu.VMEM if layers == 1 else...  47.2 us
    sub x2, other arithmetic, advect_leaves(): return voxels - advect_scale * speeds * jnp.sqrt(squared)  14.6 us
    gather x4, local copies, waits for them, and re-layouts, assemble(): picked = combined.at[:, halo_ids].get(mode='promise_in_bounds')  11.4 us
    gather x4, local copies, waits for them, and re-layouts, assemble(): lines = table.at[rows].get(mode='promise_in_bounds')  10.8 us
    unnamed x76, local copies, waits for them, and re-layouts  5.27 us
    sub x4, other arithmetic, relax_leaves(): return voxels - relax_scale * sign_field * (jnp.sqrt(squared) - 1.0)  5.09 us
    reshape x46, local copies, waits for them, and re-layouts, face_slabs(): piece.reshape(64 * layers, count)  3.99 us

profile of v10, /device:TPU:1, one launch (start us, length us, event | category | flops | bytes accessed | tf_op | source)
XLA Modules:
  0.0 155.3 jit_solution(1479072531761371781)
XLA Ops:
  0.0 1.1 fusion.156
  2.7 0.7 min.120.idx_ref
  3.4 0.6 min.123.ridx_ref
  4.0 26.5 %shard_map.55 = f32[2080,192]{1,0:T(8,128)} custom-call(f32[1536,192]{1,0:T(8,128)S(1)} %bitcast.169, s32[512]{0:T(512)} %min.120.idx_ref, s32[32]{0:T(128)} %min.123.ridx_ref), custom_call_target="tpu_custom_call" | custom-call | tf_op jit(solution)/shard_map/pallas_call | solution.py:221
  30.6 5.3 %gather_fusion = f32[1536,192]{1,0:T(8,128)S(1)} fusion(f32[192,2080]{0,1:T(8,128)} %bitcast.171, s32[2048]{0:T(1024)S(1)} %get-tuple-element.88), kind=kCustom, calls=%fused_computation | custom fusion | bytes 2365440 | tf_op jit(solution)/shard_map/gather | solution.py:363
  35.9 0.4 copy.49
  37.3 1.0 copy-done.1
  38.3 7.3 %multiply_subtract_fusion.5 = f32[8,8,8,256]{3,2,1,0:T(8,128)S(1)} fusion(f32[8,8,8,256]{3,2,1,0:T(8,128)S(1)} %bitcast.178, f32[8,8,13,256]{3,2,1,0:T(8,128)S(1)} %slice_subtract_fusion.1, f32[8,13,8,256]{3,2,1,0:T(8,128)S(1)} %slice_subtract_fusion.4, f32[13,8,8,256]{3,2,1,0:T(8,128)S(1)} %slice_subtract_fusion.5, f32[8,8,8,256]{3,2,1,0:T(8,128)S(1)} %bitcast.187), kind=kLoop, calls=%fused_computation.257 | loop fusion | flops 53739520 | bytes 11010048 | tf_op jit(solution)/shard_map/sub | solution.py:104
  46.7 12.0 %shard_map.56 = f32[1824,128]{1,0:T(8,128)S(1)} custom-call(f32[1536,128]{1,0:T(8,128)S(1)} %pad_maximum_fusion.6.tab_ref, s32[512]{0:T(512)} %min.120.idx_ref, s32[32]{0:T(128)} %min.123.ridx_ref), custom_call_target="tpu_custom_call" | custom-call | tf_op jit(solution)/shard_map/pallas_call | solution.py:323
  58.7 2.6 %gather_fusion.1 = f32[1536,128]{1,0:T(8,128)S(1)} fusion(f32[1824,128]{1,0:T(8,128)S(1)} %shard_map.56, s32[2048]{0:T(1024)S(1)} %get-tuple-element.87), kind=kCustom, calls=%fused_computation.1 | custom fusion | bytes 1579008 | tf_op jit(solution)/shard_map/gather | solution.py:358
  62.3 1.1 multiply_subtract_fusion.4
  64.5 12.0 %shard_map.57 = f32[1824,128]{1,0:T(8,128)S(1)} custom-call(f32[1536,128]{1,0:T(8,128)S(1)} %pad_maximum_fusion.7.tab_ref, s32[512]{0:T(512)} %min.120.idx_ref, s32[32]{0:T(128)} %min.123.ridx_ref), custom_call_target="tpu_custom_call" | custom-call | tf_op jit(solution)/shard_map/pallas_call | solution.py:323
  76.6 2.8 %gather_fusion.2 = f32[1536,128]{1,0:T(8,128)S(1)} fusion(f32[1824,128]{1,0:T(8,128)S(1)} %shard_map.57, s32[2048]{0:T(1024)S(1)} %get-tuple-element.87), kind=kCustom, calls=%fused_computation.2 | custom fusion | bytes 1579008 | tf_op jit(solution)/shard_map/gather | solution.py:358
  80.6 1.1 multiply_subtract_fusion.3
  83.0 20.7 %shard_map.58 = f32[2080,192]{1,0:T(8,128)} custom-call(f32[1536,192]{1,0:T(8,128)S(1)} %bitcast.170, s32[512]{0:T(512)} %min.120.idx_ref, s32[32]{0:T(128)} %min.123.ridx_ref), custom_call_target="tpu_custom_call" | custom-call | tf_op jit(solution)/shard_map/pallas_call | solution.py:221
  103.8 5.3 %gather_fusion.3 = f32[1536,192]{1,0:T(8,128)S(1)} fusion(f32[192,2080]{0,1:T(8,128)} %bitcast.172, s32[2048]{0:T(1024)S(1)} %copy-done.6), kind=kCustom, calls=%fused_computation.3 | custom fusion | bytes 2365440 | tf_op jit(solution)/shard_map/gather | solution.py:363
  110.5 1.0 copy-done.2
  111.4 7.3 %multiply_subtract_fusion.2 = f32[8,8,8,256]{3,2,1,0:T(8,128)S(1)} fusion(f32[8,8,8,256]{3,2,1,0:T(8,128)S(1)} %multiply_subtract_fusion.3, f32[8,8,13,256]{3,2,1,0:T(8,128)S(1)} %slice_subtract_fusion, f32[8,13,8,256]{3,2,1,0:T(8,128)S(1)} %slice_subtract_fusion.2, f32[13,8,8,256]{3,2,1,0:T(8,128)S(1)} %slice_subtract_fusion.3, ...), kind=kLoop, calls=%fused_computation.253 | loop fusion | flops 53739520 | bytes 11010048 | tf_op jit(solution)/shard_map/sub | solution.py:104
  119.8 11.5 %shard_map.59 = f32[1824,128]{1,0:T(8,128)S(1)} custom-call(f32[1536,128]{1,0:T(8,128)S(1)} %pad_maximum_fusion.8.tab_ref, s32[512]{0:T(512)} %min.120.idx_ref, s32[32]{0:T(128)} %min.123.ridx_ref), custom_call_target="tpu_custom_call" | custom-call | tf_op jit(solution)/shard_map/pallas_call | solution.py:323
  131.4 2.8 %gather_fusion.4 = f32[1536,128]{1,0:T(8,128)S(1)} fusion(f32[1824,128]{1,0:T(8,128)S(1)} %shard_map.59, s32[2048]{0:T(1024)S(1)} %copy-done.4), kind=kCustom, calls=%fused_computation.4 | custom fusion | bytes 1579008 | tf_op jit(solution)/shard_map/gather | solution.py:358
  135.4 1.1 multiply_subtract_fusion.1
  137.6 12.0 %shard_map.60 = f32[1824,128]{1,0:T(8,128)S(1)} custom-call(f32[1536,128]{1,0:T(8,128)S(1)} %pad_maximum_fusion.9.tab_ref, s32[512]{0:T(512)} %min.120.idx_ref, s32[32]{0:T(128)} %min.123.ridx_ref), custom_call_target="tpu_custom_call" | custom-call | tf_op jit(solution)/shard_map/pallas_call | solution.py:323
  149.7 2.6 %gather_fusion.5 = f32[1536,128]{1,0:T(8,128)S(1)} fusion(f32[1824,128]{1,0:T(8,128)S(1)} %shard_map.60, s32[2048]{0:T(1024)S(1)} %copy-done.4), kind=kCustom, calls=%fused_computation.5 | custom fusion | bytes 1579008 | tf_op jit(solution)/shard_map/gather | solution.py:358
  153.4 1.9 %multiply_subtract_fusion = f32[8,8,8,256]{3,2,1,0:T(8,128)} fusion(f32[8,8,8,256]{3,2,1,0:T(8,128)S(1)} %multiply_subtract_fusion.1, f32[8,8,1,256]{3,2,1,0:T(1,128)S(1)} %copy.104, f32[8,8,1,256]{3,2,1,0:T(1,128)S(1)} %copy.103, f32[8,1,8,256]{3,2,1,0:T(8,128)S(1)} %get-tuple-element.64, f32[8,1,8,256]{3,2,1,0:T(8,128)S(1)} %get-tuple-element.65, ...), kind=kLoop, calls=%fused_computation.250 | loop fusion | flops 7208960 | bytes 1966080 | tf_op jit(solution)/shard_map/sub | solution.py:120
  (186 shorter events, 13.5 us)
Async XLA Ops:
  0.0 1.4 copy-start
  1.9 0.7 copy-start.12
  1.9 1.5 copy-start.13
  4.0 26.5 %copy-start.11 = (s32[6,256]{1,0:T(8,128)S(1)}, s32[6,256]{1,0:T(8,128)}, u32[]{:S(2)}) copy-start(s32[6,256]{1,0:T(8,128)} %param.9) | copy-start | bytes 18436
  30.6 5.3 %copy-start.5 = (s32[2048]{0:T(1024)}, s32[2048]{0:T(1024)S(1)}, u32[]{:S(2)}) copy-start(s32[2048]{0:T(1024)S(1)} %get-tuple-element.88) | copy-start | bytes 24580
  30.6 46.0 %copy-start.3 = (s32[2048]{0:T(1024)}, s32[2048]{0:T(1024)S(1)}, u32[]{:S(2)}) copy-start(s32[2048]{0:T(1024)S(1)} %get-tuple-element.87) | copy-start | bytes 24580
  37.2 1.0 copy-start.1
  62.1 1.3 copy-start.7
  79.6 0.7 copy-start.8
  83.0 20.7 %copy-start.6 = (s32[2048]{0:T(1024)S(1)}, s32[2048]{0:T(1024)}, u32[]{:S(2)}) copy-start(s32[2048]{0:T(1024)} %copy-done.5) | copy-start | bytes 24580
  110.4 1.0 copy-start.2
  119.6 11.8 %copy-start.4 = (s32[2048]{0:T(1024)S(1)}, s32[2048]{0:T(1024)}, u32[]{:S(2)}) copy-start(s32[2048]{0:T(1024)} %copy-done.3) | copy-start | bytes 24580
  134.5 0.7 copy-start.9
  152.5 0.7 copy-start.10

commit v11 on v9

--- a/solution.py
+++ b/solution.py
@@ -332,6 +332,141 @@
     )(pltpu.with_memory_space_constraint(doubled, pltpu.VMEM), peer_ids, region_ids)
 
 
+def split_kernel(tab_ref, idx_ref, ridx_ref, comb_ref, og_ref, bd_ref, sems):
+    peers, block_rows, lane_count = og_ref.shape
+    slots = block_rows * 2 // 3
+    half = slots // 2
+    local = tab_ref.shape[0]
+    width = bd_ref.shape[2]
+    regions = lax.axis_size("group")
+    me = lax.axis_index("dev")
+    region = lax.axis_index("group")
+    up = lax.rem(region + 1, regions)
+    down = lax.rem(region + regions - 1, regions)
+    mesh_ids = pl.DeviceIdType.MESH
+    arrived = 2 * local
+    bordering = arrived + peers * block_rows
+
+    heads = pltpu.make_async_copy(tab_ref.at[:, pl.ds(0, lane_count)], comb_ref.at[pl.ds(0, local)], sems.at[4])
+    heads.start()
+    tails = pltpu.make_async_copy(
+        tab_ref.at[:, pl.ds(lane_count, lane_count)], comb_ref.at[pl.ds(local, local)], sems.at[5]
+    )
+    tails.start()
+
+    barrier = pltpu.get_barrier_semaphore()
+    targets = far_first(me, peers)
+    for e in targets:
+        pl.semaphore_signal(barrier, inc=1, device_id=(region, e), device_id_type=mesh_ids)
+    pl.semaphore_signal(barrier, inc=1, device_id=(up, me), device_id_type=mesh_ids)
+    pl.semaphore_signal(barrier, inc=1, device_id=(down, me), device_id_type=mesh_ids)
+
+    for h in range(2):
+        for p in range(width):
+            source = ridx_ref[h * width + p]
+            line = tab_ref[pl.ds(source, 1), :]
+            for part in range(2):
+                bd_ref[h, part, pl.ds(p, 1), :] = line[:, part * lane_count : (part + 1) * lane_count]
+
+    lanes = lax.broadcasted_iota(jnp.int32, (1, lane_count), 1)
+
+    def pack(e, carry):
+        for r in range(half):
+            first = tab_ref[pl.ds(idx_ref[e * slots + r], 1), :]
+            second = tab_ref[pl.ds(idx_ref[e * slots + r + half], 1), :]
+            og_ref[e, pl.ds(r, 1), :] = first[:, :lane_count]
+            og_ref[e, pl.ds(r + half, 1), :] = second[:, :lane_count]
+            og_ref[e, pl.ds(slots + r, 1), :] = jnp.where(
+                lanes < lane_count // 2, first[:, lane_count:], second[:, lane_count:]
+            )
+        return carry
+
+    lax.fori_loop(0, peers, pack, 0)
+
+    pl.semaphore_wait(barrier, peers + 1)
+
+    mine = pl.ds(pl.multiple_of(arrived + me * block_rows, 4), block_rows)
+    for e in targets:
+        pltpu.make_async_remote_copy(
+            src_ref=og_ref.at[e],
+            dst_ref=comb_ref.at[mine],
+            send_sem=sems.at[0],
+            recv_sem=sems.at[1],
+            device_id=(region, e),
+            device_id_type=mesh_ids,
+        ).start()
+    pltpu.make_async_copy(og_ref.at[me], comb_ref.at[mine], sems.at[1]).start()
+    for part in range(2):
+        pltpu.make_async_remote_copy(
+            src_ref=bd_ref.at[1, part],
+            dst_ref=comb_ref.at[pl.ds(bordering + part * 2 * width, width)],
+            send_sem=sems.at[2],
+            recv_sem=sems.at[3],
+            device_id=(up, me),
+            device_id_type=mesh_ids,
+        ).start()
+        pltpu.make_async_remote_copy(
+            src_ref=bd_ref.at[0, part],
+            dst_ref=comb_ref.at[pl.ds(bordering + part * 2 * width + width, width)],
+            send_sem=sems.at[2],
+            recv_sem=sems.at[3],
+            device_id=(down, me),
+            device_id_type=mesh_ids,
+        ).start()
+
+    pltpu.make_async_copy(og_ref.at[pl.ds(0, peers - 1)], og_ref.at[pl.ds(0, peers - 1)], sems.at[0]).wait()
+    pltpu.make_async_copy(bd_ref, bd_ref, sems.at[2]).wait()
+    pltpu.make_async_copy(og_ref, og_ref, sems.at[1]).wait()
+    pltpu.make_async_copy(bd_ref, bd_ref, sems.at[3]).wait()
+    heads.wait()
+    tails.wait()
+
+
+def split_exchange(table, peer_ids, region_ids, peers):
+    local, slab_rows = table.shape
+    slots = peer_ids.shape[0] // peers
+    width = region_ids.shape[0] // 2
+    lane_count = 128
+    widened = jnp.concatenate([table, table[:, lane_count:]], axis=1)
+    vmem = pl.BlockSpec(memory_space=pltpu.VMEM)
+    smem = pl.BlockSpec(memory_space=pltpu.SMEM)
+    block_rows = slots + slots // 2
+    return pl.pallas_call(
+        split_kernel,
+        out_shape=jax.ShapeDtypeStruct((2 * local + peers * block_rows + 4 * width, lane_count), table.dtype),
+        in_specs=[vmem, smem, smem],
+        out_specs=vmem,
+        scratch_shapes=[
+            pltpu.VMEM((peers, block_rows, lane_count), table.dtype),
+            pltpu.VMEM((2, 2, width, lane_count), table.dtype),
+            pltpu.SemaphoreType.DMA((6,)),
+        ],
+        compiler_params=pltpu.CompilerParams(collective_id=3, has_side_effects=True),
+    )(pltpu.with_memory_space_constraint(widened, pltpu.VMEM), peer_ids, region_ids)
+
+
+def split_sources(halo_ids, local, peers, slots, width):
+    half = slots // 2
+    block_rows = slots + half
+    entry = halo_ids - local
+    slot = entry % slots
+    sender = entry // slots
+    from_peer = (entry >= 0) & (entry < peers * slots)
+    from_region = entry >= peers * slots
+    place = entry - peers * slots
+    base = 2 * local + peers * block_rows
+    head = jnp.where(
+        from_peer, 2 * local + sender * block_rows + slot, jnp.where(from_region, base + place, halo_ids)
+    )
+    tail = jnp.where(
+        from_peer,
+        2 * local + sender * block_rows + slots + slot % half,
+        jnp.where(from_region, base + 2 * width + place, local + halo_ids),
+    )
+    upper = from_peer & (slot >= half)
+    return head, tail, upper
+
+
 def paired_sources(halo_ids, local, peers, slots, width):
     half = slots // 2
     entry = halo_ids - local
@@ -347,7 +482,7 @@
     return row, upper
 
 
-def assemble(voxels, layers, peer_ids, region_ids, halo_ids, paired_ids):
+def assemble(voxels, layers, peer_ids, region_ids, halo_ids, paired_ids, split_ids):
     slab_table = face_slabs(voxels, layers)
     peers = lax.axis_size("dev")
     if layers == 1 and paired_ids is not None:
@@ -357,6 +492,14 @@
         width = slab_table.shape[0]
         chosen = jnp.where(upper[..., None], lines[..., width:], lines[..., :width])
         return jnp.moveaxis(chosen, 2, 0)
+    if layers == 3 and split_ids is not None:
+        head, tail, upper = split_ids
+        table = split_exchange(slab_table.T, peer_ids, region_ids, peers)
+        first = table.at[head].get(mode="promise_in_bounds")
+        second = table.at[tail].get(mode="promise_in_bounds")
+        lanes = first.shape[-1] // 2
+        rest = jnp.where(upper[..., None], second[..., lanes:], second[..., :lanes])
+        return jnp.moveaxis(jnp.concatenate([first, rest], axis=-1), 2, 0)
     combined = exchange(slab_table.T, peer_ids, region_ids, peers, layers).T
     picked = combined.at[:, halo_ids].get(mode="promise_in_bounds")
     return picked
@@ -373,14 +516,17 @@
     paired_ids = None
     if slots % 2 == 0:
         paired_ids = paired_sources(halo_ids, local, peers, slots, region_ids.shape[0] // 2)
+    split_ids = None
+    if slots % 2 == 0:
+        split_ids = split_sources(halo_ids, local, peers, slots, region_ids.shape[0] // 2)
     voxels = level_set.reshape(8, 8, 8, count)
     speeds = speed.reshape(8, 8, 8, count)
     for offset_step in range(OFFSET_STEPS):
-        picked = assemble(voxels, 3, peer_ids, region_ids, halo_ids, paired_ids)
+        picked = assemble(voxels, 3, peer_ids, region_ids, halo_ids, paired_ids, split_ids)
         voxels = advect_leaves(voxels, lax.optimization_barrier(speeds), picked)
         sign_field = voxels / jnp.sqrt(voxels * voxels + 1.0)
         for redist_pass in range(REDIST_PASSES):
-            picked = assemble(voxels, 1, peer_ids, region_ids, halo_ids, paired_ids)
+            picked = assemble(voxels, 1, peer_ids, region_ids, halo_ids, paired_ids, split_ids)
             voxels = relax_leaves(voxels, sign_field, picked)
     return voxels.reshape(512, count)
 

time: 156 us -> 179 us (1.15)
  local copies, waits for them, and re-layouts: 37 us -> 59.4 us
  other arithmetic: 22.2 us -> 28 us
  Pallas kernels: 94.8 us -> 89.3 us
    unnamed x76 -> x72, local copies, waits for them, and re-layouts: 5.27 us -> 16 us
    gather x4 -> x6, local copies, waits for them, and re-layouts: 11.4 us -> 18.4 us  [the longest x4 10.1 us: assemble(): first = table.at[head].get(mode='promise_in_bounds')]
    pallas_call x2, Pallas kernels: 47.2 us -> 41.8 us  [split_exchange(): pl.pallas_call(split_kernel, out_shape=jax.ShapeDtypeStruct((2 * local +...]
    concatenate x0 -> x2, other arithmetic: none -> 3.37 us  [split_exchange(): widened = jnp.concatenate([table, table[:, lane_count:]], axis=1)]
    slice x0 -> x4, local copies, waits for them, and re-layouts: none -> 2.88 us  [the longest x2 2.78 us: assemble(): rest = jnp.where(upper[..., None], second[..., lanes:], second[..., :lanes])]
    select_n x0 -> x2, other arithmetic: none -> 2.1 us  [assemble(): rest = jnp.where(upper[..., None], second[..., lanes:], second[..., :lanes])]
where the time goes in v11:
time: 179 us; the launch traced here: 178 us
  Pallas kernels  89.3 us (50%)
  local copies, waits for them, and re-layouts  59.4 us (33%)
  other arithmetic  28 us (16%)
    pallas_call x4, Pallas kernels, paired_exchange(): pl.pallas_call(paired_kernel, out_shape=pltpu.VMEM((local + peers * slots...  47.5 us
    pallas_call x2, Pallas kernels, split_exchange(): pl.pallas_call(split_kernel, out_shape=jax.ShapeDtypeStruct((2 * local +...  41.8 us
    unnamed x72, local copies, waits for them, and re-layouts  16 us
    sub x2, other arithmetic, advect_leaves(): return voxels - advect_scale * speeds * jnp.sqrt(squared)  14.6 us
    gather x4, local copies, waits for them, and re-layouts, assemble(): lines = table.at[rows].get(mode='promise_in_bounds')  10.8 us
    gather x4, local copies, waits for them, and re-layouts, assemble(): first = table.at[head].get(mode='promise_in_bounds')  10.1 us
    gather x2, local copies, waits for them, and re-layouts, assemble(): second = table.at[tail].get(mode='promise_in_bounds')  8.28 us
    sub x4, other arithmetic, relax_leaves(): return voxels - relax_scale * sign_field * (jnp.sqrt(squared) - 1.0)  5.1 us

profile of v11, /device:TPU:1, one launch (start us, length us, event | category | flops | bytes accessed | tf_op | source)
XLA Modules:
  0.0 178.1 jit_solution(13589354911198093160)
XLA Ops:
  5.3 1.7 pad_maximum_fusion.tab_ref
  8.5 23.7 %shard_map.55 = f32[3904,128]{1,0:T(8,128)} custom-call(f32[1536,256]{1,0:T(8,128)S(1)} %pad_maximum_fusion.tab_ref, s32[512]{0:T(512)} %min.120.idx_ref, s32[32]{0:T(128)} %min.123.ridx_ref), custom_call_target="tpu_custom_call" | custom-call | tf_op jit(solution)/shard_map/pallas_call | solution.py:434
  32.3 4.1 %gather_fusion.1 = f32[1536,128]{1,0:T(8,128)S(1)} fusion(f32[3904,128]{1,0:T(8,128)} %shard_map.55, s32[2048]{0:T(1024)S(1)} %get-tuple-element.93), kind=kCustom, calls=%fused_computation.1 | custom fusion | bytes 1579008 | tf_op jit(solution)/shard_map/gather | solution.py:499
  37.8 1.5 copy.119
  39.4 2.1 %copy.120 = f32[6,256,64]{1,2,0:T(8,128)} copy(f32[6,256,64]{2,1,0:T(8,128)} %get-tuple-element.27) | data formatting | bytes 786432
  42.6 3.7 %gather_fusion = f32[1536,128]{1,0:T(8,128)} fusion(f32[3904,128]{1,0:T(8,128)S(1)} %copy-done, s32[2048]{0:T(1024)S(1)} %pad_clamp_fusion.2), kind=kCustom, calls=%fused_computation | custom fusion | bytes 1579008 | tf_op jit(solution)/shard_map/gather | solution.py:498
  46.3 1.4 copy.51
  49.7 7.3 %multiply_subtract_fusion.5 = f32[8,8,8,256]{3,2,1,0:T(8,128)S(1)} fusion(f32[8,8,8,256]{3,2,1,0:T(8,128)S(1)} %bitcast.176, f32[8,8,13,256]{3,2,1,0:T(8,128)S(1)} %slice_subtract_fusion.1, f32[8,13,8,256]{3,2,1,0:T(8,128)S(1)} %slice_subtract_fusion.4, f32[13,8,8,256]{3,2,1,0:T(8,128)S(1)} %slice_subtract_fusion.5, f32[8,8,8,256]{3,2,1,0:T(8,128)S(1)} %bitcast.189), kind=kLoop, calls=%fused_computation.263 | loop fusion | flops 53739520 | bytes 11010048 | tf_op jit(solution)/shard_map/sub | solution.py:104
  58.1 12.0 %shard_map.56 = f32[1824,128]{1,0:T(8,128)S(1)} custom-call(f32[1536,128]{1,0:T(8,128)S(1)} %pad_maximum_fusion.8.tab_ref, s32[512]{0:T(512)} %min.120.idx_ref, s32[32]{0:T(128)} %min.123.ridx_ref), custom_call_target="tpu_custom_call" | custom-call | tf_op jit(solution)/shard_map/pallas_call | solution.py:321
  70.1 2.6 %gather_fusion.2 = f32[1536,128]{1,0:T(8,128)S(1)} fusion(f32[1824,128]{1,0:T(8,128)S(1)} %shard_map.56, s32[2048]{0:T(1024)S(1)} %get-tuple-element.92), kind=kCustom, calls=%fused_computation.2 | custom fusion | bytes 1579008 | tf_op jit(solution)/shard_map/gather | solution.py:491
  75.9 12.0 %shard_map.57 = f32[1824,128]{1,0:T(8,128)S(1)} custom-call(f32[1536,128]{1,0:T(8,128)S(1)} %pad_maximum_fusion.9.tab_ref, s32[512]{0:T(512)} %min.120.idx_ref, s32[32]{0:T(128)} %min.123.ridx_ref), custom_call_target="tpu_custom_call" | custom-call | tf_op jit(solution)/shard_map/pallas_call | solution.py:321
  87.9 2.8 %gather_fusion.3 = f32[1536,128]{1,0:T(8,128)S(1)} fusion(f32[1824,128]{1,0:T(8,128)S(1)} %shard_map.57, s32[2048]{0:T(1024)S(1)} %get-tuple-element.92), kind=kCustom, calls=%fused_computation.3 | custom fusion | bytes 1579008 | tf_op jit(solution)/shard_map/gather | solution.py:491
  97.5 1.7 pad_maximum_fusion.1.tab_ref
  99.2 18.1 %shard_map.58 = f32[3904,128]{1,0:T(8,128)} custom-call(f32[1536,256]{1,0:T(8,128)S(1)} %pad_maximum_fusion.1.tab_ref, s32[512]{0:T(512)} %min.120.idx_ref, s32[32]{0:T(128)} %min.123.ridx_ref), custom_call_target="tpu_custom_call" | custom-call | tf_op jit(solution)/shard_map/pallas_call | solution.py:434
  117.2 4.1 %gather_fusion.5 = f32[1536,128]{1,0:T(8,128)S(1)} fusion(f32[3904,128]{1,0:T(8,128)} %shard_map.58, s32[2048]{0:T(1024)S(1)} %get-tuple-element.93), kind=kCustom, calls=%fused_computation.5 | custom fusion | bytes 1579008 | tf_op jit(solution)/shard_map/gather | solution.py:499
  122.8 1.5 copy.125
  124.3 2.1 %copy.126 = f32[6,256,64]{1,2,0:T(8,128)} copy(f32[6,256,64]{2,1,0:T(8,128)} %get-tuple-element.21) | data formatting | bytes 786432
  127.5 3.7 %gather_fusion.4 = f32[1536,128]{1,0:T(8,128)} fusion(f32[3904,128]{1,0:T(8,128)S(1)} %copy-done.1, s32[2048]{0:T(1024)S(1)} %pad_clamp_fusion.2), kind=kCustom, calls=%fused_computation.4 | custom fusion | bytes 1579008 | tf_op jit(solution)/shard_map/gather | solution.py:498
  134.6 7.3 %multiply_subtract_fusion.2 = f32[8,8,8,256]{3,2,1,0:T(8,128)S(1)} fusion(f32[8,8,8,256]{3,2,1,0:T(8,128)S(1)} %multiply_subtract_fusion.3, f32[8,8,13,256]{3,2,1,0:T(8,128)S(1)} %slice_subtract_fusion, f32[8,13,8,256]{3,2,1,0:T(8,128)S(1)} %slice_subtract_fusion.2, f32[13,8,8,256]{3,2,1,0:T(8,128)S(1)} %slice_subtract_fusion.3, ...), kind=kLoop, calls=%fused_computation.259 | loop fusion | flops 53739520 | bytes 11010048 | tf_op jit(solution)/shard_map/sub | solution.py:104
  143.0 11.4 %shard_map.59 = f32[1824,128]{1,0:T(8,128)S(1)} custom-call(f32[1536,128]{1,0:T(8,128)S(1)} %pad_maximum_fusion.10.tab_ref, s32[512]{0:T(512)} %min.120.idx_ref, s32[32]{0:T(128)} %min.123.ridx_ref), custom_call_target="tpu_custom_call" | custom-call | tf_op jit(solution)/shard_map/pallas_call | solution.py:321
  154.4 2.8 %gather_fusion.6 = f32[1536,128]{1,0:T(8,128)S(1)} fusion(f32[1824,128]{1,0:T(8,128)S(1)} %shard_map.59, s32[2048]{0:T(1024)S(1)} %get-tuple-element.92), kind=kCustom, calls=%fused_computation.6 | custom fusion | bytes 1579008 | tf_op jit(solution)/shard_map/gather | solution.py:491
  160.4 12.1 %shard_map.60 = f32[1824,128]{1,0:T(8,128)S(1)} custom-call(f32[1536,128]{1,0:T(8,128)S(1)} %pad_maximum_fusion.11.tab_ref, s32[512]{0:T(512)} %min.120.idx_ref, s32[32]{0:T(128)} %min.123.ridx_ref), custom_call_target="tpu_custom_call" | custom-call | tf_op jit(solution)/shard_map/pallas_call | solution.py:321
  172.6 2.6 %gather_fusion.7 = f32[1536,128]{1,0:T(8,128)S(1)} fusion(f32[1824,128]{1,0:T(8,128)S(1)} %shard_map.60, s32[2048]{0:T(1024)S(1)} %get-tuple-element.92), kind=kCustom, calls=%fused_computation.7 | custom fusion | bytes 1579008 | tf_op jit(solution)/shard_map/gather | solution.py:491
  176.2 1.9 %multiply_subtract_fusion = f32[8,8,8,256]{3,2,1,0:T(8,128)} fusion(f32[8,8,8,256]{3,2,1,0:T(8,128)S(1)} %multiply_subtract_fusion.1, f32[8,8,1,256]{3,2,1,0:T(1,128)S(1)} %copy.108, f32[8,8,1,256]{3,2,1,0:T(1,128)S(1)} %copy.107, f32[8,1,8,256]{3,2,1,0:T(8,128)S(1)} %get-tuple-element.68, f32[8,1,8,256]{3,2,1,0:T(8,128)S(1)} %get-tuple-element.69, ...), kind=kLoop, calls=%fused_computation.256 | loop fusion | flops 7208960 | bytes 1966080 | tf_op jit(solution)/shard_map/sub | solution.py:120
  (196 shorter events, 32.5 us)
Async XLA Ops:
  2.4 1.0 copy-start.2
  4.1 1.2 copy-start.3
  5.3 1.7 copy-start.8
  5.3 2.5 %copy-start.9 = (s32[2,16]{1,0:T(2,128)S(1)}, s32[2,16]{1,0:T(2,128)}, u32[]{:S(2)}) copy-start(s32[2,16]{1,0:T(2,128)} %param.8) | copy-start | bytes 388
  8.5 23.7 %copy-start.7 = (s32[6,256]{1,0:T(8,128)S(1)}, s32[6,256]{1,0:T(8,128)}, u32[]{:S(2)}) copy-start(s32[6,256]{1,0:T(8,128)} %param.9) | copy-start | bytes 18436
  37.8 4.8 %copy-start = (f32[3904,128]{1,0:T(8,128)S(1)}, f32[3904,128]{1,0:T(8,128)}, u32[]{:S(2)}) copy-start(f32[3904,128]{1,0:T(8,128)} %shard_map.55) | copy-start | bytes 5996548
  48.6 1.0 copy-start.5
  96.2 1.2 copy-start.4
  122.8 4.7 %copy-start.1 = (f32[3904,128]{1,0:T(8,128)S(1)}, f32[3904,128]{1,0:T(8,128)}, u32[]{:S(2)}) copy-start(f32[3904,128]{1,0:T(8,128)} %shard_map.58) | copy-start | bytes 5996548
  133.5 1.0 copy-start.6

commit v12 on v9

--- a/solution.py
+++ b/solution.py
@@ -41,19 +41,10 @@
     return jnp.concatenate([piece.reshape(64 * layers, count) for piece in pieces], axis=1)
 
 
-def weno_side(first, second, third, fourth, fifth):
+def weno_side(first, second, third, fourth, fifth, smooth_a, smooth_b, smooth_c):
     guess_a = first / 3.0 - 7.0 * second / 6.0 + 11.0 * third / 6.0
     guess_b = -second / 6.0 + 5.0 * third / 6.0 + fourth / 3.0
     guess_c = third / 3.0 + 5.0 * fourth / 6.0 - fifth / 6.0
-    bend_a = first - 2.0 * second + third
-    tilt_a = first - 4.0 * second + 3.0 * third
-    bend_b = second - 2.0 * third + fourth
-    tilt_b = second - fourth
-    bend_c = third - 2.0 * fourth + fifth
-    tilt_c = 3.0 * third - 4.0 * fourth + fifth
-    smooth_a = weno_floor + 13.0 / 12.0 * bend_a * bend_a + 0.25 * tilt_a * tilt_a
-    smooth_b = weno_floor + 13.0 / 12.0 * bend_b * bend_b + 0.25 * tilt_b * tilt_b
-    smooth_c = weno_floor + 13.0 / 12.0 * bend_c * bend_c + 0.25 * tilt_c * tilt_c
     square_a = smooth_a * smooth_a
     square_b = smooth_b * smooth_b
     square_c = smooth_c * smooth_c
@@ -67,12 +58,32 @@
 
 def one_sided(padded, along):
     differences = jnp.diff(padded, axis=along)
-
-    def window(lowest):
-        return lax.slice_in_dim(differences, lowest, lowest + 8, axis=along)
-
-    backward = weno_side(window(0), window(1), window(2), window(3), window(4))
-    forward = weno_side(window(5), window(4), window(3), window(2), window(1))
+    span = differences.shape[along] - 2
+
+    def window(lowest, size=8):
+        return lax.slice_in_dim(differences, lowest, lowest + size, axis=along)
+
+    low, mid, high = window(0, span), window(1, span), window(2, span)
+    bend = low - 2.0 * mid + high
+    curve = weno_floor + 13.0 / 12.0 * bend * bend
+    rising = low - 4.0 * mid + 3.0 * high
+    falling = 3.0 * low - 4.0 * mid + high
+    central = low - high
+    rising = curve + 0.25 * rising * rising
+    falling = curve + 0.25 * falling * falling
+    central = curve + 0.25 * central * central
+
+    def at(values, lowest):
+        return lax.slice_in_dim(values, lowest, lowest + 8, axis=along)
+
+    backward = weno_side(
+        window(0), window(1), window(2), window(3), window(4),
+        at(rising, 0), at(central, 1), at(falling, 2),
+    )
+    forward = weno_side(
+        window(5), window(4), window(3), window(2), window(1),
+        at(falling, 3), at(central, 2), at(rising, 1),
+    )
     return (backward, forward)
 
 

time: 156 us -> 166 us (1.064)
  local copies, waits for them, and re-layouts: 37 us -> 44.3 us
  other arithmetic: 22.2 us -> 24.4 us
    add x0 -> x6, other arithmetic: none -> 8.52 us  [one_sided(): rising = curve + 0.25 * rising * rising]
    sub x2, other arithmetic: 14.6 us -> 8.18 us  [advect_leaves(): return voxels - advect_scale * speeds * jnp.sqrt(squared)]
    slice x2, local copies, waits for them, and re-layouts: 0.25 us -> 3 us  [face_part(): return picked[:, side, :].reshape(extent + (count,))]
    another operation x16, local copies, waits for them, and re-layouts: 0.99 us -> 2.84 us  [face_part(): return picked[:, side, :].reshape(extent + (count,))]
    unnamed x76 -> x104, local copies, waits for them, and re-layouts: 5.27 us -> 6.36 us
where the time goes in v12:
time: 166 us; the launch traced here: 165 us
  Pallas kernels  95 us (57%)
  local copies, waits for them, and re-layouts  44.3 us (27%)
  other arithmetic  24.4 us (15%)
    pallas_call x4, Pallas kernels, paired_exchange(): pl.pallas_call(paired_kernel, out_shape=pltpu.VMEM((local + peers * slots...  47.8 us
    pallas_call x2, Pallas kernels, exchange(): pl.pallas_call(exchange_kernel, out_shape=(pltpu.VMEM if layers == 1 else...  47.2 us
    gather x4, local copies, waits for them, and re-layouts, assemble(): picked = combined.at[:, halo_ids].get(mode='promise_in_bounds')  12.5 us
    gather x4, local copies, waits for them, and re-layouts, assemble(): lines = table.at[rows].get(mode='promise_in_bounds')  10.4 us
    add x6, other arithmetic, one_sided(): rising = curve + 0.25 * rising * rising  8.52 us
    sub x2, other arithmetic, advect_leaves(): return voxels - advect_scale * speeds * jnp.sqrt(squared)  8.18 us
    unnamed x104, local copies, waits for them, and re-layouts  6.36 us
    sub x4, other arithmetic, relax_leaves(): return voxels - relax_scale * sign_field * (jnp.sqrt(squared) - 1.0)  5.09 us

profile of v12, /device:TPU:1, one launch (start us, length us, event | category | flops | bytes accessed | tf_op | source)
XLA Modules:
  0.0 165.1 jit_solution(12327872628264853659)
XLA Ops:
  5.6 26.5 %shard_map.55 = f32[2080,192]{1,0:T(8,128)} custom-call(f32[1536,192]{1,0:T(8,128)S(1)} %bitcast.169, s32[512]{0:T(512)} %min.120.idx_ref, s32[32]{0:T(128)} %min.123.ridx_ref), custom_call_target="tpu_custom_call" | custom-call | tf_op jit(solution)/shard_map/pallas_call | solution.py:231
  32.2 5.3 %gather_fusion = f32[1536,192]{1,0:T(8,128)S(1)} fusion(f32[192,2080]{0,1:T(8,128)} %bitcast.171, s32[2048]{0:T(1024)S(1)} %get-tuple-element.106), kind=kCustom, calls=%fused_computation | custom fusion | bytes 2365440 | tf_op jit(solution)/shard_map/gather | solution.py:372
  38.9 1.6 fusion.11
  40.7 1.7 %fusion.15 = (f32[8,11,8,256]{3,2,1,0:T(8,128)}, f32[8,11,8,256]{3,2,1,0:T(8,128)}, f32[8,11,8,256]{3,2,1,0:T(8,128)}) fusion(f32[8,13,8,256]{3,2,1,0:T(8,128)S(1)} %slice_subtract_fusion.4), kind=kLoop, calls=%fused_computation.65 | loop fusion | flops 4145152 | bytes 4325376 | tf_op jit(solution)/shard_map/add | solution.py:72
  46.0 4.0 %multiply_subtract_fusion.5 = f32[8,8,8,256]{3,2,1,0:T(8,128)S(1)} fusion(f32[8,8,8,256]{3,2,1,0:T(8,128)S(1)} %bitcast.178, f32[8,8,13,256]{3,2,1,0:T(8,128)S(1)} %slice_subtract_fusion.1, f32[8,8,11,256]{3,2,1,0:T(8,128)S(1)} %get-tuple-element.22, f32[8,8,11,256]{3,2,1,0:T(8,128)S(1)} %get-tuple-element.21, f32[8,8,11,256]{3,2,1,0:T(8,128)S(1)} %get-tuple-element.20, ...), kind=kLoop, calls=%fused_computation.257 | loop fusion | flops 27000832 | bytes 20447232 | tf_op jit(solution)/shard_map/sub | solution.py:115
  51.2 12.0 %shard_map.56 = f32[1824,128]{1,0:T(8,128)S(1)} custom-call(f32[1536,128]{1,0:T(8,128)S(1)} %pad_maximum_fusion.6.tab_ref, s32[512]{0:T(512)} %min.120.idx_ref, s32[32]{0:T(128)} %min.123.ridx_ref), custom_call_target="tpu_custom_call" | custom-call | tf_op jit(solution)/shard_map/pallas_call | solution.py:332
  63.1 2.6 %gather_fusion.1 = f32[1536,128]{1,0:T(8,128)S(1)} fusion(f32[1824,128]{1,0:T(8,128)S(1)} %shard_map.56, s32[2048]{0:T(1024)S(1)} %get-tuple-element.105), kind=kCustom, calls=%fused_computation.1 | custom fusion | bytes 1579008 | tf_op jit(solution)/shard_map/gather | solution.py:367
  66.8 1.1 multiply_subtract_fusion.4
  69.0 12.2 %shard_map.57 = f32[1824,128]{1,0:T(8,128)S(1)} custom-call(f32[1536,128]{1,0:T(8,128)S(1)} %pad_maximum_fusion.7.tab_ref, s32[512]{0:T(512)} %min.120.idx_ref, s32[32]{0:T(128)} %min.123.ridx_ref), custom_call_target="tpu_custom_call" | custom-call | tf_op jit(solution)/shard_map/pallas_call | solution.py:332
  81.2 2.6 %gather_fusion.2 = f32[1536,128]{1,0:T(8,128)S(1)} fusion(f32[1824,128]{1,0:T(8,128)S(1)} %shard_map.57, s32[2048]{0:T(1024)S(1)} %get-tuple-element.105), kind=kCustom, calls=%fused_computation.2 | custom fusion | bytes 1579008 | tf_op jit(solution)/shard_map/gather | solution.py:367
  85.0 1.1 multiply_subtract_fusion.3
  87.5 20.7 %shard_map.58 = f32[2080,192]{1,0:T(8,128)} custom-call(f32[1536,192]{1,0:T(8,128)S(1)} %bitcast.170, s32[512]{0:T(512)} %min.120.idx_ref, s32[32]{0:T(128)} %min.123.ridx_ref), custom_call_target="tpu_custom_call" | custom-call | tf_op jit(solution)/shard_map/pallas_call | solution.py:231
  108.2 5.3 %gather_fusion.3 = f32[1536,192]{1,0:T(8,128)S(1)} fusion(f32[192,2080]{0,1:T(8,128)} %bitcast.172, s32[2048]{0:T(1024)S(1)} %copy-done.20), kind=kCustom, calls=%fused_computation.3 | custom fusion | bytes 2365440 | tf_op jit(solution)/shard_map/gather | solution.py:372
  113.5 1.5 copy.80
  115.0 2.1 %fusion.129 = (f32[192,1,256]{2,0,1:T(8,128)S(1)}, f32[192,1,256]{2,0,1:T(8,128)S(1)}, f32[192,1,256]{2,0,1:T(8,128)S(1)}, f32[192,1,256]{2,0,1:T(8,128)S(1)}, f...) fusion(f32[192,6,256]{2,0,1:T(8,128)} %bitcast.186), kind=kLoop, calls=%fused_computation.376 | loop fusion | bytes 2359296 | tf_op jit(solution)/shard_map/slice | solution.py:94
  117.3 1.6 fusion.19
  119.1 1.7 %fusion.23 = (f32[8,11,8,256]{3,2,1,0:T(8,128)}, f32[8,11,8,256]{3,2,1,0:T(8,128)}, f32[8,11,8,256]{3,2,1,0:T(8,128)}) fusion(f32[8,13,8,256]{3,2,1,0:T(8,128)S(1)} %slice_subtract_fusion.2), kind=kLoop, calls=%fused_computation.73 | loop fusion | flops 4145152 | bytes 4325376 | tf_op jit(solution)/shard_map/add | solution.py:72
  124.4 4.2 %multiply_subtract_fusion.2 = f32[8,8,8,256]{3,2,1,0:T(8,128)S(1)} fusion(f32[8,8,8,256]{3,2,1,0:T(8,128)S(1)} %copy-done.1, f32[8,8,13,256]{3,2,1,0:T(8,128)S(1)} %slice_subtract_fusion, f32[8,8,11,256]{3,2,1,0:T(8,128)S(1)} %get-tuple-element.19, f32[8,8,11,256]{3,2,1,0:T(8,128)S(1)} %get-tuple-element.18, f32[8,8,11,256]{3,2,1,0:T(8,128)S(1)} %get-tuple-element.17, ...), kind=kLoop, calls=%fused_computation.253 | loop fusion | flops 27000832 | bytes 20447232 | tf_op jit(solution)/shard_map/sub | solution.py:115
  129.8 11.5 %shard_map.59 = f32[1824,128]{1,0:T(8,128)S(1)} custom-call(f32[1536,128]{1,0:T(8,128)S(1)} %pad_maximum_fusion.8.tab_ref, s32[512]{0:T(512)} %min.120.idx_ref, s32[32]{0:T(128)} %min.123.ridx_ref), custom_call_target="tpu_custom_call" | custom-call | tf_op jit(solution)/shard_map/pallas_call | solution.py:332
  141.3 2.6 %gather_fusion.4 = f32[1536,128]{1,0:T(8,128)S(1)} fusion(f32[1824,128]{1,0:T(8,128)S(1)} %shard_map.59, s32[2048]{0:T(1024)S(1)} %copy-done.18), kind=kCustom, calls=%fused_computation.4 | custom fusion | bytes 1579008 | tf_op jit(solution)/shard_map/gather | solution.py:367
  145.1 1.1 multiply_subtract_fusion.1
  147.3 12.0 %shard_map.60 = f32[1824,128]{1,0:T(8,128)S(1)} custom-call(f32[1536,128]{1,0:T(8,128)S(1)} %pad_maximum_fusion.9.tab_ref, s32[512]{0:T(512)} %min.120.idx_ref, s32[32]{0:T(128)} %min.123.ridx_ref), custom_call_target="tpu_custom_call" | custom-call | tf_op jit(solution)/shard_map/pallas_call | solution.py:332
  159.4 2.6 %gather_fusion.5 = f32[1536,128]{1,0:T(8,128)S(1)} fusion(f32[1824,128]{1,0:T(8,128)S(1)} %shard_map.60, s32[2048]{0:T(1024)S(1)} %copy-done.18), kind=kCustom, calls=%fused_computation.5 | custom fusion | bytes 1579008 | tf_op jit(solution)/shard_map/gather | solution.py:367
  163.2 1.9 %multiply_subtract_fusion = f32[8,8,8,256]{3,2,1,0:T(8,128)} fusion(f32[8,8,8,256]{3,2,1,0:T(8,128)S(1)} %multiply_subtract_fusion.1, f32[8,8,1,256]{3,2,1,0:T(1,128)S(1)} %copy.104, f32[8,8,1,256]{3,2,1,0:T(1,128)S(1)} %copy.103, f32[8,1,8,256]{3,2,1,0:T(8,128)S(1)} %get-tuple-element.82, f32[8,1,8,256]{3,2,1,0:T(8,128)S(1)} %get-tuple-element.83, ...), kind=kLoop, calls=%fused_computation.250 | loop fusion | flops 7208960 | bytes 1966080 | tf_op jit(solution)/shard_map/sub | solution.py:131
  (220 shorter events, 24.1 us)
Async XLA Ops:
  2.4 1.0 copy-start.2
  3.5 1.5 copy-start.27
  5.6 26.5 %copy-start.25 = (s32[6,256]{1,0:T(8,128)S(1)}, s32[6,256]{1,0:T(8,128)}, u32[]{:S(2)}) copy-start(s32[6,256]{1,0:T(8,128)} %param.9) | copy-start | bytes 18436
  32.1 5.3 %copy-start.19 = (s32[2048]{0:T(1024)}, s32[2048]{0:T(1024)S(1)}, u32[]{:S(2)}) copy-start(s32[2048]{0:T(1024)S(1)} %get-tuple-element.106) | copy-start | bytes 24580
  32.1 49.1 %copy-start.17 = (s32[2048]{0:T(1024)}, s32[2048]{0:T(1024)S(1)}, u32[]{:S(2)}) copy-start(s32[2048]{0:T(1024)S(1)} %get-tuple-element.105) | copy-start | bytes 24580
  40.7 1.8 %copy-start.16 = (f32[192,1,256]{2,0,1:T(8,128)S(1)}, f32[192,1,256]{2,0,1:T(8,128)}, u32[]{:S(2)}) copy-start(f32[192,1,256]{2,0,1:T(8,128)} %get-tuple-element.12) | copy-start | bytes 589828
  40.7 2.8 %copy-start.3 = (f32[512,256]{1,0:T(8,128)S(1)}, f32[512,256]{1,0:T(8,128)}, u32[]{:S(2)}) copy-start(f32[512,256]{1,0:T(8,128)} %param.5) | copy-start | bytes 1572868
  43.9 1.1 copy-start.6
  43.9 1.3 copy-start.7
  43.9 1.5 copy-start.11
  43.9 1.7 %copy-start.12 = (f32[8,11,8,256]{3,2,1,0:T(8,128)S(1)}, f32[8,11,8,256]{3,2,1,0:T(8,128)}, u32[]{:S(2)}) copy-start(f32[8,11,8,256]{3,2,1,0:T(8,128)} %get-tuple-element.33) | copy-start | bytes 2162692
  43.9 1.9 %copy-start.13 = (f32[8,11,8,256]{3,2,1,0:T(8,128)S(1)}, f32[8,11,8,256]{3,2,1,0:T(8,128)}, u32[]{:S(2)}) copy-start(f32[8,11,8,256]{3,2,1,0:T(8,128)} %get-tuple-element.34) | copy-start | bytes 2162692
  44.0 2.1 %copy-start.14 = (f32[512,256]{1,0:T(8,128)S(1)}, f32[512,256]{1,0:T(8,128)}, u32[]{:S(2)}) copy-start(f32[512,256]{1,0:T(8,128)} %param.6) | copy-start | bytes 1572868
  66.6 1.3 copy-start.21
  86.1 32.8 %copy-start = (f32[8,8,8,256]{3,2,1,0:T(8,128)}, f32[8,8,8,256]{3,2,1,0:T(8,128)S(1)}, u32[]{:S(2)}) copy-start(f32[8,8,8,256]{3,2,1,0:T(8,128)S(1)} %multiply_subtract_fusion.3) | copy-start | bytes 1572868
  87.5 20.7 %copy-start.20 = (s32[2048]{0:T(1024)S(1)}, s32[2048]{0:T(1024)}, u32[]{:S(2)}) copy-start(s32[2048]{0:T(1024)} %copy-done.19) | copy-start | bytes 24580
  119.1 2.8 %copy-start.1 = (f32[8,8,8,256]{3,2,1,0:T(8,128)S(1)}, f32[8,8,8,256]{3,2,1,0:T(8,128)}, u32[]{:S(2)}) copy-start(f32[8,8,8,256]{3,2,1,0:T(8,128)} %copy-done) | copy-start | bytes 1572868
  122.3 1.1 copy-start.4
  122.3 1.3 copy-start.5
  122.3 1.5 copy-start.8
  122.3 1.7 %copy-start.9 = (f32[8,11,8,256]{3,2,1,0:T(8,128)S(1)}, f32[8,11,8,256]{3,2,1,0:T(8,128)}, u32[]{:S(2)}) copy-start(f32[8,11,8,256]{3,2,1,0:T(8,128)} %get-tuple-element.27) | copy-start | bytes 2162692
  122.3 1.9 %copy-start.10 = (f32[8,11,8,256]{3,2,1,0:T(8,128)S(1)}, f32[8,11,8,256]{3,2,1,0:T(8,128)}, u32[]{:S(2)}) copy-start(f32[8,11,8,256]{3,2,1,0:T(8,128)} %get-tuple-element.28) | copy-start | bytes 2162692
  122.3 2.1 %copy-start.15 = (f32[512,256]{1,0:T(8,128)S(1)}, f32[512,256]{1,0:T(8,128)}, u32[]{:S(2)}) copy-start(f32[512,256]{1,0:T(8,128)} %param.6) | copy-start | bytes 1572868
  129.5 11.8 %copy-start.18 = (s32[2048]{0:T(1024)S(1)}, s32[2048]{0:T(1024)}, u32[]{:S(2)}) copy-start(s32[2048]{0:T(1024)} %copy-done.17) | copy-start | bytes 24580
  (4 other events, 2.7 us)

commit v13 on v9

--- a/solution.py
+++ b/solution.py
@@ -215,22 +215,24 @@
     local, slab_rows = table.shape
     slots = peer_ids.shape[0] // peers
     width = region_ids.shape[0] // 2
+    lanes = -(-slab_rows // 128) * 128
+    padded = jnp.pad(table, ((0, 0), (0, lanes - slab_rows)))
     vmem = pl.BlockSpec(memory_space=pltpu.VMEM)
     smem = pl.BlockSpec(memory_space=pltpu.SMEM)
     return pl.pallas_call(
         exchange_kernel,
         out_shape=(pltpu.VMEM if layers == 1 else jax.ShapeDtypeStruct)(
-            (local + peers * slots + 2 * width, slab_rows), table.dtype
+            (local + peers * slots + 2 * width, lanes), table.dtype
         ),
         in_specs=[vmem, smem, smem],
         out_specs=vmem,
         scratch_shapes=[
-            pltpu.VMEM((peers, slots, slab_rows), table.dtype),
-            pltpu.VMEM((2, width, slab_rows), table.dtype),
+            pltpu.VMEM((peers, slots, lanes), table.dtype),
+            pltpu.VMEM((2, width, lanes), table.dtype),
             pltpu.SemaphoreType.DMA((5,)),
         ],
         compiler_params=pltpu.CompilerParams(collective_id=layers, has_side_effects=True),
-    )(pltpu.with_memory_space_constraint(table, pltpu.VMEM), peer_ids, region_ids)
+    )(pltpu.with_memory_space_constraint(padded, pltpu.VMEM), peer_ids, region_ids)
 
 
 def paired_kernel(tab_ref, idx_ref, ridx_ref, comb_ref, og_ref, bd_ref, sems):
@@ -357,7 +359,8 @@
         width = slab_table.shape[0]
         chosen = jnp.where(upper[..., None], lines[..., width:], lines[..., :width])
         return jnp.moveaxis(chosen, 2, 0)
-    combined = exchange(slab_table.T, peer_ids, region_ids, peers, layers).T
+    slab_rows = slab_table.shape[0]
+    combined = exchange(slab_table.T, peer_ids, region_ids, peers, layers)[:, :slab_rows].T
     picked = combined.at[:, halo_ids].get(mode="promise_in_bounds")
     return picked
 

time: 156 us -> 168 us (1.077)
  local copies, waits for them, and re-layouts: 37 us -> 49.4 us
    transpose x0 -> x2, local copies, waits for them, and re-layouts: none -> 3.49 us  [assemble(): exchange(slab_table.T, peer_ids, region_ids, peers, layers)[:, :slab_rows]]
    unnamed x76 -> x80, local copies, waits for them, and re-layouts: 5.27 us -> 8.55 us
    pad x0 -> x2, local copies, waits for them, and re-layouts: none -> 3.05 us  [exchange(): padded = jnp.pad(table, ((0, 0), (0, lanes - slab_rows)))]
where the time goes in v13:
time: 168 us
  Pallas kernels  94.6 us (56%)
  local copies, waits for them, and re-layouts  49.4 us (29%)
  other arithmetic  22.2 us (13%)
    pallas_call x4, Pallas kernels, paired_exchange(): pl.pallas_call(paired_kernel, out_shape=pltpu.VMEM((local + peers * slots...  47.6 us
    pallas_call x2, Pallas kernels, exchange(): pl.pallas_call(exchange_kernel, out_shape=(pltpu.VMEM if layers == 1 else...  47.1 us
    sub x2, other arithmetic, advect_leaves(): return voxels - advect_scale * speeds * jnp.sqrt(squared)  14.6 us
    gather x4, local copies, waits for them, and re-layouts, assemble(): picked = combined.at[:, halo_ids].get(mode='promise_in_bounds')  13.1 us
    gather x4, local copies, waits for them, and re-layouts, assemble(): lines = table.at[rows].get(mode='promise_in_bounds')  10.8 us
    unnamed x80, local copies, waits for them, and re-layouts  8.55 us
    sub x4, other arithmetic, relax_leaves(): return voxels - relax_scale * sign_field * (jnp.sqrt(squared) - 1.0)  5.08 us
    reshape x46, local copies, waits for them, and re-layouts, face_slabs(): piece.reshape(64 * layers, count)  3.99 us

profile of v13, /device:TPU:1, one launch (start us, length us, event | category | flops | bytes accessed | tf_op | source)
XLA Modules:
  0.0 167.6 jit_solution(17463945976432637033)
XLA Ops:
  4.1 1.2 copy-done.1
  5.2 1.5 pad.7.tab_ref
  8.2 26.4 %shard_map.55 = f32[2080,256]{1,0:T(8,128)} custom-call(f32[1536,256]{1,0:T(8,128)S(1)} %pad.7.tab_ref, s32[512]{0:T(512)} %min.120.idx_ref, s32[32]{0:T(128)} %min.123.ridx_ref), custom_call_target="tpu_custom_call" | custom-call | tf_op jit(solution)/shard_map/pallas_call | solution.py:222
  34.6 1.7 %slice_bitcast_fusion.1 = f32[192,2080]{0,1:T(8,128)S(1)} fusion(f32[2080,256]{1,0:T(8,128)} %shard_map.55), kind=kLoop, calls=%fused_computation.7 | loop fusion | bytes 3194880 | tf_op jit(solution)/shard_map/transpose | solution.py:363
  36.4 4.7 %gather_fusion = f32[1536,192]{1,0:T(8,128)} fusion(f32[192,2080]{0,1:T(8,128)S(1)} %slice_bitcast_fusion.1, s32[2048]{0:T(1024)S(1)} %get-tuple-element.88), kind=kCustom, calls=%fused_computation | custom fusion | bytes 2365440 | tf_op jit(solution)/shard_map/gather | solution.py:364
  41.1 1.9 %copy.49 = f32[6,256,192]{1,2,0:T(8,128)S(1)} copy(f32[6,256,192]{2,1,0:T(8,128)} %bitcast.182) | data formatting | bytes 2359296 | tf_op jit(solution)/shard_map/gather | solution.py:364
  44.8 7.3 %multiply_subtract_fusion.5 = f32[8,8,8,256]{3,2,1,0:T(8,128)S(1)} fusion(f32[8,8,8,256]{3,2,1,0:T(8,128)S(1)} %bitcast.176, f32[8,8,13,256]{3,2,1,0:T(8,128)S(1)} %slice_subtract_fusion.1, f32[8,13,8,256]{3,2,1,0:T(8,128)S(1)} %slice_subtract_fusion.4, f32[13,8,8,256]{3,2,1,0:T(8,128)S(1)} %slice_subtract_fusion.5, f32[8,8,8,256]{3,2,1,0:T(8,128)S(1)} %bitcast.187), kind=kLoop, calls=%fused_computation.259 | loop fusion | flops 53739520 | bytes 11010048 | tf_op jit(solution)/shard_map/sub | solution.py:104
  53.2 12.0 %shard_map.56 = f32[1824,128]{1,0:T(8,128)S(1)} custom-call(f32[1536,128]{1,0:T(8,128)S(1)} %pad_maximum_fusion.6.tab_ref, s32[512]{0:T(512)} %min.120.idx_ref, s32[32]{0:T(128)} %min.123.ridx_ref), custom_call_target="tpu_custom_call" | custom-call | tf_op jit(solution)/shard_map/pallas_call | solution.py:323
  65.2 2.6 %gather_fusion.1 = f32[1536,128]{1,0:T(8,128)S(1)} fusion(f32[1824,128]{1,0:T(8,128)S(1)} %shard_map.56, s32[2048]{0:T(1024)S(1)} %get-tuple-element.87), kind=kCustom, calls=%fused_computation.1 | custom fusion | bytes 1579008 | tf_op jit(solution)/shard_map/gather | solution.py:358
  71.7 12.0 %shard_map.57 = f32[1824,128]{1,0:T(8,128)S(1)} custom-call(f32[1536,128]{1,0:T(8,128)S(1)} %pad_maximum_fusion.7.tab_ref, s32[512]{0:T(512)} %min.120.idx_ref, s32[32]{0:T(128)} %min.123.ridx_ref), custom_call_target="tpu_custom_call" | custom-call | tf_op jit(solution)/shard_map/pallas_call | solution.py:323
  83.7 2.8 %gather_fusion.2 = f32[1536,128]{1,0:T(8,128)S(1)} fusion(f32[1824,128]{1,0:T(8,128)S(1)} %shard_map.57, s32[2048]{0:T(1024)S(1)} %get-tuple-element.87), kind=kCustom, calls=%fused_computation.2 | custom fusion | bytes 1579008 | tf_op jit(solution)/shard_map/gather | solution.py:358
  87.7 1.1 multiply_subtract_fusion.3
  90.1 1.2 copy-done.2
  91.3 1.5 pad.8.tab_ref
  92.8 20.7 %shard_map.58 = f32[2080,256]{1,0:T(8,128)} custom-call(f32[1536,256]{1,0:T(8,128)S(1)} %pad.8.tab_ref, s32[512]{0:T(512)} %min.120.idx_ref, s32[32]{0:T(128)} %min.123.ridx_ref), custom_call_target="tpu_custom_call" | custom-call | tf_op jit(solution)/shard_map/pallas_call | solution.py:222
  113.6 1.7 %slice_bitcast_fusion = f32[192,2080]{0,1:T(8,128)S(1)} fusion(f32[2080,256]{1,0:T(8,128)} %shard_map.58), kind=kLoop, calls=%fused_computation.6 | loop fusion | bytes 3194880 | tf_op jit(solution)/shard_map/transpose | solution.py:363
  115.3 4.7 %gather_fusion.3 = f32[1536,192]{1,0:T(8,128)} fusion(f32[192,2080]{0,1:T(8,128)S(1)} %slice_bitcast_fusion, s32[2048]{0:T(1024)S(1)} %copy-done.8), kind=kCustom, calls=%fused_computation.3 | custom fusion | bytes 2365440 | tf_op jit(solution)/shard_map/gather | solution.py:364
  120.0 1.9 %copy.80 = f32[6,256,192]{1,2,0:T(8,128)S(1)} copy(f32[6,256,192]{2,1,0:T(8,128)} %bitcast.181) | data formatting | bytes 2359296 | tf_op jit(solution)/shard_map/gather | solution.py:364
  123.7 7.3 %multiply_subtract_fusion.2 = f32[8,8,8,256]{3,2,1,0:T(8,128)S(1)} fusion(f32[8,8,8,256]{3,2,1,0:T(8,128)S(1)} %multiply_subtract_fusion.3, f32[8,8,13,256]{3,2,1,0:T(8,128)S(1)} %slice_subtract_fusion, f32[8,13,8,256]{3,2,1,0:T(8,128)S(1)} %slice_subtract_fusion.2, f32[13,8,8,256]{3,2,1,0:T(8,128)S(1)} %slice_subtract_fusion.3, ...), kind=kLoop, calls=%fused_computation.255 | loop fusion | flops 53739520 | bytes 11010048 | tf_op jit(solution)/shard_map/sub | solution.py:104
  132.1 11.5 %shard_map.59 = f32[1824,128]{1,0:T(8,128)S(1)} custom-call(f32[1536,128]{1,0:T(8,128)S(1)} %pad_maximum_fusion.8.tab_ref, s32[512]{0:T(512)} %min.120.idx_ref, s32[32]{0:T(128)} %min.123.ridx_ref), custom_call_target="tpu_custom_call" | custom-call | tf_op jit(solution)/shard_map/pallas_call | solution.py:323
  143.7 2.8 %gather_fusion.4 = f32[1536,128]{1,0:T(8,128)S(1)} fusion(f32[1824,128]{1,0:T(8,128)S(1)} %shard_map.59, s32[2048]{0:T(1024)S(1)} %copy-done.6), kind=kCustom, calls=%fused_computation.4 | custom fusion | bytes 1579008 | tf_op jit(solution)/shard_map/gather | solution.py:358
  149.9 12.0 %shard_map.60 = f32[1824,128]{1,0:T(8,128)S(1)} custom-call(f32[1536,128]{1,0:T(8,128)S(1)} %pad_maximum_fusion.9.tab_ref, s32[512]{0:T(512)} %min.120.idx_ref, s32[32]{0:T(128)} %min.123.ridx_ref), custom_call_target="tpu_custom_call" | custom-call | tf_op jit(solution)/shard_map/pallas_call | solution.py:323
  162.0 2.6 %gather_fusion.5 = f32[1536,128]{1,0:T(8,128)S(1)} fusion(f32[1824,128]{1,0:T(8,128)S(1)} %shard_map.60, s32[2048]{0:T(1024)S(1)} %copy-done.6), kind=kCustom, calls=%fused_computation.5 | custom fusion | bytes 1579008 | tf_op jit(solution)/shard_map/gather | solution.py:358
  165.8 1.9 %multiply_subtract_fusion = f32[8,8,8,256]{3,2,1,0:T(8,128)} fusion(f32[8,8,8,256]{3,2,1,0:T(8,128)S(1)} %multiply_subtract_fusion.1, f32[8,8,1,256]{3,2,1,0:T(1,128)S(1)} %copy.104, f32[8,8,1,256]{3,2,1,0:T(1,128)S(1)} %copy.103, f32[8,1,8,256]{3,2,1,0:T(8,128)S(1)} %get-tuple-element.64, f32[8,1,8,256]{3,2,1,0:T(8,128)S(1)} %get-tuple-element.65, ...), kind=kLoop, calls=%fused_computation.252 | loop fusion | flops 7208960 | bytes 1966080 | tf_op jit(solution)/shard_map/sub | solution.py:120
  (194 shorter events, 21.4 us)
Async XLA Ops:
  2.4 1.0 copy-start
  4.1 1.2 copy-start.1
  5.2 1.5 copy-start.14
  5.2 2.3 %copy-start.15 = (s32[2,16]{1,0:T(2,128)S(1)}, s32[2,16]{1,0:T(2,128)}, u32[]{:S(2)}) copy-start(s32[2,16]{1,0:T(2,128)} %param.8) | copy-start | bytes 388
  34.6 1.8 %copy-start.13 = (s32[6,256]{1,0:T(8,128)S(1)}, s32[6,256]{1,0:T(8,128)}, u32[]{:S(2)}) copy-start(s32[6,256]{1,0:T(8,128)} %param.9) | copy-start | bytes 18436
  36.4 4.7 %copy-start.7 = (s32[2048]{0:T(1024)}, s32[2048]{0:T(1024)S(1)}, u32[]{:S(2)}) copy-start(s32[2048]{0:T(1024)S(1)} %get-tuple-element.88) | copy-start | bytes 24580
  36.4 47.3 %copy-start.5 = (s32[2048]{0:T(1024)}, s32[2048]{0:T(1024)S(1)}, u32[]{:S(2)}) copy-start(s32[2048]{0:T(1024)S(1)} %get-tuple-element.87) | copy-start | bytes 24580
  43.8 1.0 copy-start.3
  68.6 0.6 copy-start.9
  86.8 0.7 copy-start.10
  90.1 1.2 copy-start.2
  113.5 1.8 %copy-start.8 = (s32[2048]{0:T(1024)S(1)}, s32[2048]{0:T(1024)}, u32[]{:S(2)}) copy-start(s32[2048]{0:T(1024)} %copy-done.7) | copy-start | bytes 24580
  122.7 1.0 copy-start.4
  131.9 11.8 %copy-start.6 = (s32[2048]{0:T(1024)S(1)}, s32[2048]{0:T(1024)}, u32[]{:S(2)}) copy-start(s32[2048]{0:T(1024)} %copy-done.5) | copy-start | bytes 24580
  146.8 0.7 copy-start.11
  164.8 0.7 copy-start.12

commit v14 on v9

--- a/solution.py
+++ b/solution.py
@@ -101,7 +101,7 @@
         squared = squared + jnp.maximum(
             jnp.square(jnp.maximum(backward, 0.0)), jnp.square(jnp.minimum(forward, 0.0))
         )
-    return voxels - advect_scale * speeds * jnp.sqrt(squared)
+    return voxels - speeds * jnp.sqrt(squared)
 
 
 def relax_leaves(voxels, sign_field, picked):
@@ -134,7 +134,7 @@
 
 
 def exchange_kernel(
-    tab_ref, idx_ref, ridx_ref, comb_ref, og_ref, bd_ref, sems
+    tab_ref, idx_ref, ridx_ref, speed_hbm, comb_ref, scaled_ref, og_ref, bd_ref, sems, speed_ref
 ):
     peers, slots = og_ref.shape[0], og_ref.shape[1]
     local = tab_ref.shape[0]
@@ -150,6 +150,8 @@
 
     keep = pltpu.make_async_copy(tab_ref, comb_ref.at[pl.ds(0, local)], sems.at[4])
     keep.start()
+    fetch = pltpu.make_async_copy(speed_hbm, speed_ref, sems.at[5])
+    fetch.start()
 
     barrier = pltpu.get_barrier_semaphore()
 
@@ -171,6 +173,9 @@
         return carry
 
     lax.fori_loop(0, peers, pack, 0)
+
+    fetch.wait()
+    scaled_ref[...] = advect_scale * speed_ref[...]
 
     pl.semaphore_wait(barrier, peers + 1)
 
@@ -211,7 +216,7 @@
     keep.wait()
 
 
-def exchange(table, peer_ids, region_ids, peers, layers):
+def exchange(table, peer_ids, region_ids, peers, layers, speeds):
     local, slab_rows = table.shape
     slots = peer_ids.shape[0] // peers
     width = region_ids.shape[0] // 2
@@ -219,18 +224,22 @@
     smem = pl.BlockSpec(memory_space=pltpu.SMEM)
     return pl.pallas_call(
         exchange_kernel,
-        out_shape=(pltpu.VMEM if layers == 1 else jax.ShapeDtypeStruct)(
-            (local + peers * slots + 2 * width, slab_rows), table.dtype
+        out_shape=(
+            (pltpu.VMEM if layers == 1 else jax.ShapeDtypeStruct)(
+                (local + peers * slots + 2 * width, slab_rows), table.dtype
+            ),
+            pltpu.VMEM(speeds.shape, speeds.dtype),
         ),
-        in_specs=[vmem, smem, smem],
-        out_specs=vmem,
+        in_specs=[vmem, smem, smem, pl.BlockSpec(memory_space=pl.ANY)],
+        out_specs=(vmem, vmem),
         scratch_shapes=[
             pltpu.VMEM((peers, slots, slab_rows), table.dtype),
             pltpu.VMEM((2, width, slab_rows), table.dtype),
-            pltpu.SemaphoreType.DMA((5,)),
+            pltpu.SemaphoreType.DMA((6,)),
+            pltpu.VMEM(speeds.shape, speeds.dtype),
         ],
         compiler_params=pltpu.CompilerParams(collective_id=layers, has_side_effects=True),
-    )(pltpu.with_memory_space_constraint(table, pltpu.VMEM), peer_ids, region_ids)
+    )(pltpu.with_memory_space_constraint(table, pltpu.VMEM), peer_ids, region_ids, speeds)
 
 
 def paired_kernel(tab_ref, idx_ref, ridx_ref, comb_ref, og_ref, bd_ref, sems):
@@ -347,7 +356,7 @@
     return row, upper
 
 
-def assemble(voxels, layers, peer_ids, region_ids, halo_ids, paired_ids):
+def assemble(voxels, layers, peer_ids, region_ids, halo_ids, paired_ids, speeds=None):
     slab_table = face_slabs(voxels, layers)
     peers = lax.axis_size("dev")
     if layers == 1 and paired_ids is not None:
@@ -357,9 +366,9 @@
         width = slab_table.shape[0]
         chosen = jnp.where(upper[..., None], lines[..., width:], lines[..., :width])
         return jnp.moveaxis(chosen, 2, 0)
-    combined = exchange(slab_table.T, peer_ids, region_ids, peers, layers).T
-    picked = combined.at[:, halo_ids].get(mode="promise_in_bounds")
-    return picked
+    combined, scaled = exchange(slab_table.T, peer_ids, region_ids, peers, layers, speeds)
+    picked = combined.T.at[:, halo_ids].get(mode="promise_in_bounds")
+    return picked, scaled
 
 
 def per_device(level_set, speed, peer_slabs, region_slabs, halo_source):
@@ -376,8 +385,10 @@
     voxels = level_set.reshape(8, 8, 8, count)
     speeds = speed.reshape(8, 8, 8, count)
     for offset_step in range(OFFSET_STEPS):
-        picked = assemble(voxels, 3, peer_ids, region_ids, halo_ids, paired_ids)
-        voxels = advect_leaves(voxels, lax.optimization_barrier(speeds), picked)
+        picked, scaled = assemble(
+            voxels, 3, peer_ids, region_ids, halo_ids, paired_ids, speed
+        )
+        voxels = advect_leaves(voxels, scaled.reshape(speeds.shape), picked)
         sign_field = voxels / jnp.sqrt(voxels * voxels + 1.0)
         for redist_pass in range(REDIST_PASSES):
             picked = assemble(voxels, 1, peer_ids, region_ids, halo_ids, paired_ids)

time: 156 us -> 159 us (1.019)
  local copies, waits for them, and re-layouts: 37 us -> 40.2 us
    slice x2, local copies, waits for them, and re-layouts: 0.25 us -> 2.83 us  [face_part(): return picked[:, side, :].reshape(extent + (count,))]
    gather x4, local copies, waits for them, and re-layouts: 11.4 us -> 13.5 us  [assemble(): picked = combined.T.at[:, halo_ids].get(mode='promise_in_bounds')]
    unnamed x76 -> x72, local copies, waits for them, and re-layouts: 5.27 us -> 3.89 us
where the time goes in v14:
time: 159 us
  Pallas kernels  94.8 us (60%)
  local copies, waits for them, and re-layouts  40.2 us (25%)
  other arithmetic  22.2 us (14%)
    pallas_call x4, Pallas kernels, paired_exchange(): pl.pallas_call(paired_kernel, out_shape=pltpu.VMEM((local + peers * slots...  47.7 us
    pallas_call x2, Pallas kernels, exchange(): pl.pallas_call(exchange_kernel, out_shape=((pltpu.VMEM if layers == 1 els...  47.1 us
    sub x2, other arithmetic, advect_leaves(): return voxels - speeds * jnp.sqrt(squared)  14.6 us
    gather x4, local copies, waits for them, and re-layouts, assemble(): picked = combined.T.at[:, halo_ids].get(mode='promise_in_bounds')  13.5 us
    gather x4, local copies, waits for them, and re-layouts, assemble(): lines = table.at[rows].get(mode='promise_in_bounds')  10.8 us
    sub x4, other arithmetic, relax_leaves(): return voxels - relax_scale * sign_field * (jnp.sqrt(squared) - 1.0)  5.08 us
    reshape x46, local copies, waits for them, and re-layouts, face_slabs(): piece.reshape(64 * layers, count)  3.99 us
    unnamed x72, local copies, waits for them, and re-layouts  3.89 us

profile of v14, /device:TPU:1, one launch (start us, length us, event | category | flops | bytes accessed | tf_op | source)
XLA Modules:
  0.0 158.6 jit_solution(14670806378684235444)
XLA Ops:
  0.0 1.1 fusion.156
  2.7 0.7 min.120.idx_ref
  4.0 26.4 %shard_map.55 = (f32[2080,192]{1,0:T(8,128)}, f32[512,256]{1,0:T(8,128)S(1)}) custom-call(f32[1536,192]{1,0:T(8,128)S(1)} %bitcast.170, s32[512]{0:T(512)} %min.120.idx_ref, s32[32]{0:T(128)} %min.123.ridx_ref, f32[512,256]{1,0:T(8,128)} %speed_hbm.3), custom_call_target="tpu_custom_call" | custom-call | tf_op jit(solution)/shard_map/pallas_call | solution.py:225
  30.5 5.3 %gather_fusion = f32[1536,192]{1,0:T(8,128)S(1)} fusion(f32[192,2080]{0,1:T(8,128)} %bitcast.174, s32[2048]{0:T(1024)S(1)} %get-tuple-element.96), kind=kCustom, calls=%fused_computation | custom fusion | bytes 2365440 | tf_op jit(solution)/shard_map/gather | solution.py:370
  35.7 1.5 copy.48
  37.2 1.4 fusion.142
  39.5 7.3 %multiply_subtract_fusion.5 = f32[8,8,8,256]{3,2,1,0:T(8,128)S(1)} fusion(f32[8,8,8,256]{3,2,1,0:T(8,128)S(1)} %bitcast.181, f32[8,8,8,256]{3,2,1,0:T(8,128)S(1)} %bitcast.172, f32[8,8,13,256]{3,2,1,0:T(8,128)S(1)} %slice_subtract_fusion.1, f32[8,13,8,256]{3,2,1,0:T(8,128)S(1)} %slice_subtract_fusion.4, f32[13,8,8,256]{3,2,1,0:T(8,128)S(1)} %slice_subtract_fusion.5), kind=kLoop, calls=%fused_computation.257 | loop fusion | flops 53608448 | bytes 11010048 | tf_op jit(solution)/shard_map/sub | solution.py:104
  47.9 12.0 %shard_map.56 = f32[1824,128]{1,0:T(8,128)S(1)} custom-call(f32[1536,128]{1,0:T(8,128)S(1)} %pad_maximum_fusion.6.tab_ref, s32[512]{0:T(512)} %min.120.idx_ref, s32[32]{0:T(128)} %min.123.ridx_ref), custom_call_target="tpu_custom_call" | custom-call | tf_op jit(solution)/shard_map/pallas_call | solution.py:330
  59.9 2.6 %gather_fusion.1 = f32[1536,128]{1,0:T(8,128)S(1)} fusion(f32[1824,128]{1,0:T(8,128)S(1)} %shard_map.56, s32[2048]{0:T(1024)S(1)} %get-tuple-element.95), kind=kCustom, calls=%fused_computation.1 | custom fusion | bytes 1579008 | tf_op jit(solution)/shard_map/gather | solution.py:365
  64.1 1.1 multiply_subtract_fusion.4
  66.3 12.0 %shard_map.57 = f32[1824,128]{1,0:T(8,128)S(1)} custom-call(f32[1536,128]{1,0:T(8,128)S(1)} %pad_maximum_fusion.7.tab_ref, s32[512]{0:T(512)} %min.120.idx_ref, s32[32]{0:T(128)} %min.123.ridx_ref), custom_call_target="tpu_custom_call" | custom-call | tf_op jit(solution)/shard_map/pallas_call | solution.py:330
  78.3 2.8 %gather_fusion.2 = f32[1536,128]{1,0:T(8,128)S(1)} fusion(f32[1824,128]{1,0:T(8,128)S(1)} %shard_map.57, s32[2048]{0:T(1024)S(1)} %get-tuple-element.95), kind=kCustom, calls=%fused_computation.2 | custom fusion | bytes 1579008 | tf_op jit(solution)/shard_map/gather | solution.py:365
  82.3 1.1 multiply_subtract_fusion.3
  84.8 20.7 %shard_map.58 = (f32[2080,192]{1,0:T(8,128)}, f32[512,256]{1,0:T(8,128)S(1)}) custom-call(f32[1536,192]{1,0:T(8,128)S(1)} %bitcast.171, s32[512]{0:T(512)} %min.120.idx_ref, s32[32]{0:T(128)} %min.123.ridx_ref, f32[512,256]{1,0:T(8,128)} %speed_hbm.3), custom_call_target="tpu_custom_call" | custom-call | tf_op jit(solution)/shard_map/pallas_call | solution.py:225
  105.5 5.3 %gather_fusion.3 = f32[1536,192]{1,0:T(8,128)S(1)} fusion(f32[192,2080]{0,1:T(8,128)} %bitcast.175, s32[2048]{0:T(1024)S(1)} %copy-done.4), kind=kCustom, calls=%fused_computation.3 | custom fusion | bytes 2365440 | tf_op jit(solution)/shard_map/gather | solution.py:370
  110.8 1.5 copy.79
  112.3 1.4 fusion.141
  114.5 7.3 %multiply_subtract_fusion.2 = f32[8,8,8,256]{3,2,1,0:T(8,128)S(1)} fusion(f32[8,8,8,256]{3,2,1,0:T(8,128)S(1)} %multiply_subtract_fusion.3, f32[8,8,8,256]{3,2,1,0:T(8,128)S(1)} %bitcast.173, f32[8,8,13,256]{3,2,1,0:T(8,128)S(1)} %slice_subtract_fusion, f32[8,13,8,256]{3,2,1,0:T(8,128)S(1)} %slice_subtract_fusion.2, ...), kind=kLoop, calls=%fused_computation.253 | loop fusion | flops 53608448 | bytes 11010048 | tf_op jit(solution)/shard_map/sub | solution.py:104
  123.0 11.5 %shard_map.59 = f32[1824,128]{1,0:T(8,128)S(1)} custom-call(f32[1536,128]{1,0:T(8,128)S(1)} %pad_maximum_fusion.8.tab_ref, s32[512]{0:T(512)} %min.120.idx_ref, s32[32]{0:T(128)} %min.123.ridx_ref), custom_call_target="tpu_custom_call" | custom-call | tf_op jit(solution)/shard_map/pallas_call | solution.py:330
  134.5 2.8 %gather_fusion.4 = f32[1536,128]{1,0:T(8,128)S(1)} fusion(f32[1824,128]{1,0:T(8,128)S(1)} %shard_map.59, s32[2048]{0:T(1024)S(1)} %copy-done.2), kind=kCustom, calls=%fused_computation.4 | custom fusion | bytes 1579008 | tf_op jit(solution)/shard_map/gather | solution.py:365
  138.5 1.1 multiply_subtract_fusion.1
  140.7 12.2 %shard_map.60 = f32[1824,128]{1,0:T(8,128)S(1)} custom-call(f32[1536,128]{1,0:T(8,128)S(1)} %pad_maximum_fusion.9.tab_ref, s32[512]{0:T(512)} %min.120.idx_ref, s32[32]{0:T(128)} %min.123.ridx_ref), custom_call_target="tpu_custom_call" | custom-call | tf_op jit(solution)/shard_map/pallas_call | solution.py:330
  152.9 2.6 %gather_fusion.5 = f32[1536,128]{1,0:T(8,128)S(1)} fusion(f32[1824,128]{1,0:T(8,128)S(1)} %shard_map.60, s32[2048]{0:T(1024)S(1)} %copy-done.2), kind=kCustom, calls=%fused_computation.5 | custom fusion | bytes 1579008 | tf_op jit(solution)/shard_map/gather | solution.py:365
  156.7 1.9 %multiply_subtract_fusion = f32[8,8,8,256]{3,2,1,0:T(8,128)} fusion(f32[8,8,8,256]{3,2,1,0:T(8,128)S(1)} %multiply_subtract_fusion.1, f32[8,8,1,256]{3,2,1,0:T(1,128)S(1)} %copy.103, f32[8,8,1,256]{3,2,1,0:T(1,128)S(1)} %copy.102, f32[8,1,8,256]{3,2,1,0:T(8,128)S(1)} %get-tuple-element.72, f32[8,1,8,256]{3,2,1,0:T(8,128)S(1)} %get-tuple-element.73, ...), kind=kLoop, calls=%fused_computation.250 | loop fusion | flops 7208960 | bytes 1966080 | tf_op jit(solution)/shard_map/sub | solution.py:120
  (182 shorter events, 13.9 us)
Async XLA Ops:
  0.0 1.4 copy-start
  1.9 0.7 copy-start.10
  1.9 1.5 copy-start.11
  2.3 28.0 %copy-start.9 = (s32[6,256]{1,0:T(8,128)S(1)}, s32[6,256]{1,0:T(8,128)}, u32[]{:S(2)}) copy-start(s32[6,256]{1,0:T(8,128)} %param.9) | copy-start | bytes 18436
  30.4 5.3 %copy-start.3 = (s32[2048]{0:T(1024)}, s32[2048]{0:T(1024)S(1)}, u32[]{:S(2)}) copy-start(s32[2048]{0:T(1024)S(1)} %get-tuple-element.96) | copy-start | bytes 24580
  30.5 47.9 %copy-start.1 = (s32[2048]{0:T(1024)}, s32[2048]{0:T(1024)S(1)}, u32[]{:S(2)}) copy-start(s32[2048]{0:T(1024)S(1)} %get-tuple-element.95) | copy-start | bytes 24580
  63.3 0.6 copy-start.5
  81.4 0.7 copy-start.6
  84.6 20.9 %copy-start.4 = (s32[2048]{0:T(1024)S(1)}, s32[2048]{0:T(1024)}, u32[]{:S(2)}) copy-start(s32[2048]{0:T(1024)} %copy-done.3) | copy-start | bytes 24580
  122.7 11.8 %copy-start.2 = (s32[2048]{0:T(1024)S(1)}, s32[2048]{0:T(1024)}, u32[]{:S(2)}) copy-start(s32[2048]{0:T(1024)} %copy-done.1) | copy-start | bytes 24580
  137.6 0.7 copy-start.7
  155.8 0.7 copy-start.8

commit v15 on v9

--- a/solution.py
+++ b/solution.py
@@ -128,8 +128,10 @@
     ]
     moves.sort(key=lambda m: -(min(m[0], 8 - m[0]) + min(m[1], 4 - m[1])))
     z, x, c = me // 8, (me // 2) % 4, me % 2
+    way = 1 - 2 * c
     return [
-        lax.rem(z + dz, 8) * 8 + lax.rem(x + dx, 4) * 2 + lax.rem(c + dc, 2) for dz, dx, dc in moves
+        lax.rem(z + way * dz + 8, 8) * 8 + lax.rem(x + way * dx + 4, 4) * 2 + lax.rem(c + dc, 2)
+        for dz, dx, dc in moves
     ]
 
 

time: 156 us -> 156 us (level)
  no operation moved by 1% of the time
where the time goes in v15:
time: 156 us
  Pallas kernels  95.1 us (61%)
  local copies, waits for them, and re-layouts  37 us (24%)
  other arithmetic  22.2 us (14%)
    pallas_call x4, Pallas kernels, paired_exchange(): pl.pallas_call(paired_kernel, out_shape=pltpu.VMEM((local + peers * slots...  47.6 us
    pallas_call x2, Pallas kernels, exchange(): pl.pallas_call(exchange_kernel, out_shape=(pltpu.VMEM if layers == 1 else...  47.5 us
    sub x2, other arithmetic, advect_leaves(): return voxels - advect_scale * speeds * jnp.sqrt(squared)  14.6 us
    gather x4, local copies, waits for them, and re-layouts, assemble(): picked = combined.at[:, halo_ids].get(mode='promise_in_bounds')  11.4 us
    gather x4, local copies, waits for them, and re-layouts, assemble(): lines = table.at[rows].get(mode='promise_in_bounds')  10.8 us
    unnamed x76, local copies, waits for them, and re-layouts  5.27 us
    sub x4, other arithmetic, relax_leaves(): return voxels - relax_scale * sign_field * (jnp.sqrt(squared) - 1.0)  5.09 us
    reshape x46, local copies, waits for them, and re-layouts, face_slabs(): piece.reshape(64 * layers, count)  3.99 us

profile of v15, /device:TPU:1, one launch (start us, length us, event | category | flops | bytes accessed | tf_op | source)
XLA Modules:
  0.0 155.6 jit_solution(12067746392891088419)
XLA Ops:
  0.0 1.1 fusion.156
  2.7 0.7 min.120.idx_ref
  3.4 0.6 min.123.ridx_ref
  4.0 26.6 %shard_map.55 = f32[2080,192]{1,0:T(8,128)} custom-call(f32[1536,192]{1,0:T(8,128)S(1)} %bitcast.169, s32[512]{0:T(512)} %min.120.idx_ref, s32[32]{0:T(128)} %min.123.ridx_ref), custom_call_target="tpu_custom_call" | custom-call | tf_op jit(solution)/shard_map/pallas_call | solution.py:222
  30.7 5.3 %gather_fusion = f32[1536,192]{1,0:T(8,128)S(1)} fusion(f32[192,2080]{0,1:T(8,128)} %bitcast.171, s32[2048]{0:T(1024)S(1)} %get-tuple-element.88), kind=kCustom, calls=%fused_computation | custom fusion | bytes 2365440 | tf_op jit(solution)/shard_map/gather | solution.py:363
  36.0 0.4 copy.49
  37.4 1.0 copy-done.1
  38.4 7.3 %multiply_subtract_fusion.5 = f32[8,8,8,256]{3,2,1,0:T(8,128)S(1)} fusion(f32[8,8,8,256]{3,2,1,0:T(8,128)S(1)} %bitcast.178, f32[8,8,13,256]{3,2,1,0:T(8,128)S(1)} %slice_subtract_fusion.1, f32[8,13,8,256]{3,2,1,0:T(8,128)S(1)} %slice_subtract_fusion.4, f32[13,8,8,256]{3,2,1,0:T(8,128)S(1)} %slice_subtract_fusion.5, f32[8,8,8,256]{3,2,1,0:T(8,128)S(1)} %bitcast.187), kind=kLoop, calls=%fused_computation.257 | loop fusion | flops 53739520 | bytes 11010048 | tf_op jit(solution)/shard_map/sub | solution.py:104
  46.8 11.8 %shard_map.56 = f32[1824,128]{1,0:T(8,128)S(1)} custom-call(f32[1536,128]{1,0:T(8,128)S(1)} %pad_maximum_fusion.6.tab_ref, s32[512]{0:T(512)} %min.120.idx_ref, s32[32]{0:T(128)} %min.123.ridx_ref), custom_call_target="tpu_custom_call" | custom-call | tf_op jit(solution)/shard_map/pallas_call | solution.py:323
  58.5 2.6 %gather_fusion.1 = f32[1536,128]{1,0:T(8,128)S(1)} fusion(f32[1824,128]{1,0:T(8,128)S(1)} %shard_map.56, s32[2048]{0:T(1024)S(1)} %get-tuple-element.87), kind=kCustom, calls=%fused_computation.1 | custom fusion | bytes 1579008 | tf_op jit(solution)/shard_map/gather | solution.py:358
  62.2 1.1 multiply_subtract_fusion.4
  64.4 12.2 %shard_map.57 = f32[1824,128]{1,0:T(8,128)S(1)} custom-call(f32[1536,128]{1,0:T(8,128)S(1)} %pad_maximum_fusion.7.tab_ref, s32[512]{0:T(512)} %min.120.idx_ref, s32[32]{0:T(128)} %min.123.ridx_ref), custom_call_target="tpu_custom_call" | custom-call | tf_op jit(solution)/shard_map/pallas_call | solution.py:323
  76.6 2.8 %gather_fusion.2 = f32[1536,128]{1,0:T(8,128)S(1)} fusion(f32[1824,128]{1,0:T(8,128)S(1)} %shard_map.57, s32[2048]{0:T(1024)S(1)} %get-tuple-element.87), kind=kCustom, calls=%fused_computation.2 | custom fusion | bytes 1579008 | tf_op jit(solution)/shard_map/gather | solution.py:358
  80.6 1.1 multiply_subtract_fusion.3
  83.0 20.9 %shard_map.58 = f32[2080,192]{1,0:T(8,128)} custom-call(f32[1536,192]{1,0:T(8,128)S(1)} %bitcast.170, s32[512]{0:T(512)} %min.120.idx_ref, s32[32]{0:T(128)} %min.123.ridx_ref), custom_call_target="tpu_custom_call" | custom-call | tf_op jit(solution)/shard_map/pallas_call | solution.py:222
  104.0 5.3 %gather_fusion.3 = f32[1536,192]{1,0:T(8,128)S(1)} fusion(f32[192,2080]{0,1:T(8,128)} %bitcast.172, s32[2048]{0:T(1024)S(1)} %copy-done.6), kind=kCustom, calls=%fused_computation.3 | custom fusion | bytes 2365440 | tf_op jit(solution)/shard_map/gather | solution.py:363
  110.7 1.0 copy-done.2
  111.6 7.3 %multiply_subtract_fusion.2 = f32[8,8,8,256]{3,2,1,0:T(8,128)S(1)} fusion(f32[8,8,8,256]{3,2,1,0:T(8,128)S(1)} %multiply_subtract_fusion.3, f32[8,8,13,256]{3,2,1,0:T(8,128)S(1)} %slice_subtract_fusion, f32[8,13,8,256]{3,2,1,0:T(8,128)S(1)} %slice_subtract_fusion.2, f32[13,8,8,256]{3,2,1,0:T(8,128)S(1)} %slice_subtract_fusion.3, ...), kind=kLoop, calls=%fused_computation.253 | loop fusion | flops 53739520 | bytes 11010048 | tf_op jit(solution)/shard_map/sub | solution.py:104
  120.1 11.3 %shard_map.59 = f32[1824,128]{1,0:T(8,128)S(1)} custom-call(f32[1536,128]{1,0:T(8,128)S(1)} %pad_maximum_fusion.8.tab_ref, s32[512]{0:T(512)} %min.120.idx_ref, s32[32]{0:T(128)} %min.123.ridx_ref), custom_call_target="tpu_custom_call" | custom-call | tf_op jit(solution)/shard_map/pallas_call | solution.py:323
  131.4 2.8 %gather_fusion.4 = f32[1536,128]{1,0:T(8,128)S(1)} fusion(f32[1824,128]{1,0:T(8,128)S(1)} %shard_map.59, s32[2048]{0:T(1024)S(1)} %copy-done.4), kind=kCustom, calls=%fused_computation.4 | custom fusion | bytes 1579008 | tf_op jit(solution)/shard_map/gather | solution.py:358
  135.4 1.1 multiply_subtract_fusion.1
  137.6 12.3 %shard_map.60 = f32[1824,128]{1,0:T(8,128)S(1)} custom-call(f32[1536,128]{1,0:T(8,128)S(1)} %pad_maximum_fusion.9.tab_ref, s32[512]{0:T(512)} %min.120.idx_ref, s32[32]{0:T(128)} %min.123.ridx_ref), custom_call_target="tpu_custom_call" | custom-call | tf_op jit(solution)/shard_map/pallas_call | solution.py:323
  149.9 2.6 %gather_fusion.5 = f32[1536,128]{1,0:T(8,128)S(1)} fusion(f32[1824,128]{1,0:T(8,128)S(1)} %shard_map.60, s32[2048]{0:T(1024)S(1)} %copy-done.4), kind=kCustom, calls=%fused_computation.5 | custom fusion | bytes 1579008 | tf_op jit(solution)/shard_map/gather | solution.py:358
  153.7 1.9 %multiply_subtract_fusion = f32[8,8,8,256]{3,2,1,0:T(8,128)} fusion(f32[8,8,8,256]{3,2,1,0:T(8,128)S(1)} %multiply_subtract_fusion.1, f32[8,8,1,256]{3,2,1,0:T(1,128)S(1)} %copy.104, f32[8,8,1,256]{3,2,1,0:T(1,128)S(1)} %copy.103, f32[8,1,8,256]{3,2,1,0:T(8,128)S(1)} %get-tuple-element.64, f32[8,1,8,256]{3,2,1,0:T(8,128)S(1)} %get-tuple-element.65, ...), kind=kLoop, calls=%fused_computation.250 | loop fusion | flops 7208960 | bytes 1966080 | tf_op jit(solution)/shard_map/sub | solution.py:120
  (186 shorter events, 13.5 us)
Async XLA Ops:
  0.0 1.4 copy-start
  1.9 0.7 copy-start.12
  1.9 1.5 copy-start.13
  4.0 26.6 %copy-start.11 = (s32[6,256]{1,0:T(8,128)S(1)}, s32[6,256]{1,0:T(8,128)}, u32[]{:S(2)}) copy-start(s32[6,256]{1,0:T(8,128)} %param.9) | copy-start | bytes 18436
  30.7 5.3 %copy-start.5 = (s32[2048]{0:T(1024)}, s32[2048]{0:T(1024)S(1)}, u32[]{:S(2)}) copy-start(s32[2048]{0:T(1024)S(1)} %get-tuple-element.88) | copy-start | bytes 24580
  30.7 45.9 %copy-start.3 = (s32[2048]{0:T(1024)}, s32[2048]{0:T(1024)S(1)}, u32[]{:S(2)}) copy-start(s32[2048]{0:T(1024)S(1)} %get-tuple-element.87) | copy-start | bytes 24580
  37.3 1.0 copy-start.1
  62.0 1.3 copy-start.7
  79.7 0.7 copy-start.8
  83.0 20.9 %copy-start.6 = (s32[2048]{0:T(1024)S(1)}, s32[2048]{0:T(1024)}, u32[]{:S(2)}) copy-start(s32[2048]{0:T(1024)} %copy-done.5) | copy-start | bytes 24580
  110.6 1.0 copy-start.2
  119.8 11.6 %copy-start.4 = (s32[2048]{0:T(1024)S(1)}, s32[2048]{0:T(1024)}, u32[]{:S(2)}) copy-start(s32[2048]{0:T(1024)} %copy-done.3) | copy-start | bytes 24580
  134.5 0.7 copy-start.9
  152.8 0.7 copy-start.10

commit v16 on v9

--- a/solution.py
+++ b/solution.py
@@ -161,12 +161,12 @@
 
     for h in range(2):
         for p in range(width):
-            source = ridx_ref[h * width + p]
+            source = jnp.clip(ridx_ref[h, p], 0, local - 1)
             bd_ref[h, pl.ds(p, 1), :] = tab_ref[pl.ds(source, 1), :]
 
     def pack(e, carry):
         for c in range(slots):
-            source = idx_ref[e * slots + c]
+            source = jnp.clip(idx_ref[e, c], 0, local - 1)
             og_ref[e, pl.ds(c, 1), :] = tab_ref[pl.ds(source, 1), :]
         return carry
 
@@ -213,8 +213,8 @@
 
 def exchange(table, peer_ids, region_ids, peers, layers):
     local, slab_rows = table.shape
-    slots = peer_ids.shape[0] // peers
-    width = region_ids.shape[0] // 2
+    slots = peer_ids.shape[1]
+    width = region_ids.shape[1]
     vmem = pl.BlockSpec(memory_space=pltpu.VMEM)
     smem = pl.BlockSpec(memory_space=pltpu.SMEM)
     return pl.pallas_call(
@@ -259,15 +259,15 @@
 
     for h in range(2):
         for p in range(width):
-            source = ridx_ref[h * width + p]
+            source = jnp.clip(ridx_ref[h, p], 0, local - 1)
             bd_ref[h, pl.ds(p, 1), :] = tab_ref[pl.ds(source, 1), :]
 
     lanes = lax.broadcasted_iota(jnp.int32, (1, lane_count), 1)
 
     def pack(e, carry):
         for r in range(half):
-            first = tab_ref[pl.ds(idx_ref[e * slots + r], 1), :]
-            second = tab_ref[pl.ds(idx_ref[e * slots + r + half], 1), :]
+            first = tab_ref[pl.ds(jnp.clip(idx_ref[e, r], 0, local - 1), 1), :]
+            second = tab_ref[pl.ds(jnp.clip(idx_ref[e, r + half], 0, local - 1), 1), :]
             og_ref[e, pl.ds(r, 1), :] = jnp.where(lanes < slab_rows, first, second)
         return carry
 
@@ -313,8 +313,8 @@
 
 def paired_exchange(table, peer_ids, region_ids, peers):
     local, slab_rows = table.shape
-    slots = peer_ids.shape[0] // peers
-    width = region_ids.shape[0] // 2
+    slots = peer_ids.shape[1]
+    width = region_ids.shape[1]
     doubled = jnp.concatenate([table, table], axis=1)
     vmem = pl.BlockSpec(memory_space=pltpu.VMEM)
     smem = pl.BlockSpec(memory_space=pltpu.SMEM)
@@ -365,14 +365,14 @@
 def per_device(level_set, speed, peer_slabs, region_slabs, halo_source):
     count = level_set.shape[1]
     local = 6 * count
-    peer_ids = jnp.clip(peer_slabs.reshape(-1), 0, local - 1)
-    region_ids = jnp.clip(region_slabs.reshape(-1), 0, local - 1)
-    halo_ids = jnp.clip(halo_source, 0, local + peer_ids.shape[0] + region_ids.shape[0] - 1)
+    peer_ids = peer_slabs
+    region_ids = region_slabs
+    halo_ids = jnp.clip(halo_source, 0, local + peer_ids.size + region_ids.size - 1)
     peers = lax.axis_size("dev")
-    slots = peer_ids.shape[0] // peers
+    slots = peer_ids.shape[1]
     paired_ids = None
     if slots % 2 == 0:
-        paired_ids = paired_sources(halo_ids, local, peers, slots, region_ids.shape[0] // 2)
+        paired_ids = paired_sources(halo_ids, local, peers, slots, region_ids.shape[1])
     voxels = level_set.reshape(8, 8, 8, count)
     speeds = speed.reshape(8, 8, 8, count)
     for offset_step in range(OFFSET_STEPS):

time: 156 us -> 159 us (1.019)
  Pallas kernels: 94.8 us -> 98 us
    pallas_call x4, Pallas kernels: 47.6 us -> 49.7 us  [paired_exchange(): pl.pallas_call(paired_kernel, out_shape=pltpu.VMEM((local + peers * slots...]
    unnamed x76 -> x75, local copies, waits for them, and re-layouts: 5.27 us -> 6.03 us
where the time goes in v16:
time: 159 us; the launch traced here: 158 us
  Pallas kernels  98 us (62%)
  local copies, waits for them, and re-layouts  36.4 us (23%)
  other arithmetic  22.2 us (14%)
    pallas_call x4, Pallas kernels, paired_exchange(): pl.pallas_call(paired_kernel, out_shape=pltpu.VMEM((local + peers * slots...  49.7 us
    pallas_call x2, Pallas kernels, exchange(): pl.pallas_call(exchange_kernel, out_shape=(pltpu.VMEM if layers == 1 else...  48.3 us
    sub x2, other arithmetic, advect_leaves(): return voxels - advect_scale * speeds * jnp.sqrt(squared)  14.6 us
    gather x4, local copies, waits for them, and re-layouts, assemble(): picked = combined.at[:, halo_ids].get(mode='promise_in_bounds')  11.4 us
    gather x4, local copies, waits for them, and re-layouts, assemble(): lines = table.at[rows].get(mode='promise_in_bounds')  10.8 us
    unnamed x75, local copies, waits for them, and re-layouts  6.03 us
    sub x4, other arithmetic, relax_leaves(): return voxels - relax_scale * sign_field * (jnp.sqrt(squared) - 1.0)  5.09 us
    reshape x46, local copies, waits for them, and re-layouts, face_slabs(): piece.reshape(64 * layers, count)  3.99 us

profile of v16, /device:TPU:1, one launch (start us, length us, event | category | flops | bytes accessed | tf_op | source)
XLA Modules:
  0.0 157.9 jit_solution(13716426678600477045)
XLA Ops:
  0.0 1.1 fusion.156
  2.6 0.7 copy.54.idx_ref
  3.3 27.0 %shard_map.55 = f32[2080,192]{1,0:T(8,128)} custom-call(f32[1536,192]{1,0:T(8,128)S(1)} %bitcast.169, s32[64,8]{1,0:T(8,128)} %copy.54.idx_ref, s32[2,16]{1,0:T(2,128)} %ridx_ref.11), custom_call_target="tpu_custom_call" | custom-call | tf_op jit(solution)/shard_map/pallas_call | solution.py:220
  30.4 5.3 %gather_fusion = f32[1536,192]{1,0:T(8,128)S(1)} fusion(f32[192,2080]{0,1:T(8,128)} %bitcast.171, s32[2048]{0:T(1024)S(1)} %get-tuple-element.88), kind=kCustom, calls=%fused_computation | custom fusion | bytes 2365440 | tf_op jit(solution)/shard_map/gather | solution.py:361
  35.7 0.4 copy.55
  37.2 1.0 copy-done.1
  38.1 7.3 %multiply_subtract_fusion.5 = f32[8,8,8,256]{3,2,1,0:T(8,128)S(1)} fusion(f32[8,8,8,256]{3,2,1,0:T(8,128)S(1)} %bitcast.178, f32[8,8,13,256]{3,2,1,0:T(8,128)S(1)} %slice_subtract_fusion.1, f32[8,13,8,256]{3,2,1,0:T(8,128)S(1)} %slice_subtract_fusion.4, f32[13,8,8,256]{3,2,1,0:T(8,128)S(1)} %slice_subtract_fusion.5, f32[8,8,8,256]{3,2,1,0:T(8,128)S(1)} %bitcast.187), kind=kLoop, calls=%fused_computation.257 | loop fusion | flops 53739520 | bytes 11010048 | tf_op jit(solution)/shard_map/sub | solution.py:104
  46.5 12.5 %shard_map.56 = f32[1824,128]{1,0:T(8,128)S(1)} custom-call(f32[1536,128]{1,0:T(8,128)S(1)} %pad_maximum_fusion.6.tab_ref, s32[64,8]{1,0:T(8,128)} %copy.54.idx_ref, s32[2,16]{1,0:T(2,128)} %ridx_ref.11), custom_call_target="tpu_custom_call" | custom-call | tf_op jit(solution)/shard_map/pallas_call | solution.py:321
  59.1 2.6 %gather_fusion.1 = f32[1536,128]{1,0:T(8,128)S(1)} fusion(f32[1824,128]{1,0:T(8,128)S(1)} %shard_map.56, s32[2048]{0:T(1024)S(1)} %get-tuple-element.87), kind=kCustom, calls=%fused_computation.1 | custom fusion | bytes 1579008 | tf_op jit(solution)/shard_map/gather | solution.py:356
  62.7 1.1 multiply_subtract_fusion.4
  64.9 12.6 %shard_map.57 = f32[1824,128]{1,0:T(8,128)S(1)} custom-call(f32[1536,128]{1,0:T(8,128)S(1)} %pad_maximum_fusion.7.tab_ref, s32[64,8]{1,0:T(8,128)} %copy.54.idx_ref, s32[2,16]{1,0:T(2,128)} %ridx_ref.11), custom_call_target="tpu_custom_call" | custom-call | tf_op jit(solution)/shard_map/pallas_call | solution.py:321
  77.5 2.8 %gather_fusion.2 = f32[1536,128]{1,0:T(8,128)S(1)} fusion(f32[1824,128]{1,0:T(8,128)S(1)} %shard_map.57, s32[2048]{0:T(1024)S(1)} %get-tuple-element.87), kind=kCustom, calls=%fused_computation.2 | custom fusion | bytes 1579008 | tf_op jit(solution)/shard_map/gather | solution.py:356
  81.5 1.1 multiply_subtract_fusion.3
  84.0 21.3 %shard_map.58 = f32[2080,192]{1,0:T(8,128)} custom-call(f32[1536,192]{1,0:T(8,128)S(1)} %bitcast.170, s32[64,8]{1,0:T(8,128)} %copy.54.idx_ref, s32[2,16]{1,0:T(2,128)} %ridx_ref.11), custom_call_target="tpu_custom_call" | custom-call | tf_op jit(solution)/shard_map/pallas_call | solution.py:220
  105.2 5.3 %gather_fusion.3 = f32[1536,192]{1,0:T(8,128)S(1)} fusion(f32[192,2080]{0,1:T(8,128)} %bitcast.172, s32[2048]{0:T(1024)S(1)} %copy-done.6), kind=kCustom, calls=%fused_computation.3 | custom fusion | bytes 2365440 | tf_op jit(solution)/shard_map/gather | solution.py:361
  110.5 0.4 copy.89
  111.9 1.0 copy-done.2
  112.9 7.3 %multiply_subtract_fusion.2 = f32[8,8,8,256]{3,2,1,0:T(8,128)S(1)} fusion(f32[8,8,8,256]{3,2,1,0:T(8,128)S(1)} %multiply_subtract_fusion.3, f32[8,8,13,256]{3,2,1,0:T(8,128)S(1)} %slice_subtract_fusion, f32[8,13,8,256]{3,2,1,0:T(8,128)S(1)} %slice_subtract_fusion.2, f32[13,8,8,256]{3,2,1,0:T(8,128)S(1)} %slice_subtract_fusion.3, ...), kind=kLoop, calls=%fused_computation.253 | loop fusion | flops 53739520 | bytes 11010048 | tf_op jit(solution)/shard_map/sub | solution.py:104
  121.3 12.1 %shard_map.59 = f32[1824,128]{1,0:T(8,128)S(1)} custom-call(f32[1536,128]{1,0:T(8,128)S(1)} %pad_maximum_fusion.8.tab_ref, s32[64,8]{1,0:T(8,128)} %copy.54.idx_ref, s32[2,16]{1,0:T(2,128)} %ridx_ref.11), custom_call_target="tpu_custom_call" | custom-call | tf_op jit(solution)/shard_map/pallas_call | solution.py:321
  133.4 2.8 %gather_fusion.4 = f32[1536,128]{1,0:T(8,128)S(1)} fusion(f32[1824,128]{1,0:T(8,128)S(1)} %shard_map.59, s32[2048]{0:T(1024)S(1)} %copy-done.4), kind=kCustom, calls=%fused_computation.4 | custom fusion | bytes 1579008 | tf_op jit(solution)/shard_map/gather | solution.py:356
  137.4 1.1 multiply_subtract_fusion.1
  139.6 12.6 %shard_map.60 = f32[1824,128]{1,0:T(8,128)S(1)} custom-call(f32[1536,128]{1,0:T(8,128)S(1)} %pad_maximum_fusion.9.tab_ref, s32[64,8]{1,0:T(8,128)} %copy.54.idx_ref, s32[2,16]{1,0:T(2,128)} %ridx_ref.11), custom_call_target="tpu_custom_call" | custom-call | tf_op jit(solution)/shard_map/pallas_call | solution.py:321
  152.2 2.6 %gather_fusion.5 = f32[1536,128]{1,0:T(8,128)S(1)} fusion(f32[1824,128]{1,0:T(8,128)S(1)} %shard_map.60, s32[2048]{0:T(1024)S(1)} %copy-done.4), kind=kCustom, calls=%fused_computation.5 | custom fusion | bytes 1579008 | tf_op jit(solution)/shard_map/gather | solution.py:356
  156.0 1.9 %multiply_subtract_fusion = f32[8,8,8,256]{3,2,1,0:T(8,128)} fusion(f32[8,8,8,256]{3,2,1,0:T(8,128)S(1)} %multiply_subtract_fusion.1, f32[8,8,1,256]{3,2,1,0:T(1,128)S(1)} %copy.115, f32[8,8,1,256]{3,2,1,0:T(1,128)S(1)} %copy.114, f32[8,1,8,256]{3,2,1,0:T(8,128)S(1)} %get-tuple-element.64, f32[8,1,8,256]{3,2,1,0:T(8,128)S(1)} %get-tuple-element.65, ...), kind=kLoop, calls=%fused_computation.250 | loop fusion | flops 7208960 | bytes 1966080 | tf_op jit(solution)/shard_map/sub | solution.py:120
  (180 shorter events, 13.0 us)
Async XLA Ops:
  0.0 1.4 copy-start
  1.9 0.7 copy-start.12
  3.3 27.0 %copy-start.11 = (s32[6,256]{1,0:T(8,128)S(1)}, s32[6,256]{1,0:T(8,128)}, u32[]{:S(2)}) copy-start(s32[6,256]{1,0:T(8,128)} %param.9) | copy-start | bytes 18436
  30.4 5.3 %copy-start.5 = (s32[2048]{0:T(1024)}, s32[2048]{0:T(1024)S(1)}, u32[]{:S(2)}) copy-start(s32[2048]{0:T(1024)S(1)} %get-tuple-element.88) | copy-start | bytes 24580
  30.4 47.1 %copy-start.3 = (s32[2048]{0:T(1024)}, s32[2048]{0:T(1024)S(1)}, u32[]{:S(2)}) copy-start(s32[2048]{0:T(1024)S(1)} %get-tuple-element.87) | copy-start | bytes 24580
  37.1 1.0 copy-start.1
  62.5 1.3 copy-start.7
  80.6 0.7 copy-start.8
  83.9 21.3 %copy-start.6 = (s32[2048]{0:T(1024)S(1)}, s32[2048]{0:T(1024)}, u32[]{:S(2)}) copy-start(s32[2048]{0:T(1024)} %copy-done.5) | copy-start | bytes 24580
  111.8 1.0 copy-start.2
  121.0 12.4 %copy-start.4 = (s32[2048]{0:T(1024)S(1)}, s32[2048]{0:T(1024)}, u32[]{:S(2)}) copy-start(s32[2048]{0:T(1024)} %copy-done.3) | copy-start | bytes 24580
  136.5 0.7 copy-start.9
  155.1 0.7 copy-start.10
